TPU v7x, 128 devices: a whole 4x4x4 slice. The times are simulated.
128 devices in a mesh: apa: 4 (over x), tick: 32 (over z, y, core).
Axes of the slice: x: 4, y: 4, z: 4, core: 2. Of those that a mesh axis runs over, the one named last changes fastest.
Arguments:
- raw: float32 [61440, 3200], P('apa', 'tick'), may hold values from -90 to 90
- bad: int32 [61440], P('apa'), may hold values 0 or 1
- group_id: int32 [61440], P('apa'), may hold values from 0 to 479, as said below
- chan_plane: int32 [61440], P('apa'), may hold values from 0 to 127, as said below
- chan_wire: int32 [61440], P('apa'), may hold values from 0 to 479, as said below
- plane_offset: int32 [128], replicated, may hold values from 0 to 479
- wire_kernel: float32 [480], replicated, may hold values from -0.2738613 to 0.2738613
- time_kernel: float32 [3200], replicated, may hold values from -0.10606602 to 0.10606602
Outputs:
- deconvolved: float32 [128, 480, 3200], P(('apa', 'tick'))
Inputs may be any that keep to these rules, and one draw needn't show every extreme that they name: `group_id`: each block of 15360 consecutive channels holds whole groups of exactly 128 channels each, with the ids of that block's groups only. `chan_plane`: blocks of 15360 consecutive channels form aligned pairs (blocks 2m and 2m + 1); the channels of a pair go to planes 2m 32 to 2m 32 + 2 * 32 - 1 only, and each plane receives exactly 480 channels. A block names each plane of its pair either 240 - 180 or 420 times, the same number for all planes of one run of 32 consecutive planes (aligned runs), so at most 13440 for a run; both counts occur in every draw. `chan_wire`: the channels of one plane have distinct values.
All inputs are finite; a program needn't handle non-finite values. No bound on the sum of `bad` on one device may be relied on, other than what follows from the above.
Results may differ from a plain program's by a relative error of at most 0.000075.
Values sent between devices are 32-bit elements; how exact they have to be, the bound alone decides.
No kernel may reach another device: no remote copies, remote signals or barrier semaphores. Data moves between devices by JAX's collectives and lax.ppermute only.
A program may use at most 128 MiB of HBM per device.

v0:
```python
import math

import jax
import jax.numpy as jnp
from jax import lax
from jax.sharding import PartitionSpec as P

TICKS = 3200
GROUP = 128


highest = lax.Precision.HIGHEST
epsilon_power = 1e-06
regular_term = 0.25


def partner(value, axis, apart):
    return lax.ppermute(value, axis, [(i, i ^ 1 << apart) for i in range(lax.axis_size(axis))])


def factor_pair(length):
    lead_size = 1
    for candidate in range(1, math.isqrt(length) + 1):
        if length % candidate == 0:
            lead_size = candidate
    return (lead_size, length // lead_size)


def angle_table(row_count, col_count, length, direction):
    product_index = (
        jnp.arange(row_count, dtype=jnp.int32)[:, None]
        * jnp.arange(col_count, dtype=jnp.int32)[None, :]
        % length
    )
    phase_angle = direction * 2.0 * math.pi / length * product_index.astype(jnp.float32)
    return (jnp.cos(phase_angle), jnp.sin(phase_angle))


def block_table(size, direction):
    table_cos, table_sin = angle_table(size, size, size, direction)
    upper = jnp.stack([table_cos, -table_sin], axis=0)
    lower = jnp.stack([table_sin, table_cos], axis=0)
    return jnp.stack([upper, lower], axis=0)


def twist_stack(stacked, twist_cos, twist_sin):
    real_part = stacked[0] * twist_cos - stacked[1] * twist_sin
    imag_part = stacked[0] * twist_sin + stacked[1] * twist_cos
    return jnp.stack([real_part, imag_part], axis=0)


def forward_last(data):
    row_count, length = data.shape
    lead_size, trail_size = factor_pair(length)
    first = block_table(lead_size, -1.0)
    middle = jnp.einsum(
        "akm,cmj->ackj",
        first[:, 0],
        data.reshape(row_count, lead_size, trail_size),
        precision=highest,
    )
    twist_cos, twist_sin = angle_table(lead_size, trail_size, length, -1.0)
    middle = twist_stack(middle, twist_cos[None], twist_sin[None])
    second = block_table(trail_size, -1.0)
    result = jnp.einsum("abjl,bckj->ackl", second, middle, precision=highest)
    return result.reshape(2, row_count, length)


def inverse_last(data):
    row_count, length = (data.shape[1], data.shape[2])
    lead_size, trail_size = factor_pair(length)
    second = block_table(trail_size, 1.0)
    middle = jnp.einsum(
        "ablj,bckl->ackj",
        second,
        data.reshape(2, row_count, lead_size, trail_size),
        precision=highest,
    )
    twist_cos, twist_sin = angle_table(lead_size, trail_size, length, 1.0)
    middle = twist_stack(middle, twist_cos[None], twist_sin[None])
    first = block_table(lead_size, 1.0)
    real_out = jnp.einsum("bmk,bckj->cmj", first[0], middle, precision=highest)
    return real_out.reshape(row_count, length)


def forward_lead(data, is_real):
    if is_real:
        length, col_count = data.shape
    else:
        length, col_count = (data.shape[1], data.shape[2])
    lead_size, trail_size = factor_pair(length)
    first = block_table(lead_size, -1.0)
    if is_real:
        middle = jnp.einsum(
            "akm,mjc->akjc",
            first[:, 0],
            data.reshape(lead_size, trail_size, col_count),
            precision=highest,
        )
    else:
        middle = jnp.einsum(
            "abkm,bmjc->akjc",
            first,
            data.reshape(2, lead_size, trail_size, col_count),
            precision=highest,
        )
    twist_cos, twist_sin = angle_table(lead_size, trail_size, length, -1.0)
    middle = twist_stack(middle, twist_cos[:, :, None], twist_sin[:, :, None])
    second = block_table(trail_size, -1.0)
    result = jnp.einsum("abjl,bkjc->aklc", second, middle, precision=highest)
    return result.reshape(2, length, col_count)


def inverse_lead(data):
    length, col_count = (data.shape[1], data.shape[2])
    lead_size, trail_size = factor_pair(length)
    second = block_table(trail_size, 1.0)
    middle = jnp.einsum(
        "ablj,bklc->akjc",
        second,
        data.reshape(2, lead_size, trail_size, col_count),
        precision=highest,
    )
    twist_cos, twist_sin = angle_table(lead_size, trail_size, length, 1.0)
    middle = twist_stack(middle, twist_cos[:, :, None], twist_sin[:, :, None])
    first = block_table(lead_size, 1.0)
    result = jnp.einsum("abmk,bkjc->amjc", first, middle, precision=highest)
    return result.reshape(2, length, col_count)


def pack_rows(cleaned, target, dest_index, dest_count, capacity, sentinel):
    dest_onehot = (dest_index[:, None] == jnp.arange(dest_count, dtype=jnp.int32)[None, :]).astype(
        jnp.int32
    )
    slot_rank = jnp.sum(jnp.cumsum(dest_onehot, axis=0) * dest_onehot, axis=1) - 1
    position = dest_index * capacity + slot_rank
    send_rows = (
        jnp.zeros((dest_count * capacity, cleaned.shape[1]), jnp.float32).at[position].set(cleaned)
    )
    labels = jnp.full((dest_count * capacity,), sentinel, jnp.int32).at[position].set(target)
    return (
        send_rows.reshape(dest_count, capacity, cleaned.shape[1]),
        labels.reshape(dest_count, capacity),
    )


def shards(raw, bad, group_id, chan_plane, chan_wire, plane_offset, wire_kernel, time_kernel):
    chan_count, tick_slab = raw.shape
    group_count = chan_count // GROUP
    wire_width = wire_kernel.shape[0]
    tick_count = lax.axis_size("tick")
    apa_index = lax.axis_index("apa")
    local_group = group_id - apa_index * group_count
    member = (local_group[None, :] == jnp.arange(group_count, dtype=jnp.int32)[:, None]).astype(
        jnp.float32
    )
    good_mask = 1.0 - bad.astype(jnp.float32)
    common = jnp.dot(member * good_mask[None, :], raw, precision=highest)
    spread_common = jnp.take(common, local_group, axis=0)
    covar_part = jnp.sum(raw * spread_common, axis=1)
    power_part = jnp.sum(common * common, axis=1)
    covar, power = lax.psum((covar_part, power_part), "tick")
    power_chan = jnp.take(power, local_group, axis=0)
    weight = covar / TICKS / (power_chan / TICKS + epsilon_power)
    cleaned = good_mask[:, None] * (raw - weight[:, None] * spread_common)
    wire_shift = jnp.take(plane_offset, chan_plane, axis=0)
    wire_index = (chan_wire + wire_shift) % wire_width
    base_count = wire_width // 2
    cap_plane = base_count + 3 * base_count // 4
    dest_side = (chan_plane // tick_count != apa_index).astype(jnp.int32)
    plane_slot = chan_plane % tick_count
    target = plane_slot * wire_width + wire_index
    send_rows, labels = pack_rows(
        cleaned, target, dest_side, 2, tick_count * cap_plane, tick_count * wire_width
    )
    got_rows, got_labels = partner((send_rows[1], labels[1]), "apa", 0)
    all_rows = jnp.concatenate([send_rows[0], got_rows], axis=0)
    all_labels = jnp.concatenate([labels[0], got_labels], axis=0)
    owned = jnp.zeros((tick_count * wire_width, tick_slab), jnp.float32)
    owned = owned.at[all_labels].set(all_rows, mode="drop")
    owned = owned.reshape(tick_count, wire_width, tick_slab)
    spectrum = forward_last(
        lax.all_to_all(owned, "tick", split_axis=0, concat_axis=2, tiled=True)[0]
    )
    wire_spec = forward_lead(spectrum, False)
    kernel_wire = forward_lead(wire_kernel[:, None], True)
    kernel_time = forward_last(time_kernel[None, :])
    resp_real = kernel_wire[0] * kernel_time[0] - kernel_wire[1] * kernel_time[1]
    resp_imag = kernel_wire[0] * kernel_time[1] + kernel_wire[1] * kernel_time[0]
    denominator = resp_real * resp_real + resp_imag * resp_imag + regular_term
    filter_real = resp_real / denominator
    filter_imag = -resp_imag / denominator
    mixed_real = wire_spec[0] * filter_real - wire_spec[1] * filter_imag
    mixed_imag = wire_spec[0] * filter_imag + wire_spec[1] * filter_real
    back = inverse_lead(jnp.stack([mixed_real, mixed_imag], axis=0))
    result = inverse_last(back) / (wire_width * TICKS)
    return result[None]


def solution(mesh):
    placed = (P("apa", "tick"), P("apa"), P("apa"), P("apa"), P("apa"), P(), P(), P())
    return jax.shard_map(
        shards,
        mesh=mesh,
        in_specs=placed,
        out_specs=P(("apa", "tick"), None, None),
        check_vma=False,
    )
```

profile of v0, /device:TPU:1, one launch (start us, length us, event | category | flops | bytes accessed | tf_op | source)
XLA Modules:
  0.0 1090.0 jit_solution(12439678432374062362)
XLA Ops:
  0.0 0.8 convert_subtract_fusion
  0.9 0.9 compare_and_fusion
  1.7 8.5 copy.91
  10.2 8.7 multiply_reduce_fusion.1
  19.0 51.5 %gather_fusion.1 = f32[15360,100]{1,0:T(8,128)} fusion(f32[120,100]{1,0:T(8,128)S(1)} %copy.89, s32[15360]{0:T(1024)S(1)} %fusion.76), kind=kCustom, calls=%fused_computation.1 | custom fusion | bytes 12349440 | tf_op jit(solution)/shard_map/jit(_take)/gather | solution.py:159
  70.5 12.5 %multiply_reduce_fusion = f32[15360]{0:T(1024)S(1)} fusion(f32[15360,100]{1,0:T(8,128)} %copy.91, f32[15360,100]{1,0:T(8,128)} %gather_fusion.1, pred[15360]{0:T(1024)(128)(4,1)S(1)} %get-tuple-element.7), kind=kLoop, calls=%fused_computation.43 | loop fusion | flops 4592640 | bytes 12364800 | tf_op jit(solution)/shard_map/reduce_sum | solution.py:160
  83.0 125.6 %all-reduce = (f32[120]{0:T(128)S(1)}, f32[15360]{0:T(1024)S(1)}) all-reduce(f32[120]{0:T(128)S(1)} %get-tuple-element.47, f32[15360]{0:T(1024)S(1)} %multiply_reduce_fusion), channel_id=1, replica_groups=mesh['apa'=4,'tick'=32] {'tick'}, use_global_device_ids=true, to_apply=%region_7.8 | all-reduce | flops 15480 | bytes 123840 | tf_op jit(solution)/shard_map/psum | solution.py:162
  208.6 91.2 %gather_fusion.2 = f32[15360]{0:T(1024)S(1)} fusion(f32[120]{0:T(128)S(1)} %get-tuple-element.5, s32[15360]{0:T(1024)S(1)} %fusion.76), kind=kCustom, calls=%fused_computation.2 | custom fusion | bytes 184320 | tf_op jit(solution)/shard_map/jit(_take)/gather | solution.py:163
  299.9 0.7 reduce-window.6
  300.5 0.2 slice_reduce_fusion
  300.7 0.3 reduce-window.9
  301.1 0.2 fusion.61
  301.4 56.8 %scatter_custom_fusion.1 = f32[26880,100]{1,0:T(8,128)} fusion(s32[15360]{0:T(1024)S(1)} %compare_select_fusion.3, f32[15360,100]{1,0:T(8,128)} %copy.91, f32[15360,100]{1,0:T(8,128)} %gather_fusion.1, f32[]{:T(128)} %constant.206.clone.1, f32[15360]{0:T(1024)S(1)} %add_divide_fusion, f32[]{:T(128)} %constant.224.clone.1, ...), kind=kCustom, calls=%fused_computation.39 | custom fusion | flops 6144000 | bytes 23178248 | tf_op jit(solution)/shard_map/scatter | solution.py:138
  358.2 9.5 fusion.182
  367.7 8.0 copy.92
  375.8 1.6 collective-permute-start.1
  377.4 91.2 %gather_fusion = s32[15360]{0:T(1024)S(1)} fusion(s32[128]{0:T(128)S(1)} %copy-done, s32[15360]{0:T(1024)S(1)} %fusion.84), kind=kCustom, calls=%fused_computation | custom fusion | bytes 184320 | tf_op jit(solution)/shard_map/jit(_take)/gather | solution.py:166
  468.7 56.6 %scatter_custom_fusion = s32[26880]{0:T(1024)S(1)} fusion(s32[15360]{0:T(1024)S(1)} %compare_select_fusion.3, s32[15360]{0:T(1024)S(1)} %fusion.66, s32[]{:T(128)} %constant.207.clone.1), kind=kCustom, calls=%fused_computation.128 | custom fusion | bytes 107524 | tf_op jit(solution)/shard_map/scatter | solution.py:140
  525.3 0.3 collective-permute-start
  525.7 2.7 collective-permute-done
  528.5 0.3 fusion.63
  528.8 7.9 copy.93
  536.7 104.0 %scatter_custom_fusion.2 = f32[15360,100]{1,0:T(8,128)} fusion(s32[26880]{0:T(1024)S(1)} %fusion.63, f32[13440,100]{1,0:T(8,128)} %copy.93, f32[]{:T(128)} %constant.247, f32[13440,100]{1,0:T(8,128)} %get-tuple-element.15, f32[]{:T(128)} %constant.206.clone.1), kind=kCustom, calls=%fused_computation.18 | custom fusion | flops 2688000 | bytes 16896008 | tf_op jit(solution)/shard_map/scatter | solution.py:180
  640.7 8.7 copy.95
  649.4 11.7 %all-to-all-start = ((f32[32,480,100]{1,2,0:T(8,128)}), f32[32,480,100]{1,2,0:T(8,128)}, u32[]{:S(2)}, u32[]{:S(2)}) async-start(f32[32,480,100]{1,2,0:T(8,128)} %copy.95), calls=%async_computation | async-start | bytes 13631488 | tf_op jit(solution)/shard_map/all_to_all | solution.py:183
  661.3 0.1 fusion.123
  661.6 0.1 multiply_sine_fusion.1
  661.8 0.2 convolution_bitcast_fusion.2
  662.0 0.1 multiply_subtract_fusion.6
  662.2 0.3 convolution_bitcast_fusion.1
  663.0 0.1 fusion.98
  663.2 0.7 copy.109
  663.9 0.1 fusion.97
  664.0 0.7 copy.110
  665.7 0.2 convolution_bitcast_fusion.3
  665.9 0.1 fusion.124
  666.1 0.8 sine_negate_fusion
  666.9 0.2 fusion.95
  667.0 0.1 multiply_sine_fusion
  667.2 73.9 %all-to-all-done = f32[32,480,100]{1,2,0:T(8,128)} async-done(((f32[32,480,100]{1,2,0:T(8,128)}), f32[32,480,100]{1,2,0:T(8,128)}, u32[]{:S(2)}, u32[]{:S(2)}) %all-to-all-start) | async-done | bytes 6144032 | tf_op jit(solution)/shard_map/all_to_all | solution.py:183
  741.1 7.5 reshape_squeeze.3
  748.6 21.9 %convolution_bitcast_fusion = f32[2,480,50,64]{1,2,0,3:T(8,128)S(1)} fusion(f32[480,50,64,1]{0,2,1,3:T(8,128)} %bitcast.195, f32[1,2,50,50]{3,2,0,1:T(8,128)S(1)} %get-tuple-element.34, f32[1,2,50,50]{3,2,0,1:T(8,128)S(1)} %get-tuple-element.33), kind=kOutput, calls=%fused_computation.34 | convolution fusion | flops 1843204992 | bytes 18472000 | tf_op jit(solution)/shard_map/akm,cmj->ackj/dot_general | solution.py:56
  770.5 6.2 multiply_subtract_fusion.1
  776.7 12.7 %maximum_bitcast_fusion.1 = f32[2,480,50,64,1]{1,2,0,3,4:T(8,128)} fusion(f32[1,480,50,64]{1,2,0,3:T(8,128)} %get-tuple-element.14, f32[1,480,50,64]{1,2,0,3:T(8,128)} %get-tuple-element.13), kind=kLoop, calls=%fused_computation.15 | loop fusion | flops 3072000 | bytes 24576000 | tf_op jit(solution)/shard_map/stack | solution.py:49
  789.4 21.3 %fusion.27 = f32[2,480,50,64]{1,3,0,2:T(8,128)} fusion(f32[2,480,50,64,1]{1,2,0,3,4:T(8,128)} %maximum_bitcast_fusion.1, f32[1,2,64,64]{2,3,1,0:T(8,128)S(1)} %get-tuple-element.32, f32[1,2,64,64]{2,3,1,0:T(8,128)S(1)} %get-tuple-element.31), kind=kOutput, calls=%fused_computation.35 | convolution fusion | flops 4718608384 | bytes 24641536 | tf_op jit(solution)/shard_map/abjl,bckj->ackl/dot_general | solution.py:65
  810.7 19.4 %copy.99 = f32[2,480,50,64]{3,2,1,0:T(8,128)} copy(f32[2,480,50,64]{1,3,0,2:T(8,128)} %fusion.27) | data formatting | bytes 24576000 | tf_op jit(solution)/shard_map/abjl,bckj->ackl/transpose | solution.py:65
  830.1 21.4 %reshape_reshape.6 = f32[2,20,24,3200]{3,2,1,0:T(8,128)} reshape(f32[2,480,50,64]{3,2,1,0:T(8,128)} %copy.99) | data formatting | bytes 24576000 | tf_op jit(solution)/shard_map/reshape;reshape | solution.py:104
  851.5 20.2 %fusion.21 = f32[2,20,24,3200]{3,1,2,0:T(8,128)S(1)} fusion(f32[2,20,24,3200]{3,2,1,0:T(8,128)} %reshape_reshape.6, f32[1,2,20,20]{3,2,1,0:T(8,128)S(1)} %get-tuple-element.46, f32[1,2,20,20]{3,2,1,0:T(8,128)S(1)} %get-tuple-element.45), kind=kOutput, calls=%fused_computation.32 | convolution fusion | flops 1474561536 | bytes 24582400 | tf_op jit(solution)/shard_map/abkm,bmjc->akjc/dot_general | solution.py:101
  871.7 6.2 multiply_subtract_fusion
  877.9 11.4 %maximum_bitcast_fusion = f32[2,20,24,3200,1]{3,1,2,0,4:T(8,128)} fusion(f32[1,20,24,3200]{3,1,2,0:T(8,128)} %get-tuple-element.12, f32[1,20,24,3200]{3,1,2,0:T(8,128)} %get-tuple-element.11), kind=kLoop, calls=%fused_computation.8 | loop fusion | flops 3072000 | bytes 24576000 | tf_op jit(solution)/shard_map/stack | solution.py:49
  889.3 16.9 %fusion.33 = f32[2,20,24,3200]{3,2,0,1:T(8,128)S(1)} fusion(f32[2,20,24,3200,1]{3,1,2,0,4:T(8,128)} %maximum_bitcast_fusion, f32[1,2,24,24]{2,3,1,0:T(8,128)S(1)} %get-tuple-element.44, f32[1,2,24,24]{2,3,1,0:T(8,128)S(1)} %get-tuple-element.43), kind=kOutput, calls=%fused_computation.37 | convolution fusion | flops 1769474304 | bytes 24585216 | tf_op jit(solution)/shard_map/abjl,bkjc->aklc/dot_general | solution.py:110
  906.1 4.7 multiply_subtract_fusion.4
  910.9 11.8 %fusion.36 = f32[2,20,24,3200]{3,2,0,1:T(8,128)S(1)} fusion(f32[1,20,24,3200]{3,2,0,1:T(8,128)S(1)} %get-tuple-element.20, f32[1,20,24,3200]{3,2,0,1:T(8,128)S(1)} %get-tuple-element.19, f32[1,2,24,24]{2,3,1,0:T(8,128)S(1)} %get-tuple-element.42, f32[1,2,24,24]{2,3,1,0:T(8,128)S(1)} %get-tuple-element.41), kind=kOutput, calls=%fused_computation.38 | convolution fusion | flops 1772546304 | bytes 24585216 | tf_op jit(solution)/shard_map/ablj,bklc->akjc/dot_general | solution.py:118
  922.7 3.6 multiply_subtract_fusion.3
  926.3 8.1 pad_maximum_fusion.1
  934.3 23.4 %fusion.24 = f32[2,20,24,3200]{3,1,2,0:T(8,128)} fusion(f32[2,20,24,3200]{3,2,0,1:T(8,128)} %pad_maximum_fusion.1, f32[1,2,20,20]{3,2,1,0:T(8,128)S(1)} %get-tuple-element.40, f32[1,2,20,20]{3,2,1,0:T(8,128)S(1)} %get-tuple-element.39), kind=kOutput, calls=%fused_computation.33 | convolution fusion | flops 1474561536 | bytes 24582400 | tf_op jit(solution)/shard_map/abmk,bkjc->amjc/dot_general | solution.py:127
  957.8 12.0 %copy.107 = f32[2,20,24,3200]{3,2,1,0:T(8,128)} copy(f32[2,20,24,3200]{3,1,2,0:T(8,128)} %fusion.24) | data formatting | bytes 24576000 | tf_op jit(solution)/shard_map/abmk,bkjc->amjc/dot_general | solution.py:127
  969.7 20.4 %reshape_reshape.7 = f32[2,480,50,64]{3,2,1,0:T(8,128)} reshape(f32[2,20,24,3200]{3,2,1,0:T(8,128)} %copy.107) | data formatting | bytes 24576000 | tf_op jit(solution)/shard_map/reshape;reshape | solution.py:76
  990.1 37.4 %fusion.30 = f32[2,480,50,64]{1,3,0,2:T(8,128)} fusion(f32[2,480,50,64,1]{3,2,1,0,4:T(8,128)} %bitcast.193, f32[1,2,64,64]{2,3,1,0:T(8,128)S(1)} %get-tuple-element.30, f32[1,2,64,64]{2,3,1,0:T(8,128)S(1)} %get-tuple-element.29), kind=kOutput, calls=%fused_computation.36 | convolution fusion | flops 4718608384 | bytes 24641536 | tf_op jit(solution)/shard_map/ablj,bckl->ackj/dot_general | solution.py:73
  1027.5 8.5 multiply_subtract_fusion.2
  1036.0 12.5 %pad_maximum_fusion = f32[2,480,50,64]{1,3,0,2:T(8,128)} fusion(f32[1,480,50,64]{1,3,0,2:T(8,128)} %get-tuple-element.18, f32[1,480,50,64]{1,3,0,2:T(8,128)} %get-tuple-element.17), kind=kLoop, calls=%fused_computation.22 | loop fusion | flops 3072000 | bytes 24576000 | tf_op jit(solution)/shard_map/stack | solution.py:49
  1048.5 26.9 %fusion.44 = f32[480,50,64]{0,1,2:T(8,128)S(1)} fusion(f32[2,480,50,64]{1,3,0,2:T(8,128)} %pad_maximum_fusion, f32[1,50,50]{2,1,0:T(8,128)S(1)} %copy-done.3, f32[1,50,50]{2,1,0:T(8,128)S(1)} %copy-done.4), kind=kOutput, calls=%fused_computation.51 | convolution fusion | flops 1844740992 | bytes 18452000 | tf_op jit(solution)/shard_map/bmk,bckj->cmj/dot_general | solution.py:82
  1075.4 6.5 copy.112
  1081.9 8.0 copy.113
  (64 shorter events, 2.4 us)
Async XLA Ops:
  0.0 377.4 %copy-start = (s32[128]{0:T(128)S(1)}, s32[128]{0:T(128)}, u32[]{:S(2)}) copy-start(s32[128]{0:T(128)} %param.13) | copy-start | bytes 1540
  208.6 91.2 %copy-start.2 = (s32[15360]{0:T(1024)S(1)}, s32[15360]{0:T(1024)}, u32[]{:S(2)}) copy-start(s32[15360]{0:T(1024)} %param.11) | copy-start | bytes 184324
  375.8 153.1 %collective-permute-start.1 = (f32[13440,100]{0,1:T(8,128)}, f32[13440,100]{0,1:T(8,128)}, u32[]{:S(2)}, u32[]{:S(2)}) collective-permute-start(f32[13440,100]{0,1:T(8,128)} %copy.92), channel_id=1, source_target_pairs={{0,32},{32,0},{64,96},{96,64},{1,33},{33,1},{65,97},{97,65},{2,34}... | collective-permute-start | bytes 16128008 | tf_op jit(solution)/shard_map/ppermute | solution.py:18
  377.4 91.2 %copy-start.7 = (s32[15360]{0:T(1024)S(1)}, s32[15360]{0:T(1024)}, u32[]{:S(2)}) copy-start(s32[15360]{0:T(1024)} %param.12) | copy-start | bytes 184324
  525.3 3.1 collective-permute-start
  649.4 11.7 %copy-start.8 = (f32[3200]{0:T(1024)S(1)}, f32[3200]{0:T(1024)}, u32[]{:S(2)}) copy-start(f32[3200]{0:T(1024)} %param.15) | copy-start | bytes 38404
  649.4 13.2 %copy-start.9 = (f32[480]{0:T(512)S(1)}, f32[480]{0:T(512)}, u32[]{:S(2)}) copy-start(f32[480]{0:T(512)} %param.14) | copy-start | bytes 5764
  649.4 91.7 %all-to-all-start = ((f32[32,480,100]{1,2,0:T(8,128)}), f32[32,480,100]{1,2,0:T(8,128)}, u32[]{:S(2)}, u32[]{:S(2)}) async-start(f32[32,480,100]{1,2,0:T(8,128)} %copy.95), calls=%async_computation | async-start | bytes 13631488 | tf_op jit(solution)/shard_map/all_to_all | solution.py:183
  990.1 37.4 %copy-start.5 = (f32[50,64]{1,0:T(8,128)S(1)}, f32[50,64]{1,0:T(8,128)}, u32[]{:S(2)}) copy-start(f32[50,64]{1,0:T(8,128)} %copy.109) | copy-start | bytes 38404
  990.1 37.4 %copy-start.6 = (f32[50,64]{1,0:T(8,128)S(1)}, f32[50,64]{1,0:T(8,128)}, u32[]{:S(2)}) copy-start(f32[50,64]{1,0:T(8,128)} %copy.110) | copy-start | bytes 38404
  1036.0 12.5 %copy-start.3 = (f32[1,50,50]{2,1,0:T(8,128)S(1)}, f32[1,50,50]{2,1,0:T(8,128)}, u32[]{:S(2)}) copy-start(f32[1,50,50]{2,1,0:T(8,128)} %get-tuple-element.67) | copy-start | bytes 30004
  1036.0 12.5 %copy-start.4 = (f32[1,50,50]{2,1,0:T(8,128)S(1)}, f32[1,50,50]{2,1,0:T(8,128)}, u32[]{:S(2)}) copy-start(f32[1,50,50]{2,1,0:T(8,128)} %get-tuple-element.68) | copy-start | bytes 30004
  1075.4 14.5 %copy-start.1 = (s32[128]{0:T(128)S(1)}, s32[128]{0:T(128)}, u32[]{:S(2)}) copy-start(s32[128]{0:T(128)} %param.13) | copy-start | bytes 1540
where the time goes:
time: 1100 us; the launch traced here: 1090 us
  local copies, waits for them, and re-layouts  430 us (39%)
  other arithmetic  254 us (23%)
  matrix products  189 us (17%)
  blocking collectives  126 us (11%)
  waiting for transfers between devices  76.6 us (7%)
  starting transfers between devices  13.6 us (1%)
    psum x1, blocking collectives, shards(): covar, power = lax.psum((covar_part, power_part), 'tick')  126 us
    scatter x1, other arithmetic, shards(): owned = owned.at[all_labels].set(all_rows, mode='drop')  104 us
    gather x1, local copies, waits for them, and re-layouts, shards(): wire_shift = jnp.take(plane_offset, chan_plane, axis=0)  91.2 us
    gather x1, local copies, waits for them, and re-layouts, shards(): power_chan = jnp.take(power, local_group, axis=0)  91.2 us
    all_to_all x1, waiting for transfers between devices, shards(): lax.all_to_all(owned, 'tick', split_axis=0, concat_axis=2, tiled=True)[0]  73.9 us
    scatter x1, other arithmetic, pack_rows(): jnp.zeros((dest_count * capacity, cleaned.shape[1]), jnp.float32)  56.8 us
    scatter x1, local copies, waits for them, and re-layouts, pack_rows(): jnp.full((dest_count * capacity,), sentinel, jnp.int32).at[position]  56.6 us
    gather x1, local copies, waits for them, and re-layouts, shards(): spread_common = jnp.take(common, local_group, axis=0)  51.5 us
  transfers between devices with their start and end apart: 3, of which 2 were waited for; matrix products, arithmetic and copies ran while one was open for 14% of the time, Pallas kernels for 0%

commit v1 on v0

v1 whole, which is shorter than its diff:
```python
import math

import jax
import jax.numpy as jnp
import ml_dtypes
import numpy as np
from jax import lax
from jax.experimental import pallas as pl
from jax.experimental.pallas import tpu as pltpu
from jax.sharding import PartitionSpec as P

TICKS = 3200
GROUP = 128
WIRES = 480
SLABS = 32
SLAB = 100
PART = 128
HALF = 256
PIECE = 32
LANES = 5
WIDE = 512
BLOCK = 256
SENT = (32, 32, 24)

highest = lax.Precision.HIGHEST
epsilon_power = 1e-06
regular_term = 0.25
mega = 1024 * 1024


def roomy(size):
    return pltpu.CompilerParams(vmem_limit_bytes=size * mega)


def two_halves(table):
    high = table.astype(ml_dtypes.bfloat16)
    low = (table - high.astype(np.float64)).astype(ml_dtypes.bfloat16)
    return high, low


def split(value):
    high = value.astype(jnp.bfloat16)
    low = (value - high.astype(jnp.float32)).astype(jnp.bfloat16)
    return high, low


def dot(left, right):
    return jnp.dot(left, right, preferred_element_type=jnp.float32)


def three_dot(left_high, left_low, right_high, right_low):
    return dot(left_high, right_high) + (dot(left_high, right_low) + dot(left_low, right_high))


def wire_tables():
    spread = np.outer(np.arange(WIRES // 2 + 1), np.arange(WIRES)) % WIRES
    angle = 2.0 * np.pi * spread / WIRES
    forward = np.zeros((2, HALF, WIRES))
    forward[0, : WIRES // 2 + 1] = np.cos(angle)
    forward[1, : WIRES // 2 + 1] = -np.sin(angle)
    weight = np.full((WIRES // 2 + 1, 1), 2.0)
    weight[0] = weight[-1] = 1.0
    weight /= WIRES * TICKS
    backward = np.zeros((2, HALF, WIRES))
    backward[0, : WIRES // 2 + 1] = weight * np.cos(angle)
    backward[1, : WIRES // 2 + 1] = -weight * np.sin(angle)
    return forward.reshape(2 * HALF, WIRES), backward.reshape(2 * HALF, WIRES).T.copy()


def tick_tables():
    first = np.arange(SLABS)[:, None, None]
    inner = np.arange(SLAB)[None, :, None]
    second = np.arange(SLAB)[None, None, :]
    angle = 2.0 * np.pi * ((inner * first + SLABS * inner * second) % TICKS) / TICKS
    table = np.zeros((SLABS, 2, PART, 2, PART))
    table[:, 0, :SLAB, 0, :SLAB] = np.cos(angle)
    table[:, 1, :SLAB, 1, :SLAB] = np.cos(angle)
    table[:, 0, :SLAB, 1, :SLAB] = -np.sin(angle)
    table[:, 1, :SLAB, 0, :SLAB] = np.sin(angle)
    table = table.reshape(SLABS, HALF, HALF)
    return table, np.swapaxes(table, 1, 2).copy()


def row_order():
    row = np.arange(WIRES)
    place = row - 320
    late = np.where(place % 32 < 20, 320 + place // 32 * 20 + place % 32, 420 + place // 32 * 12 + place % 32 - 20)
    return np.where(row < 320, row, late).astype(np.int32)


def rank_kernel(plane_ref, base_ref, cross_ref, place_ref, count_ref):
    tri_row = lax.broadcasted_iota(jnp.int32, (BLOCK, BLOCK), 0)
    tri_col = lax.broadcasted_iota(jnp.int32, (BLOCK, BLOCK), 1)
    earlier = (tri_row < tri_col).astype(jnp.float32).astype(jnp.bfloat16)
    names = lax.broadcasted_iota(jnp.int32, (2 * SLABS, BLOCK), 0)
    pair_base = base_ref[0]
    cross_side = cross_ref[0]
    chan_count = plane_ref.shape[1]
    local = plane_ref[...] - pair_base
    is_cross = (local // SLABS == cross_side).astype(jnp.float32)
    cross_count = jnp.sum(is_cross, axis=1, keepdims=True) * (1.0 / SLABS)
    before = jnp.zeros((2 * SLABS, 1), jnp.float32)
    for block in range(chan_count // BLOCK):
        part = slice(block * BLOCK, (block + 1) * BLOCK)
        member = (names == local[:, part]).astype(jnp.float32)
        prefix = dot(member.astype(jnp.bfloat16), earlier) + before
        rank = jnp.sum(member * prefix, axis=0, keepdims=True)
        before = before + jnp.sum(member, axis=1, keepdims=True)
        order = (rank + (1.0 - is_cross[:, part]) * cross_count).astype(jnp.int32)
        near = order - 320
        far = order - 420
        near_piece = (near * 205) >> 12
        far_piece = (far * 171) >> 11
        near_row = 320 + near_piece * 32 + (near - near_piece * 20)
        far_row = 340 + far_piece * 32 + (far - far_piece * 12)
        row = jnp.where(order < 320, order, jnp.where(order < 420, near_row, far_row))
        place_ref[:, part] = (local[:, part] % SLABS) * WIRES + row
    count_ref[...] = jnp.broadcast_to(cross_count.astype(jnp.int32), count_ref.shape)


def rank_rows(chan_plane, pair_base, cross_side):
    chan_count = chan_plane.shape[0]
    scalar = pl.BlockSpec(memory_space=pltpu.SMEM)
    whole = pl.BlockSpec(memory_space=pltpu.VMEM)
    place, count = pl.pallas_call(
        rank_kernel,
        in_specs=[whole, scalar, scalar],
        out_specs=[whole, whole],
        out_shape=[
            jax.ShapeDtypeStruct((1, chan_count), jnp.int32),
            jax.ShapeDtypeStruct((8, 128), jnp.int32),
        ],
        compiler_params=roomy(16),
        name="rank_rows",
    )(chan_plane[None, :], pair_base[None], cross_side[None])
    return place[0], count[0, 0]


def pack_kernel(place_ref, group_ref, good_ref, raw_ref, out0, out1, out2, common_ref, source_ref, rows_ref):
    step = pl.program_id(0)
    first = step * BLOCK

    @pl.when(step == 0)
    def clear():
        common_ref[...] = jnp.zeros_like(common_ref)

    group_count = common_ref.shape[0]
    names = lax.broadcasted_iota(jnp.int32, (group_count, BLOCK), 0)
    member = jnp.where(names == group_ref[0], good_ref[0], 0.0).astype(jnp.bfloat16)
    high, low = split(raw_ref[...])
    common_ref[...] += dot(member, high) + dot(member, low)
    for row in range(BLOCK):
        place = place_ref[first + row]
        rows_ref[pl.ds(place, 1), pl.ds(0, SLAB)] = raw_ref[pl.ds(row, 1), :]
        source_ref[place] = first + row

    @pl.when(step == pl.num_programs(0) - 1)
    def lay():
        def one_slot(slot, carry):
            start = pl.multiple_of(slot * WIRES, PIECE)
            for which, out in enumerate((out0, out1, out2)):
                for piece in range(LANES):
                    at = start + (which * LANES + piece) * PIECE
                    out[slot, :, piece * SLAB : (piece + 1) * SLAB] = rows_ref[pl.ds(at, PIECE), pl.ds(0, SLAB)]
            return carry

        lax.fori_loop(0, SLABS, one_slot, 0)


def pack_rows(raw, place, local_group, good_mask):
    chan_count = raw.shape[0]
    group_count = chan_count // GROUP
    steps = chan_count // BLOCK
    packed = jax.ShapeDtypeStruct((SLABS, PIECE, WIDE), jnp.float32)
    fixed = pl.BlockSpec((SLABS, PIECE, WIDE), lambda step, table: (0, 0, 0))
    line = pl.BlockSpec((1, 1, BLOCK), lambda step, table: (step, 0, 0))
    return pl.pallas_call(
        pack_kernel,
        grid_spec=pltpu.PrefetchScalarGridSpec(
            num_scalar_prefetch=1,
            grid=(steps,),
            in_specs=[line, line, pl.BlockSpec((BLOCK, SLAB), lambda step, table: (step, 0))],
            out_specs=[
                fixed,
                fixed,
                fixed,
                pl.BlockSpec((group_count, SLAB), lambda step, table: (0, 0)),
                pl.BlockSpec(memory_space=pltpu.SMEM),
            ],
            scratch_shapes=[pltpu.VMEM((chan_count, 128), jnp.float32)],
        ),
        out_shape=[
            packed,
            packed,
            packed,
            jax.ShapeDtypeStruct((group_count, SLAB), jnp.float32),
            jax.ShapeDtypeStruct((chan_count,), jnp.int32),
        ],
        compiler_params=roomy(40),
        name="pack_rows",
    )(place, local_group.reshape(steps, 1, BLOCK), good_mask.reshape(steps, 1, BLOCK), raw)


def clean_kernel(rows_ref, common_ref, member_ref, good_ref, out_ref, spread_ref, weight_ref, keep_ref):
    member = member_ref[...]

    def gather(slab, sums):
        covar, power = sums
        high, low = split(common_ref[slab])
        spread = dot(member, high) + dot(member, low)
        for piece in range(LANES):
            spread_ref[slab, :, piece * SLAB : (piece + 1) * SLAB] = spread[piece * PIECE : (piece + 1) * PIECE]
        value = rows_ref[slab]
        grouped = spread_ref[slab]
        return covar + value * grouped, power + grouped * grouped

    zero = jnp.zeros((PIECE, WIDE), jnp.float32)
    covar, power = lax.fori_loop(0, SLABS, gather, (zero, zero))
    for piece in range(LANES):
        part = slice(piece * SLAB, (piece + 1) * SLAB)
        covar_row = jnp.sum(covar[:, part], axis=1, keepdims=True) / TICKS
        power_row = jnp.sum(power[:, part], axis=1, keepdims=True) / TICKS
        weight = covar_row / (power_row + epsilon_power)
        weight_ref[:, part] = jnp.broadcast_to(weight, (PIECE, SLAB))
        keep_ref[:, part] = jnp.broadcast_to(good_ref[piece * PIECE : (piece + 1) * PIECE, :], (PIECE, SLAB))

    def apply(slab, carry):
        out_ref[slab] = keep_ref[...] * (rows_ref[slab] - weight_ref[...] * spread_ref[slab])
        return carry

    lax.fori_loop(0, SLABS, apply, 0)


def clean_rows(rows, commons, member, good):
    whole = pl.BlockSpec(memory_space=pltpu.VMEM)
    return pl.pallas_call(
        clean_kernel,
        in_specs=[whole] * 4,
        out_specs=whole,
        out_shape=jax.ShapeDtypeStruct(rows.shape, jnp.float32),
        scratch_shapes=[
            pltpu.VMEM(rows.shape, jnp.float32),
            pltpu.VMEM((PIECE, WIDE), jnp.float32),
            pltpu.VMEM((PIECE, WIDE), jnp.float32),
        ],
        compiler_params=roomy(24),
        name="clean_rows",
    )(rows, commons, member, good)


def wire_kernel_forward(own0, own1, own2, got0, got1, got2, take_ref, high_ref, low_ref, out_ref, rows_ref):
    @pl.when(pl.program_id(0) == 0)
    def clear():
        rows_ref[...] = jnp.zeros_like(rows_ref)

    for slab in range(2):
        for which, (own, got) in enumerate(((own0, got0), (own1, got1), (own2, got2))):
            sent = SENT[which]
            for piece in range(LANES):
                part = slice(piece * SLAB, (piece + 1) * SLAB)
                at = (which * LANES + piece) * PIECE
                mine = own[slab, :, part]
                theirs = got[slab, :, part]
                take = take_ref[at : at + sent, :] > 0.5
                lanes = slice(slab * PART, slab * PART + SLAB)
                rows_ref[at : at + sent, lanes] = jnp.where(take, theirs, mine[:sent])
                if sent < PIECE:
                    rows_ref[at + sent : at + PIECE, lanes] = mine[sent:]
    row_high, row_low = split(rows_ref[...])
    result = three_dot(high_ref[...], low_ref[...], row_high, row_low)
    for slab in range(2):
        for part in range(2):
            out_ref[slab, part] = result[part * HALF : (part + 1) * HALF, slab * PART : (slab + 1) * PART]


def wire_forward(own, got, take, high, low):
    def slabs(size):
        return pl.BlockSpec((2, size, WIDE), lambda step: (step, 0, 0))

    fixed = pl.BlockSpec((2 * HALF, WIRES), lambda step: (0, 0))
    return pl.pallas_call(
        wire_kernel_forward,
        grid=(SLABS // 2,),
        in_specs=[slabs(PIECE)] * 3
        + [slabs(size) for size in SENT]
        + [pl.BlockSpec((WIRES, 1), lambda step: (0, 0)), fixed, fixed],
        out_specs=pl.BlockSpec((2, 2, HALF, PART), lambda step: (step, 0, 0, 0)),
        out_shape=jax.ShapeDtypeStruct((SLABS, 2, HALF, PART), jnp.float32),
        scratch_shapes=[pltpu.VMEM((WIRES, 2 * PART), jnp.float32)],
        compiler_params=roomy(24),
        name="wire_forward",
    )(*own, *got, take, high, low)


def add(first, second):
    return (first[0] + second[0], first[1] + second[1])


def sub(first, second):
    return (first[0] - second[0], first[1] - second[1])


def turn(value, sign):
    if sign < 0:
        return (value[1], -value[0])
    return (-value[1], value[0])


def scaled(value, angle):
    real, imag = math.cos(angle), math.sin(angle)
    if abs(angle) < 1e-12:
        return value
    return (value[0] * real - value[1] * imag, value[0] * imag + value[1] * real)


def four_point(items, sign):
    even_sum, even_diff = add(items[0], items[2]), sub(items[0], items[2])
    odd_sum, odd_diff = add(items[1], items[3]), turn(sub(items[1], items[3]), sign)
    return [add(even_sum, odd_sum), add(even_diff, odd_diff), sub(even_sum, odd_sum), sub(even_diff, odd_diff)]


def eighth(value, count, sign):
    root = math.sqrt(0.5)
    if count == 0:
        return value
    if count == 2:
        return turn(value, sign)
    real, imag = value
    if count == 1:
        return ((real - sign * imag) * root, (imag + sign * real) * root)
    return ((-real - sign * imag) * root, (sign * real - imag) * root)


def eight_point(items, sign):
    even = four_point(items[0::2], sign)
    odd = four_point(items[1::2], sign)
    odd = [eighth(value, count, sign) for count, value in enumerate(odd)]
    return [add(even[k], odd[k]) for k in range(4)] + [sub(even[k], odd[k]) for k in range(4)]


def slab_points(load, store, middle_ref, sign):
    for low in range(8):
        outs = four_point([load(8 * high + low) for high in range(4)], sign)
        for k, value in enumerate(outs):
            value = scaled(value, sign * 2.0 * math.pi * low * k / 32)
            middle_ref[8 * k + low, 0] = value[0]
            middle_ref[8 * k + low, 1] = value[1]
    for k in range(4):
        outs = eight_point([(middle_ref[8 * k + low, 0], middle_ref[8 * k + low, 1]) for low in range(8)], sign)
        for big, value in enumerate(outs):
            store(k + 4 * big, value)


ROWS = 32


def slab_kernel_forward(in_ref, out_ref, middle_ref):
    def some(index, carry):
        rows = pl.ds(pl.multiple_of(index * 8, 8), 8)

        def load(item):
            return (in_ref[item, 0, rows, :], in_ref[item, 1, rows, :])

        def store(item, value):
            out_ref[item, rows, 0:PART] = value[0]
            out_ref[item, rows, PART : 2 * PART] = value[1]

        slab_points(load, store, middle_ref, -1)
        return carry

    lax.fori_loop(0, ROWS // 8, some, 0)


def slab_kernel_backward(in_ref, out_ref, middle_ref):
    def some(index, carry):
        rows = pl.ds(pl.multiple_of(index * 8, 8), 8)

        def load(item):
            return (in_ref[item, rows, 0:PART], in_ref[item, rows, PART : 2 * PART])

        def store(item, value):
            out_ref[item, 0, rows, :] = value[0]
            out_ref[item, 1, rows, :] = value[1]

        slab_points(load, store, middle_ref, 1)
        return carry

    lax.fori_loop(0, ROWS // 8, some, 0)


def slab_transform(data, forward):
    parted = pl.BlockSpec((SLABS, 2, ROWS, PART), lambda step: (0, 0, step, 0))
    joined = pl.BlockSpec((SLABS, ROWS, HALF), lambda step: (0, step, 0))
    shape = (SLABS, HALF, HALF) if forward else (SLABS, 2, HALF, PART)
    return pl.pallas_call(
        slab_kernel_forward if forward else slab_kernel_backward,
        grid=(HALF // ROWS,),
        in_specs=[parted if forward else joined],
        out_specs=joined if forward else parted,
        out_shape=jax.ShapeDtypeStruct(shape, jnp.float32),
        scratch_shapes=[pltpu.VMEM((SLABS, 2, 8, PART), jnp.float32)],
        compiler_params=roomy(24),
        name="slab_forward" if forward else "slab_backward",
    )(data)


def filter_kernel(in_ref, high_ref, low_ref, filter_ref, back_high_ref, back_low_ref, out_ref):
    for item in range(in_ref.shape[0]):
        data_high, data_low = split(in_ref[item])
        spectrum = three_dot(data_high, data_low, high_ref[item], low_ref[item])
        real, imag = spectrum[:, :PART], spectrum[:, PART:]
        filter_real, filter_imag = filter_ref[item, :, :PART], filter_ref[item, :, PART:]
        mixed = jnp.concatenate(
            [real * filter_real - imag * filter_imag, real * filter_imag + imag * filter_real], axis=1
        )
        mixed_high, mixed_low = split(mixed)
        out_ref[item] = three_dot(mixed_high, mixed_low, back_high_ref[item], back_low_ref[item])


def filter_ticks(data, high, low, filters, back_high, back_low):
    some = pl.BlockSpec((2, HALF, HALF), lambda step: (step, 0, 0))
    return pl.pallas_call(
        filter_kernel,
        grid=(SLABS // 2,),
        in_specs=[some] * 6,
        out_specs=some,
        out_shape=jax.ShapeDtypeStruct((SLABS, HALF, HALF), jnp.float32),
        compiler_params=roomy(24),
        name="filter_ticks",
    )(data, high, low, filters, back_high, back_low)


def wire_kernel_backward(in_ref, high_ref, low_ref, out_ref):
    for pair in range(SLABS // 2):
        both = jnp.concatenate(
            [in_ref[2 * pair + slab].reshape(2 * HALF, PART) for slab in range(2)], axis=1
        )
        data_high, data_low = split(both)
        result = three_dot(high_ref[...], low_ref[...], data_high, data_low)
        for slab in range(2):
            at = (2 * pair + slab) * SLAB
            out_ref[:, at : at + SLAB] = result[:, slab * PART : slab * PART + SLAB]


def wire_backward(data, high, low):
    whole = pl.BlockSpec(memory_space=pltpu.VMEM)
    return pl.pallas_call(
        wire_kernel_backward,
        in_specs=[whole] * 3,
        out_specs=whole,
        out_shape=jax.ShapeDtypeStruct((WIRES, TICKS), jnp.float32),
        compiler_params=roomy(40),
        name="wire_backward",
    )(data, high, low)


def make_filter(wire_kernel, time_kernel):
    forward, _ = wire_tables()
    wire_resp = jnp.dot(forward.astype(np.float32), wire_kernel, precision=highest).reshape(2, 1, HALF, 1)
    first = np.arange(SLABS)
    angle = 2.0 * np.pi * (np.outer(first, first) % SLABS) / SLABS
    slabs = time_kernel.reshape(SLABS, SLAB)
    real = jnp.dot(np.cos(angle).astype(np.float32), slabs, precision=highest)
    imag = jnp.dot(-np.sin(angle).astype(np.float32), slabs, precision=highest)
    twist = 2.0 * np.pi * np.outer(first, np.arange(SLAB)) / TICKS
    cosine, sine = np.cos(twist).astype(np.float32), np.sin(twist).astype(np.float32)
    real, imag = real * cosine + imag * sine, imag * cosine - real * sine
    inner = np.arange(SLAB)
    angle = 2.0 * np.pi * (np.outer(inner, inner) % SLAB) / SLAB
    cosine, sine = np.cos(angle).astype(np.float32), np.sin(angle).astype(np.float32)
    both = jnp.dot(
        jnp.concatenate([real, imag], axis=1),
        np.block([[cosine, -sine], [sine, cosine]]).astype(np.float32),
        precision=highest,
    )
    time_resp = jnp.pad(both.reshape(SLABS, 2, SLAB), ((0, 0), (0, 0), (0, PART - SLAB)))
    time_real, time_imag = time_resp[:, 0][:, None, :], time_resp[:, 1][:, None, :]
    real = wire_resp[0] * time_real - wire_resp[1] * time_imag
    imag = wire_resp[0] * time_imag + wire_resp[1] * time_real
    denominator = real * real + imag * imag + regular_term
    return jnp.concatenate([real / denominator, -imag / denominator], axis=2)


def deconvolve(own, got, take, wires, filters):
    wire_high, wire_low = two_halves(wire_tables()[0])
    picked = (jnp.arange(WIRES, dtype=jnp.int32)[:, None] == wires[None, :]).astype(jnp.bfloat16)
    high = dot(jnp.asarray(wire_high), picked).astype(jnp.bfloat16)
    low = dot(jnp.asarray(wire_low), picked).astype(jnp.bfloat16)
    back_high, back_low = two_halves(wire_tables()[1])
    tick_forward, tick_backward = tick_tables()
    spectrum = wire_forward(own, got, take, high, low)
    spectrum = slab_transform(spectrum, True)
    spectrum = filter_ticks(spectrum, *two_halves(tick_forward), filters, *two_halves(tick_backward))
    spectrum = slab_transform(spectrum, False)
    return wire_backward(spectrum, back_high, back_low)


def shards(raw, bad, group_id, chan_plane, chan_wire, plane_offset, wire_kernel, time_kernel):
    chan_count = raw.shape[0]
    group_count = chan_count // GROUP
    apa_index = lax.axis_index("apa")
    tick_index = lax.axis_index("tick")
    swap = [(i, i ^ 1) for i in range(lax.axis_size("apa"))]
    local_group = group_id - apa_index * group_count
    good_mask = 1.0 - bad.astype(jnp.float32)
    pair_base = (apa_index // 2 * 2 * SLABS).astype(jnp.int32)
    cross_side = (1 - apa_index % 2).astype(jnp.int32)
    place, cross_count = rank_rows(chan_plane, pair_base, cross_side)
    *packed, common, source = pack_rows(raw, place, local_group, good_mask)
    commons = lax.all_gather(common, "tick")
    mine = lax.dynamic_slice(source, (tick_index * WIRES,), (WIRES,))
    row_group = jnp.take(local_group, mine)
    row_good = jnp.take(good_mask, mine)[:, None]
    row_plane = jnp.take(chan_plane, mine)
    row_wire = (jnp.take(chan_wire, mine) + jnp.take(plane_offset, row_plane)) % WIRES
    member = (row_group[:, None] == jnp.arange(group_count, dtype=jnp.int32)[None, :]).astype(jnp.bfloat16)
    take = jnp.asarray(row_order()) < cross_count
    wires = jnp.where(take, lax.ppermute(row_wire, "apa", swap), row_wire)
    filters = make_filter(wire_kernel, time_kernel)
    own, got = [], []
    for which, rows in enumerate(packed):
        rows = lax.all_to_all(rows, "tick", split_axis=0, concat_axis=0, tiled=True)
        part = slice(which * PIECE * LANES, (which + 1) * PIECE * LANES)
        cleaned = clean_rows(rows, commons, member[part], row_good[part])
        own.append(cleaned)
        got.append(lax.ppermute(cleaned[:, : SENT[which]], "apa", swap))
    return deconvolve(own, got, take.astype(jnp.float32)[:, None], wires, filters)[None]


def solution(mesh):
    placed = (P("apa", "tick"), P("apa"), P("apa"), P("apa"), P("apa"), P(), P(), P())
    return jax.shard_map(
        shards,
        mesh=mesh,
        in_specs=placed,
        out_specs=P(("apa", "tick"), None, None),
        check_vma=False,
    )
```

time: 1100 us -> 370 us (0.34)
  local copies, waits for them, and re-layouts: 430 us -> 42.2 us
  other arithmetic: 254 us -> 8.51 us
  matrix products: 189 us -> 5.32 us
  Pallas kernels: 0 us -> 117 us
  blocking collectives: 126 us -> 37.9 us
  waiting for transfers between devices: 76.6 us -> 129 us
  between operations: 0.63 us -> 14 us
    gather x3 -> x5, local copies, waits for them, and re-layouts: 234 us -> 15.9 us  [the longest x1 3.35 us: shards(): jnp.take(plane_offset, row_plane)]
    dot_general x13 -> x7, matrix products: 189 us -> 5.32 us  [the longest x2 2.82 us: dot(): return jnp.dot(left, right, preferred_element_type=jnp.float32)]
    scatter x2 -> x0, other arithmetic: 161 us -> none  [the longest x1 104 us: shards(): owned = owned.at[all_labels].set(all_rows, mode='drop')]
    psum x1 -> x0, blocking collectives: 126 us -> none  [shards(): covar, power = lax.psum((covar_part, power_part), 'tick')]
    pallas_call x0 -> x10, Pallas kernels: none -> 117 us  [the longest x3 31.5 us: clean_rows(): pl.pallas_call(clean_kernel, in_specs=[whole] * 4, out_specs=whole, out_s...]
    ppermute x2 -> x4, waiting for transfers between devices: 2.73 us -> 88.5 us  [the longest x3 88.5 us: shards(): got.append(lax.ppermute(cleaned[:, :SENT[which]], 'apa', swap))]
    all_to_all x1 -> x2, waiting for transfers between devices: 73.9 us -> 12.9 us  [shards(): rows = lax.all_to_all(rows, 'tick', split_axis=0, concat_axis=0, tiled=True)]
    scatter x1 -> x0, local copies, waits for them, and re-layouts: 56.6 us -> none  [pack_rows(): jnp.full((dest_count * capacity,), sentinel, jnp.int32).at[position]]
  transfers between devices with their start and end apart: 3 -> 7, of which waited for: 2 -> 4; matrix products, arithmetic and copies ran while one was open for 14% -> 10% of each run, Pallas kernels for 0% -> 9%
where the time goes in v1:
time: 370 us; the launch traced here: 368 us
  waiting for transfers between devices  129 us (35%)
  Pallas kernels  117 us (32%)
  local copies, waits for them, and re-layouts  42.2 us (11%)
  blocking collectives  37.9 us (10%)
  starting transfers between devices  14.8 us (4%)
  between operations  14 us (4%)
  other arithmetic  8.51 us (2%)
  matrix products  5.32 us (1%)
    ppermute x3, waiting for transfers between devices, shards(): got.append(lax.ppermute(cleaned[:, :SENT[which]], 'apa', swap))  88.5 us
    all_to_all x1, blocking collectives, shards(): rows = lax.all_to_all(rows, 'tick', split_axis=0, concat_axis=0, tiled=True)  37.9 us
    pallas_call x3, Pallas kernels, clean_rows(): pl.pallas_call(clean_kernel, in_specs=[whole] * 4, out_specs=whole, out_s...  31.5 us
    pallas_call x1, Pallas kernels, pack_rows(): pl.pallas_call(pack_kernel, grid_spec=pltpu.PrefetchScalarGridSpec(num_sc...  30 us
    all_gather x1, waiting for transfers between devices, shards(): commons = lax.all_gather(common, 'tick')  27.5 us
    unnamed x62, local copies, waits for them, and re-layouts  20.3 us
    pallas_call x1, Pallas kernels, wire_forward(): pl.pallas_call(wire_kernel_forward, grid=(SLABS // 2,), in_specs=[slabs(P...  18.1 us
    pallas_call x1, Pallas kernels, filter_ticks(): pl.pallas_call(filter_kernel, grid=(SLABS // 2,), in_specs=[some] * 6, ou...  17.5 us
  transfers between devices with their start and end apart: 7, of which 4 were waited for; matrix products, arithmetic and copies ran while one was open for 10% of the time, Pallas kernels for 9%

profile of v1, /device:TPU:1, one launch (start us, length us, event | category | flops | bytes accessed | tf_op | source)
XLA Modules:
  0.0 368.4 jit_solution(17278631736310094339)
XLA Ops:
  6.5 0.8 convert_subtract_fusion
  7.4 8.5 %copy.48.raw_ref = f32[15360,100]{1,0:T(8,128)} copy(f32[15360,100]{0,1:T(8,128)} %param.25) | data formatting | bytes 12288000 | tf_op args[0]
  16.0 2.2 rank_rows.1
  18.2 3.2 copy-done.4
  21.4 30.0 %pack_rows.1 = (f32[32,32,512]{2,1,0:T(8,128)S(1)}, f32[32,32,512]{2,1,0:T(8,128)S(1)}, f32[32,32,512]{2,1,0:T(8,128)S(1)}, f32[120,100]{1,0:T(8,128)S(1)}, s32[15360]{0:T(1024)S(1)}) custom-call(s32[15360]{0:T(1024)S(1)} %bitcast.36, s32[60,1,256]{2,1,0:T(1,128)S(1)} %bitcast.32, f32[60,1,256]{2,1,0:T(1,128)S(1)} %bitcast.31, f32[15360,100]{1,0:T(8,128)S(1)} %copy-done.4), custom_call_target="tpu_custom_call" | custom-call | tf_op jit(solution)/shard_map/pack_rows/pallas_call | solution.py:177
  51.5 1.3 copy-done.14
  52.8 37.9 %all_to_all.15.rows_ref = f32[32,32,512]{2,1,0:T(8,128)} all-to-all(f32[32,32,512]{2,1,0:T(8,128)S(1)} %get-tuple-element.14), channel_id=1, replica_groups=mesh['apa'=4,'tick'=32] {'tick'}, dimensions={0} | all-to-all | bytes 4194304 | tf_op jit(solution)/shard_map/all_to_all | solution.py:522
  90.7 4.1 %all-to-all-start.2 = ((f32[32,32,512]{2,1,0:T(8,128)}), f32[32,32,512]{2,1,0:T(8,128)S(1)}, u32[]{:S(2)}, u32[]{:S(2)}) async-start(f32[32,32,512]{2,1,0:T(8,128)} %copy-done.15), calls=%async_computation.2 | async-start | bytes 4194304 | tf_op jit(solution)/shard_map/all_to_all | solution.py:522
  94.8 0.0 all-gather.4.cloned.1.call-start
  94.8 0.7 copy.49
  95.5 0.0 all-gather.4.cloned.1.call-update
  95.6 0.1 compare_select_fusion
  95.7 3.1 gather_fusion.2
  98.8 3.1 gather_fusion.4
  102.0 0.0 copy-start.24
  102.0 3.1 gather_fusion.3
  105.1 0.1 compare_select_fusion.1
  105.2 0.0 copy-start.20
  105.3 3.3 gather_fusion.1
  108.7 1.3 collective-permute-start.3
  110.0 0.1 reshape.41
  110.1 0.1 fusion.22
  110.2 12.9 %all-to-all-done.2.rows_ref = f32[32,32,512]{2,1,0:T(8,128)S(1)} async-done(((f32[32,32,512]{2,1,0:T(8,128)}), f32[32,32,512]{2,1,0:T(8,128)S(1)}, u32[]{:S(2)}, u32[]{:S(2)}) %all-to-all-start.2) | async-done | bytes 2097184 | tf_op jit(solution)/shard_map/all_to_all | solution.py:522
  123.2 6.8 %all-to-all-start.1 = ((f32[32,32,512]{2,1,0:T(8,128)}), f32[32,32,512]{2,1,0:T(8,128)}, u32[]{:S(2)}, u32[]{:S(2)}) async-start(f32[32,32,512]{2,1,0:T(8,128)} %copy-done.14), calls=%async_computation.1 | async-start | bytes 4194304 | tf_op jit(solution)/shard_map/all_to_all | solution.py:522
  129.9 0.1 fusion.21
  130.1 3.2 gather_fusion
  133.3 0.2 fusion.12
  133.4 1.1 convolution_add_fusion
  134.5 0.1 reshape.42
  134.6 0.1 fusion.19
  134.7 0.1 copy.53.good_ref
  134.8 0.1 copy.55.good_ref
  135.0 0.1 copy.51.good_ref
  135.1 1.0 fusion.20
  136.1 0.1 fusion.6
  136.3 27.5 %all-gather.4.cloned.1.call-done = f32[32,120,100]{1,2,0:T(8,128)} async-done(((f32[1,120,100]{1,2,0:T(8,128)}), f32[32,120,100]{1,2,0:T(8,128)}) %all-gather.4.cloned.1.call-update) | async-done | bytes 1536016 | tf_op jit(solution)/shard_map/all_gather | solution.py:510
  163.8 1.8 copy.50.common_ref
  165.6 1.6 copy-done.9
  167.2 9.1 %clean_rows.5.own2 = f32[32,32,512]{2,1,0:T(8,128)S(1)} custom-call(f32[32,32,512]{2,1,0:T(8,128)S(1)} %copy-done.9, f32[32,120,100]{2,1,0:T(8,128)S(1)} %copy.50.common_ref, bf16[160,120]{1,0:T(8,128)(2,1)S(1)} %get-tuple-element.22.member_ref, f32[160,1]{1,0:T(8,128)S(1)} %copy.55.good_ref), custom_call_target="tpu_custom_call" | custom-call | tf_op jit(solution)/shard_map/clean_rows/pallas_call | solution.py:236
  176.3 1.4 slice.79
  177.7 1.3 copy-done.5
  179.0 1.2 collective-permute-start.2
  180.2 10.4 %clean_rows.3.own0 = f32[32,32,512]{2,1,0:T(8,128)} custom-call(f32[32,32,512]{2,1,0:T(8,128)S(1)} %copy-done.7, f32[32,120,100]{2,1,0:T(8,128)S(1)} %copy.50.common_ref, bf16[160,120]{1,0:T(8,128)(2,1)S(1)} %get-tuple-element.24.member_ref, f32[160,1]{1,0:T(8,128)S(1)} %copy.51.good_ref), custom_call_target="tpu_custom_call" | custom-call | tf_op jit(solution)/shard_map/clean_rows/pallas_call | solution.py:236
  190.6 0.3 collective-permute-start
  190.9 12.0 %clean_rows.4.own1 = f32[32,32,512]{2,1,0:T(8,128)} custom-call(f32[32,32,512]{2,1,0:T(8,128)} %all-to-all-done.1.rows_ref, f32[32,120,100]{2,1,0:T(8,128)S(1)} %copy.50.common_ref, bf16[160,120]{1,0:T(8,128)(2,1)S(1)} %get-tuple-element.23.member_ref, f32[160,1]{1,0:T(8,128)S(1)} %copy.53.good_ref), custom_call_target="tpu_custom_call" | custom-call | tf_op jit(solution)/shard_map/clean_rows/pallas_call | solution.py:236
  202.9 1.2 collective-permute-start.1
  204.1 2.0 fusion
  206.0 0.5 slice.59
  206.6 4.0 %pad_maximum_fusion.filter_ref = f32[32,256,256]{2,1,0:T(8,128)} fusion(f32[32,256,128]{2,1,0:T(8,128)S(1)} %get-tuple-element.26, f32[32,256,128]{2,1,0:T(8,128)S(1)} %get-tuple-element.25), kind=kLoop, calls=%fused_computation.5 | loop fusion | flops 2097152 | bytes 16777216 | tf_op jit(solution)/shard_map/concatenate | solution.py:481
  210.6 0.8 compare_convert_fusion
  211.3 0.1 copy.58.take_ref
  211.5 0.6 compare_select_fusion.2
  212.1 0.5 convolution_convert_fusion
  212.6 0.2 copy.57
  212.8 2.3 convolution_convert_fusion.1
  215.1 1.2 copy.56
  216.4 43.6 %collective-permute-done.got0 = f32[32,32,512]{2,1,0:T(8,128)} collective-permute-done((f32[32,32,512]{2,1,0:T(8,128)}, f32[32,32,512]{2,1,0:T(8,128)}, u32[]{:S(2)}, u32[]{:S(2)}) %collective-permute-start) | collective-permute-done | bytes 2097184 | tf_op jit(solution)/shard_map/ppermute | solution.py:526
  260.0 44.9 %collective-permute-done.1.got1 = f32[32,32,512]{2,1,0:T(8,128)} collective-permute-done((f32[32,32,512]{2,1,0:T(8,128)}, f32[32,32,512]{2,1,0:T(8,128)}, u32[]{:S(2)}, u32[]{:S(2)}) %collective-permute-start.1) | collective-permute-done | bytes 2097184 | tf_op jit(solution)/shard_map/ppermute | solution.py:526
  304.9 18.1 %wire_forward.1.in_ref = f32[32,2,256,128]{3,2,1,0:T(8,128)S(1)} custom-call(f32[32,32,512]{2,1,0:T(8,128)} %clean_rows.3.own0, f32[32,32,512]{2,1,0:T(8,128)} %clean_rows.4.own1, f32[32,32,512]{2,1,0:T(8,128)S(1)} %copy-done.6, f32[32,32,512]{2,1,0:T(8,128)} %collective-permute-done.got0, f32[32,32,512]{2,1,0:T(8,128)} %collective-permute-done.1.got1, ...), custom_call_target="tpu_custom_call" | custom-call | tf_op jit(solution)/shard_map/wire_forward/pallas_call | solution.py:281
  323.1 4.2 %slab_forward.1.in_ref = f32[32,256,256]{2,1,0:T(8,128)S(1)} custom-call(f32[32,2,256,128]{3,2,1,0:T(8,128)S(1)} %wire_forward.1.in_ref), custom_call_target="tpu_custom_call" | custom-call | tf_op jit(solution)/shard_map/slab_forward/pallas_call | solution.py:395
  327.3 3.4 copy-done.3
  330.8 17.5 %filter_ticks.1.in_ref = f32[32,256,256]{2,1,0:T(8,128)S(1)} custom-call(f32[32,256,256]{2,1,0:T(8,128)} %copy-done.3, bf16[32,256,256]{2,1,0:T(8,128)(2,1)S(1)} %copy-done.13, bf16[32,256,256]{2,1,0:T(8,128)(2,1)S(1)} %copy-done.12, f32[32,256,256]{2,1,0:T(8,128)} %pad_maximum_fusion.filter_ref, bf16[32,256,256]{2,1,0:T(8,128)(2,1)S(1)} %copy-done.11, ...), custom_call_target="tpu_custom_call" | custom-call | tf_op jit(solution)/shard_map/filter_ticks/pallas_call | solution.py:422
  348.3 4.0 %slab_backward.1.in_ref = f32[32,2,256,128]{3,2,1,0:T(8,128)S(1)} custom-call(f32[32,256,256]{2,1,0:T(8,128)S(1)} %filter_ticks.1.in_ref), custom_call_target="tpu_custom_call" | custom-call | tf_op jit(solution)/shard_map/slab_backward/pallas_call | solution.py:395
  352.4 9.1 %wire_backward.1 = f32[480,3200]{1,0:T(8,128)} custom-call(f32[32,2,256,128]{3,2,1,0:T(8,128)S(1)} %slab_backward.1.in_ref, bf16[480,512]{1,0:T(8,128)(2,1)S(1)} %copy-done.17, bf16[480,512]{1,0:T(8,128)(2,1)S(1)} %copy-done.16), custom_call_target="tpu_custom_call" | custom-call | tf_op jit(solution)/shard_map/wire_backward/pallas_call | solution.py:447
  (65 shorter events, 0.2 us)
Async XLA Ops:
  6.5 95.4 %copy-start = (s32[15360]{0:T(1024)S(1)}, s32[15360]{0:T(1024)}, u32[]{:S(2)}) copy-start(s32[15360]{0:T(1024)} %param.29) | copy-start | bytes 184324
  7.4 8.6 %copy-start.23 = (s32[15360]{0:T(1024)S(1)}, s32[15360]{0:T(1024)}, u32[]{:S(2)}) copy-start(s32[15360]{0:T(1024)} %param.27) | copy-start | bytes 184324
  7.4 8.6 %copy-start.2 = (s32[15360]{0:T(1024)S(1)}, s32[15360]{0:T(1024)}, u32[]{:S(2)}) copy-start(s32[15360]{0:T(1024)} %param.28) | copy-start | bytes 184324
  18.2 3.2 copy-start.4
  51.4 1.3 copy-start.14
  52.8 37.9 %copy-start.15 = (f32[32,32,512]{2,1,0:T(8,128)}, f32[32,32,512]{2,1,0:T(8,128)S(1)}, u32[]{:S(2)}) copy-start(f32[32,32,512]{2,1,0:T(8,128)S(1)} %get-tuple-element.18) | copy-start | bytes 6291460
  90.7 32.5 %all-to-all-start.2 = ((f32[32,32,512]{2,1,0:T(8,128)}), f32[32,32,512]{2,1,0:T(8,128)S(1)}, u32[]{:S(2)}, u32[]{:S(2)}) async-start(f32[32,32,512]{2,1,0:T(8,128)} %copy-done.15), calls=%async_computation.2 | async-start | bytes 4194304 | tf_op jit(solution)/shard_map/all_to_all | solution.py:522
  94.8 10.5 %copy-start.18 = (s32[128]{0:T(128)S(1)}, s32[128]{0:T(128)}, u32[]{:S(2)}) copy-start(s32[128]{0:T(128)} %param.30) | copy-start | bytes 1540
  94.8 69.0 %all-gather.4.cloned.1.call-start = ((), (), s32[]{:S(2)}) async-start(), calls=%async_computation.3 | async-start | bytes 1757184 | tf_op jit(solution)/shard_map/all_gather | solution.py:510
  95.6 14.3 %copy-start.26 = (f32[3200]{0:T(1024)S(1)}, f32[3200]{0:T(1024)}, u32[]{:S(2)}) copy-start(f32[3200]{0:T(1024)} %param.32) | copy-start | bytes 38404
  95.7 14.4 %copy-start.25 = (f32[32,32]{1,0:T(8,128)S(1)}, f32[32,32]{1,0:T(8,128)}, u32[]{:S(2)}) copy-start(f32[32,32]{1,0:T(8,128)} %constant.131.clone) | copy-start | bytes 12292
  102.0 28.0 %copy-start.24 = (f32[32,32]{1,0:T(8,128)S(1)}, f32[32,32]{1,0:T(8,128)}, u32[]{:S(2)}) copy-start(f32[32,32]{1,0:T(8,128)} %constant.130.clone) | copy-start | bytes 12292
  105.2 28.0 %copy-start.20 = (f32[100,200]{1,0:T(8,128)S(1)}, f32[100,200]{1,0:T(8,128)}, u32[]{:S(2)}) copy-start(f32[100,200]{1,0:T(8,128)} %constant.146) | copy-start | bytes 240004
  105.3 28.0 %copy-start.21 = (f32[32,100]{1,0:T(8,128)S(1)}, f32[32,100]{1,0:T(8,128)}, u32[]{:S(2)}) copy-start(f32[32,100]{1,0:T(8,128)} %constant.133.clone) | copy-start | bytes 38404
  105.3 28.0 %copy-start.22 = (f32[32,100]{1,0:T(8,128)S(1)}, f32[32,100]{1,0:T(8,128)}, u32[]{:S(2)}) copy-start(f32[32,100]{1,0:T(8,128)} %constant.132.clone) | copy-start | bytes 38404
  108.6 26.5 %copy-start.19 = (f32[512,480]{1,0:T(8,128)S(1)}, f32[512,480]{1,0:T(8,128)}, u32[]{:S(2)}) copy-start(f32[512,480]{1,0:T(8,128)} %constant.129.clone) | copy-start | bytes 2949124
  108.7 26.5 %copy-start.28 = (f32[480]{0:T(512)S(1)}, f32[480]{0:T(512)}, u32[]{:S(2)}) copy-start(f32[480]{0:T(512)} %param.31) | copy-start | bytes 5764
  108.7 102.8 %collective-permute-start.3 = (s32[480]{0:T(512)S(1)}, s32[480]{0:T(512)S(1)}, u32[]{:S(2)}, u32[]{:S(2)}) collective-permute-start(s32[480]{0:T(512)S(1)} %get-tuple-element.34), channel_id=1, source_target_pairs={{0,32},{32,0},{64,96},{96,64},{1,33},{33,1},{65,97},{97,65},{2,34}... | collective-permute-start | bytes 5768 | tf_op jit(solution)/shard_map/ppermute | solution.py:518
  123.2 13.1 %copy-start.8 = (f32[32,32,512]{2,1,0:T(8,128)}, f32[32,32,512]{2,1,0:T(8,128)S(1)}, u32[]{:S(2)}) copy-start(f32[32,32,512]{2,1,0:T(8,128)S(1)} %all-to-all-done.2.rows_ref) | copy-start | bytes 6291460
  123.2 67.7 %all-to-all-start.1 = ((f32[32,32,512]{2,1,0:T(8,128)}), f32[32,32,512]{2,1,0:T(8,128)}, u32[]{:S(2)}, u32[]{:S(2)}) async-start(f32[32,32,512]{2,1,0:T(8,128)} %copy-done.14), calls=%async_computation.1 | async-start | bytes 4194304 | tf_op jit(solution)/shard_map/all_to_all | solution.py:522
  165.6 1.6 copy-start.9
  167.2 13.0 %copy-start.7 = (f32[32,32,512]{2,1,0:T(8,128)S(1)}, f32[32,32,512]{2,1,0:T(8,128)}, u32[]{:S(2)}) copy-start(f32[32,32,512]{2,1,0:T(8,128)} %all_to_all.15.rows_ref) | copy-start | bytes 6291460
  177.7 1.3 copy-start.5
  179.0 37.4 %collective-permute-start.2 = (f32[32,24,512]{2,1,0:T(8,128)}, f32[32,24,512]{2,1,0:T(8,128)}, u32[]{:S(2)}, u32[]{:S(2)}) collective-permute-start(f32[32,24,512]{2,1,0:T(8,128)} %slice.79), channel_id=1, source_target_pairs={{0,32},{32,0},{64,96},{96,64},{1,33},{33,1},{65,97},{97,65},{2,34}... | collective-permute-start | bytes 4718600 | tf_op jit(solution)/shard_map/ppermute | solution.py:526
  190.6 69.4 %collective-permute-start = (f32[32,32,512]{2,1,0:T(8,128)}, f32[32,32,512]{2,1,0:T(8,128)}, u32[]{:S(2)}, u32[]{:S(2)}) collective-permute-start(f32[32,32,512]{2,1,0:T(8,128)} %clean_rows.3.own0), channel_id=1, source_target_pairs={{0,32},{32,0},{64,96},{96,64},{1,33},{33,1},{65,97},{97,65},{2,34}... | collective-permute-start | bytes 6291464 | tf_op jit(solution)/shard_map/ppermute | solution.py:526
  202.9 102.1 %collective-permute-start.1 = (f32[32,32,512]{2,1,0:T(8,128)}, f32[32,32,512]{2,1,0:T(8,128)}, u32[]{:S(2)}, u32[]{:S(2)}) collective-permute-start(f32[32,32,512]{2,1,0:T(8,128)} %clean_rows.4.own1), channel_id=1, source_target_pairs={{0,32},{32,0},{64,96},{96,64},{1,33},{33,1},{65,97},{97,65},{2,34}... | collective-permute-start | bytes 6291464 | tf_op jit(solution)/shard_map/ppermute | solution.py:526
  206.6 4.0 %copy-start.27 = (s32[480]{0:T(512)S(1)}, s32[480]{0:T(512)}, u32[]{:S(2)}) copy-start(s32[480]{0:T(512)} %constant.128.clone) | copy-start | bytes 5764
  206.6 5.5 %copy-start.29 = (bf16[512,480]{1,0:T(8,128)(2,1)S(1)}, bf16[512,480]{1,0:T(8,128)(2,1)}, u32[]{:S(2)}) copy-start(bf16[512,480]{1,0:T(8,128)(2,1)} %constant.136.clone) | copy-start | bytes 1474564
  210.6 94.4 %copy-start.6 = (f32[32,32,512]{2,1,0:T(8,128)S(1)}, f32[32,32,512]{2,1,0:T(8,128)}, u32[]{:S(2)}) copy-start(f32[32,32,512]{2,1,0:T(8,128)} %copy-done.5) | copy-start | bytes 6291460
  323.0 7.7 %copy-start.10 = (bf16[32,256,256]{2,1,0:T(8,128)(2,1)S(1)}, bf16[32,256,256]{2,1,0:T(8,128)(2,1)}, u32[]{:S(2)}) copy-start(bf16[32,256,256]{2,1,0:T(8,128)(2,1)} %constant.140.clone.back_low_ref) | copy-start | bytes 12582916
  323.1 7.7 %copy-start.11 = (bf16[32,256,256]{2,1,0:T(8,128)(2,1)S(1)}, bf16[32,256,256]{2,1,0:T(8,128)(2,1)}, u32[]{:S(2)}) copy-start(bf16[32,256,256]{2,1,0:T(8,128)(2,1)} %constant.139.clone.back_high_ref) | copy-start | bytes 12582916
  323.1 7.7 %copy-start.12 = (bf16[32,256,256]{2,1,0:T(8,128)(2,1)S(1)}, bf16[32,256,256]{2,1,0:T(8,128)(2,1)}, u32[]{:S(2)}) copy-start(bf16[32,256,256]{2,1,0:T(8,128)(2,1)} %constant.138.clone.low_ref) | copy-start | bytes 12582916
  323.1 7.7 %copy-start.13 = (bf16[32,256,256]{2,1,0:T(8,128)(2,1)S(1)}, bf16[32,256,256]{2,1,0:T(8,128)(2,1)}, u32[]{:S(2)}) copy-start(bf16[32,256,256]{2,1,0:T(8,128)(2,1)} %constant.137.clone.high_ref) | copy-start | bytes 12582916
  327.3 3.4 copy-start.3
  348.3 4.1 %copy-start.16 = (bf16[480,512]{1,0:T(8,128)(2,1)S(1)}, bf16[480,512]{1,0:T(8,128)(2,1)}, u32[]{:S(2)}) copy-start(bf16[480,512]{1,0:T(8,128)(2,1)} %constant.142.clone.low_ref) | copy-start | bytes 1474564
  348.3 4.1 %copy-start.17 = (bf16[480,512]{1,0:T(8,128)(2,1)S(1)}, bf16[480,512]{1,0:T(8,128)(2,1)}, u32[]{:S(2)}) copy-start(bf16[480,512]{1,0:T(8,128)(2,1)} %constant.141.clone.high_ref) | copy-start | bytes 1474564
  348.3 13.2 %copy-start.1 = (s32[15360]{0:T(1024)S(1)}, s32[15360]{0:T(1024)}, u32[]{:S(2)}) copy-start(s32[15360]{0:T(1024)} %param.29) | copy-start | bytes 184324
Sparse Core Ops, SparseCore 0:
  97.9 65.7 all-gather.3

commit v2 on v1

--- a/solution.py
+++ b/solution.py
@@ -16,11 +16,12 @@
 SLAB = 100
 PART = 128
 HALF = 256
-PIECE = 32
-LANES = 5
-WIDE = 512
+EARLY = 40
+LATE = 60
+EARLY_ROWS = 160
+LATE_ROWS = 80
 BLOCK = 256
-SENT = (32, 32, 24)
+SENT = (80, 80, 56)
 
 highest = lax.Precision.HIGHEST
 epsilon_power = 1e-06
@@ -83,8 +84,9 @@
 
 def row_order():
     row = np.arange(WIRES)
-    place = row - 320
-    late = np.where(place % 32 < 20, 320 + place // 32 * 20 + place % 32, 420 + place // 32 * 12 + place % 32 - 20)
+    piece = (row >= 400).astype(np.int32)
+    place = row - 320 - 80 * piece
+    late = np.where(place < 50, 320 + 50 * piece + place, 420 + 30 * piece + place - 50)
     return np.where(row < 320, row, late).astype(np.int32)
 
 
@@ -107,12 +109,8 @@
         rank = jnp.sum(member * prefix, axis=0, keepdims=True)
         before = before + jnp.sum(member, axis=1, keepdims=True)
         order = (rank + (1.0 - is_cross[:, part]) * cross_count).astype(jnp.int32)
-        near = order - 320
-        far = order - 420
-        near_piece = (near * 205) >> 12
-        far_piece = (far * 171) >> 11
-        near_row = 320 + near_piece * 32 + (near - near_piece * 20)
-        far_row = 340 + far_piece * 32 + (far - far_piece * 12)
+        near_row = order + jnp.where(order >= 370, 30, 0)
+        far_row = order - 50 + jnp.where(order >= 450, 50, 0)
         row = jnp.where(order < 320, order, jnp.where(order < 420, near_row, far_row))
         place_ref[:, part] = (local[:, part] % SLABS) * WIRES + row
     count_ref[...] = jnp.broadcast_to(cross_count.astype(jnp.int32), count_ref.shape)
@@ -136,7 +134,13 @@
     return place[0], count[0, 0]
 
 
-def pack_kernel(place_ref, group_ref, good_ref, raw_ref, out0, out1, out2, common_ref, source_ref, rows_ref):
+def lay_early(slot, rows_ref):
+    start = pl.multiple_of(slot * WIRES, 32)
+    for piece in range(3):
+        yield piece, rows_ref[pl.ds(start + piece * EARLY_ROWS, EARLY_ROWS), 0:EARLY]
+
+
+def pack_kernel(place_ref, group_ref, good_ref, raw_ref, early, out0, out1, out2, common_ref, source_ref, rows_ref, turn_ref):
     step = pl.program_id(0)
     first = step * BLOCK
 
@@ -144,152 +148,214 @@
     def clear():
         common_ref[...] = jnp.zeros_like(common_ref)
 
+    turn_ref[:, 0:SLAB] = raw_ref[...].T
     group_count = common_ref.shape[0]
     names = lax.broadcasted_iota(jnp.int32, (group_count, BLOCK), 0)
     member = jnp.where(names == group_ref[0], good_ref[0], 0.0).astype(jnp.bfloat16)
-    high, low = split(raw_ref[...])
+    high, low = split(turn_ref[:, 0:SLAB])
     common_ref[...] += dot(member, high) + dot(member, low)
     for row in range(BLOCK):
         place = place_ref[first + row]
-        rows_ref[pl.ds(place, 1), pl.ds(0, SLAB)] = raw_ref[pl.ds(row, 1), :]
+        rows_ref[pl.ds(place, 1), :] = turn_ref[pl.ds(row, 1), :]
         source_ref[place] = first + row
 
     @pl.when(step == pl.num_programs(0) - 1)
     def lay():
         def one_slot(slot, carry):
-            start = pl.multiple_of(slot * WIRES, PIECE)
+            for piece, value in lay_early(slot, rows_ref):
+                early[slot, :, piece * EARLY : (piece + 1) * EARLY] = value
+            start = pl.multiple_of(slot * WIRES, 32)
             for which, out in enumerate((out0, out1, out2)):
-                for piece in range(LANES):
-                    at = start + (which * LANES + piece) * PIECE
-                    out[slot, :, piece * SLAB : (piece + 1) * SLAB] = rows_ref[pl.ds(at, PIECE), pl.ds(0, SLAB)]
+                for piece in range(2):
+                    at = start + (which * 2 + piece) * LATE_ROWS
+                    out[slot, :, piece * LATE : (piece + 1) * LATE] = rows_ref[pl.ds(at, LATE_ROWS), EARLY:SLAB]
             return carry
 
         lax.fori_loop(0, SLABS, one_slot, 0)
 
 
-def pack_rows(raw, place, local_group, good_mask):
-    chan_count = raw.shape[0]
+def pack_rows(raw_turned, place, local_group, good_mask):
+    chan_count = raw_turned.shape[1]
     group_count = chan_count // GROUP
     steps = chan_count // BLOCK
-    packed = jax.ShapeDtypeStruct((SLABS, PIECE, WIDE), jnp.float32)
-    fixed = pl.BlockSpec((SLABS, PIECE, WIDE), lambda step, table: (0, 0, 0))
+    sizes = (EARLY_ROWS, LATE_ROWS, LATE_ROWS, LATE_ROWS)
     line = pl.BlockSpec((1, 1, BLOCK), lambda step, table: (step, 0, 0))
     return pl.pallas_call(
         pack_kernel,
         grid_spec=pltpu.PrefetchScalarGridSpec(
             num_scalar_prefetch=1,
             grid=(steps,),
-            in_specs=[line, line, pl.BlockSpec((BLOCK, SLAB), lambda step, table: (step, 0))],
-            out_specs=[
-                fixed,
-                fixed,
-                fixed,
+            in_specs=[line, line, pl.BlockSpec((SLAB, BLOCK), lambda step, table: (0, step))],
+            out_specs=[pl.BlockSpec((SLABS, size, PART), lambda step, table: (0, 0, 0)) for size in sizes]
+            + [
                 pl.BlockSpec((group_count, SLAB), lambda step, table: (0, 0)),
                 pl.BlockSpec(memory_space=pltpu.SMEM),
             ],
-            scratch_shapes=[pltpu.VMEM((chan_count, 128), jnp.float32)],
+            scratch_shapes=[pltpu.VMEM((chan_count, PART), jnp.float32), pltpu.VMEM((BLOCK, PART), jnp.float32)],
         ),
-        out_shape=[
-            packed,
-            packed,
-            packed,
+        out_shape=[jax.ShapeDtypeStruct((SLABS, size, PART), jnp.float32) for size in sizes]
+        + [
             jax.ShapeDtypeStruct((group_count, SLAB), jnp.float32),
             jax.ShapeDtypeStruct((chan_count,), jnp.int32),
         ],
         compiler_params=roomy(40),
         name="pack_rows",
-    )(place, local_group.reshape(steps, 1, BLOCK), good_mask.reshape(steps, 1, BLOCK), raw)
-
-
-def clean_kernel(rows_ref, common_ref, member_ref, good_ref, out_ref, spread_ref, weight_ref, keep_ref):
-    member = member_ref[...]
-
-    def gather(slab, sums):
-        covar, power = sums
-        high, low = split(common_ref[slab])
-        spread = dot(member, high) + dot(member, low)
-        for piece in range(LANES):
-            spread_ref[slab, :, piece * SLAB : (piece + 1) * SLAB] = spread[piece * PIECE : (piece + 1) * PIECE]
-        value = rows_ref[slab]
-        grouped = spread_ref[slab]
-        return covar + value * grouped, power + grouped * grouped
-
-    zero = jnp.zeros((PIECE, WIDE), jnp.float32)
-    covar, power = lax.fori_loop(0, SLABS, gather, (zero, zero))
-    for piece in range(LANES):
-        part = slice(piece * SLAB, (piece + 1) * SLAB)
-        covar_row = jnp.sum(covar[:, part], axis=1, keepdims=True) / TICKS
-        power_row = jnp.sum(power[:, part], axis=1, keepdims=True) / TICKS
-        weight = covar_row / (power_row + epsilon_power)
-        weight_ref[:, part] = jnp.broadcast_to(weight, (PIECE, SLAB))
-        keep_ref[:, part] = jnp.broadcast_to(good_ref[piece * PIECE : (piece + 1) * PIECE, :], (PIECE, SLAB))
-
-    def apply(slab, carry):
-        out_ref[slab] = keep_ref[...] * (rows_ref[slab] - weight_ref[...] * spread_ref[slab])
-        return carry
-
-    lax.fori_loop(0, SLABS, apply, 0)
-
-
-def clean_rows(rows, commons, member, good):
-    whole = pl.BlockSpec(memory_space=pltpu.VMEM)
+    )(place, local_group.reshape(steps, 1, BLOCK), good_mask.reshape(steps, 1, BLOCK), raw_turned)
+
+
+def merge_kernel(place_ref, raw_ref, own_ref, take_ref, out_ref, rows_ref, turn_ref):
+    step = pl.program_id(0)
+    first = step * BLOCK
+    turn_ref[:, 0:EARLY] = raw_ref[...].T
+    for row in range(BLOCK):
+        place = place_ref[first + row]
+        rows_ref[pl.ds(place, 1), :] = turn_ref[pl.ds(row, 1), :]
+
+    @pl.when(step == pl.num_programs(0) - 1)
+    def lay():
+        def one_slot(slot, carry):
+            for piece, value in lay_early(slot, rows_ref):
+                part = slice(piece * EARLY, (piece + 1) * EARLY)
+                take = take_ref[piece * EARLY_ROWS : (piece + 1) * EARLY_ROWS, :] > 0.5
+                out_ref[slot, :, part] = jnp.where(take, value, own_ref[slot, :, part])
+            return carry
+
+        lax.fori_loop(0, SLABS, one_slot, 0)
+
+
+def merge_rows(raw_turned, place, own, take):
+    chan_count = raw_turned.shape[1]
+    steps = chan_count // BLOCK
+    fixed = pl.BlockSpec((SLABS, EARLY_ROWS, PART), lambda step, table: (0, 0, 0))
     return pl.pallas_call(
-        clean_kernel,
-        in_specs=[whole] * 4,
-        out_specs=whole,
-        out_shape=jax.ShapeDtypeStruct(rows.shape, jnp.float32),
+        merge_kernel,
+        grid_spec=pltpu.PrefetchScalarGridSpec(
+            num_scalar_prefetch=1,
+            grid=(steps,),
+            in_specs=[
+                pl.BlockSpec((EARLY, BLOCK), lambda step, table: (0, step)),
+                fixed,
+                pl.BlockSpec((WIRES, 1), lambda step, table: (0, 0)),
+            ],
+            out_specs=fixed,
+            scratch_shapes=[pltpu.VMEM((chan_count, PART), jnp.float32), pltpu.VMEM((BLOCK, PART), jnp.float32)],
+        ),
+        out_shape=jax.ShapeDtypeStruct((SLABS, EARLY_ROWS, PART), jnp.float32),
+        compiler_params=roomy(32),
+        name="merge_rows",
+    )(place, raw_turned, own, take)
+
+
+def spread_common(common_ref, member, both_ref):
+    for slab in range(2):
+        both_ref[:, slab * PART : slab * PART + SLAB] = common_ref[slab]
+    high, low = split(both_ref[...])
+    return dot(member, high) + dot(member, low)
+
+
+def weigh_kernel(early, own0, own1, own2, got0, got1, got2, take_ref, common_ref, member_ref, out_ref, weight_ref, both_ref, covar_ref, power_ref):
+    step = pl.program_id(0)
+
+    @pl.when(step == 0)
+    def clear():
+        both_ref[...] = jnp.zeros_like(both_ref)
+        covar_ref[...] = jnp.zeros_like(covar_ref)
+        power_ref[...] = jnp.zeros_like(power_ref)
+
+    for slab in range(2):
+        base = slab * PART
+        out_ref[0, :, base + SLAB : base + PART] = jnp.zeros((WIRES, PART - SLAB), jnp.float32)
+        for piece in range(3):
+            rows = slice(piece * EARLY_ROWS, (piece + 1) * EARLY_ROWS)
+            out_ref[0, rows, base : base + EARLY] = early[slab, :, piece * EARLY : (piece + 1) * EARLY]
+        for which, (own, got) in enumerate(((own0, got0), (own1, got1), (own2, got2))):
+            sent = SENT[which]
+            for piece in range(2):
+                part = slice(piece * LATE, (piece + 1) * LATE)
+                at = (which * 2 + piece) * LATE_ROWS
+                take = take_ref[at : at + sent, :] > 0.5
+                lanes = slice(base + EARLY, base + SLAB)
+                out_ref[0, at : at + sent, lanes] = jnp.where(take, got[slab, :, part], own[slab, 0:sent, part])
+                if sent < LATE_ROWS:
+                    out_ref[0, at + sent : at + LATE_ROWS, lanes] = own[slab, sent:LATE_ROWS, part]
+    spread = spread_common(common_ref, member_ref[...], both_ref)
+    covar_ref[...] += out_ref[0] * spread
+    power_ref[...] += spread * spread
+
+    @pl.when(step == pl.num_programs(0) - 1)
+    def close():
+        covar = jnp.sum(covar_ref[...], axis=1, keepdims=True) / TICKS
+        power = jnp.sum(power_ref[...], axis=1, keepdims=True) / TICKS
+        weight_ref[...] = covar / (power + epsilon_power)
+
+
+def weigh_rows(early, own, got, take, commons, member):
+    def slabs(size, lanes=PART):
+        return pl.BlockSpec((2, size, lanes), lambda step: (step, 0, 0))
+
+    def fixed(*shape):
+        return pl.BlockSpec(shape, lambda step: (0,) * len(shape))
+
+    pair_groups = commons.shape[1]
+    return pl.pallas_call(
+        weigh_kernel,
+        grid=(SLABS // 2,),
+        in_specs=[slabs(EARLY_ROWS)]
+        + [slabs(LATE_ROWS)] * 3
+        + [slabs(size) for size in SENT]
+        + [fixed(WIRES, 1), slabs(pair_groups, SLAB), fixed(WIRES, pair_groups)],
+        out_specs=[pl.BlockSpec((1, WIRES, HALF), lambda step: (step, 0, 0)), fixed(WIRES, 1)],
+        out_shape=[
+            jax.ShapeDtypeStruct((SLABS // 2, WIRES, HALF), jnp.float32),
+            jax.ShapeDtypeStruct((WIRES, 1), jnp.float32),
+        ],
         scratch_shapes=[
-            pltpu.VMEM(rows.shape, jnp.float32),
-            pltpu.VMEM((PIECE, WIDE), jnp.float32),
-            pltpu.VMEM((PIECE, WIDE), jnp.float32),
+            pltpu.VMEM((pair_groups, HALF), jnp.float32),
+            pltpu.VMEM((WIRES, HALF), jnp.float32),
+            pltpu.VMEM((WIRES, HALF), jnp.float32),
         ],
         compiler_params=roomy(24),
-        name="clean_rows",
-    )(rows, commons, member, good)
-
-
-def wire_kernel_forward(own0, own1, own2, got0, got1, got2, take_ref, high_ref, low_ref, out_ref, rows_ref):
+        name="weigh_rows",
+    )(early, *own, *got, take, commons, member)
+
+
+def wire_kernel_forward(rows_ref, weight_ref, good_ref, common_ref, member_ref, high_ref, low_ref, out_ref, both_ref):
     @pl.when(pl.program_id(0) == 0)
     def clear():
-        rows_ref[...] = jnp.zeros_like(rows_ref)
-
-    for slab in range(2):
-        for which, (own, got) in enumerate(((own0, got0), (own1, got1), (own2, got2))):
-            sent = SENT[which]
-            for piece in range(LANES):
-                part = slice(piece * SLAB, (piece + 1) * SLAB)
-                at = (which * LANES + piece) * PIECE
-                mine = own[slab, :, part]
-                theirs = got[slab, :, part]
-                take = take_ref[at : at + sent, :] > 0.5
-                lanes = slice(slab * PART, slab * PART + SLAB)
-                rows_ref[at : at + sent, lanes] = jnp.where(take, theirs, mine[:sent])
-                if sent < PIECE:
-                    rows_ref[at + sent : at + PIECE, lanes] = mine[sent:]
-    row_high, row_low = split(rows_ref[...])
+        both_ref[...] = jnp.zeros_like(both_ref)
+
+    spread = spread_common(common_ref, member_ref[...], both_ref)
+    cleaned = good_ref[...] * (rows_ref[0] - weight_ref[...] * spread)
+    row_high, row_low = split(cleaned)
     result = three_dot(high_ref[...], low_ref[...], row_high, row_low)
     for slab in range(2):
         for part in range(2):
             out_ref[slab, part] = result[part * HALF : (part + 1) * HALF, slab * PART : (slab + 1) * PART]
 
 
-def wire_forward(own, got, take, high, low):
-    def slabs(size):
-        return pl.BlockSpec((2, size, WIDE), lambda step: (step, 0, 0))
-
-    fixed = pl.BlockSpec((2 * HALF, WIRES), lambda step: (0, 0))
+def wire_forward(rows, weight, good, commons, member, high, low):
+    def fixed(*shape):
+        return pl.BlockSpec(shape, lambda step: (0,) * len(shape))
+
+    pair_groups = commons.shape[1]
     return pl.pallas_call(
         wire_kernel_forward,
         grid=(SLABS // 2,),
-        in_specs=[slabs(PIECE)] * 3
-        + [slabs(size) for size in SENT]
-        + [pl.BlockSpec((WIRES, 1), lambda step: (0, 0)), fixed, fixed],
+        in_specs=[
+            pl.BlockSpec((1, WIRES, HALF), lambda step: (step, 0, 0)),
+            fixed(WIRES, 1),
+            fixed(WIRES, 1),
+            pl.BlockSpec((2, pair_groups, SLAB), lambda step: (step, 0, 0)),
+            fixed(WIRES, pair_groups),
+            fixed(2 * HALF, WIRES),
+            fixed(2 * HALF, WIRES),
+        ],
         out_specs=pl.BlockSpec((2, 2, HALF, PART), lambda step: (step, 0, 0, 0)),
         out_shape=jax.ShapeDtypeStruct((SLABS, 2, HALF, PART), jnp.float32),
-        scratch_shapes=[pltpu.VMEM((WIRES, 2 * PART), jnp.float32)],
+        scratch_shapes=[pltpu.VMEM((pair_groups, HALF), jnp.float32)],
         compiler_params=roomy(24),
         name="wire_forward",
-    )(*own, *got, take, high, low)
+    )(rows, weight, good, commons, member, high, low)
 
 
 def add(first, second):
@@ -481,14 +547,17 @@
     return jnp.concatenate([real / denominator, -imag / denominator], axis=2)
 
 
-def deconvolve(own, got, take, wires, filters):
+def picked_tables(wires):
     wire_high, wire_low = two_halves(wire_tables()[0])
     picked = (jnp.arange(WIRES, dtype=jnp.int32)[:, None] == wires[None, :]).astype(jnp.bfloat16)
-    high = dot(jnp.asarray(wire_high), picked).astype(jnp.bfloat16)
-    low = dot(jnp.asarray(wire_low), picked).astype(jnp.bfloat16)
+    return dot(jnp.asarray(wire_high), picked).astype(jnp.bfloat16), dot(jnp.asarray(wire_low), picked).astype(
+        jnp.bfloat16
+    )
+
+
+def deconvolve(spectrum, filters):
     back_high, back_low = two_halves(wire_tables()[1])
     tick_forward, tick_backward = tick_tables()
-    spectrum = wire_forward(own, got, take, high, low)
     spectrum = slab_transform(spectrum, True)
     spectrum = filter_ticks(spectrum, *two_halves(tick_forward), filters, *two_halves(tick_backward))
     spectrum = slab_transform(spectrum, False)
@@ -500,31 +569,43 @@
     group_count = chan_count // GROUP
     apa_index = lax.axis_index("apa")
     tick_index = lax.axis_index("tick")
+    parity = apa_index % 2
     swap = [(i, i ^ 1) for i in range(lax.axis_size("apa"))]
+    raw_turned = raw.T
+    early_got = lax.ppermute(raw_turned[:EARLY], "apa", swap)
     local_group = group_id - apa_index * group_count
     good_mask = 1.0 - bad.astype(jnp.float32)
     pair_base = (apa_index // 2 * 2 * SLABS).astype(jnp.int32)
-    cross_side = (1 - apa_index % 2).astype(jnp.int32)
-    place, cross_count = rank_rows(chan_plane, pair_base, cross_side)
-    *packed, common, source = pack_rows(raw, place, local_group, good_mask)
-    commons = lax.all_gather(common, "tick")
+    place, cross_count = rank_rows(chan_plane, pair_base, (1 - parity).astype(jnp.int32))
+    place_got = lax.ppermute(place, "apa", swap)
+    early_own, late0, late1, late2, common, source = pack_rows(raw_turned, place, local_group, good_mask)
+    common_got = lax.ppermute(common, "apa", swap)
+    first = jnp.where(parity == 0, common, common_got)
+    second = jnp.where(parity == 0, common_got, common)
+    commons = lax.all_gather(jnp.concatenate([first, second], axis=0), "tick")
     mine = lax.dynamic_slice(source, (tick_index * WIRES,), (WIRES,))
-    row_group = jnp.take(local_group, mine)
-    row_good = jnp.take(good_mask, mine)[:, None]
+    row_group = jnp.take(local_group, mine) + parity * group_count
+    row_bad = jnp.take(bad, mine)
     row_plane = jnp.take(chan_plane, mine)
     row_wire = (jnp.take(chan_wire, mine) + jnp.take(plane_offset, row_plane)) % WIRES
-    member = (row_group[:, None] == jnp.arange(group_count, dtype=jnp.int32)[None, :]).astype(jnp.bfloat16)
+    facts = jnp.stack([row_wire, row_group, row_bad])
     take = jnp.asarray(row_order()) < cross_count
-    wires = jnp.where(take, lax.ppermute(row_wire, "apa", swap), row_wire)
+    facts = jnp.where(take[None, :], lax.ppermute(facts, "apa", swap), facts)
+    row_take = take.astype(jnp.float32)[:, None]
+    row_good = 1.0 - facts[2].astype(jnp.float32)[:, None]
+    member = (facts[1][:, None] == jnp.arange(2 * group_count, dtype=jnp.int32)[None, :]).astype(jnp.bfloat16)
+    high, low = picked_tables(facts[0])
     filters = make_filter(wire_kernel, time_kernel)
     own, got = [], []
-    for which, rows in enumerate(packed):
+    for which, rows in enumerate((late0, late1, late2)):
         rows = lax.all_to_all(rows, "tick", split_axis=0, concat_axis=0, tiled=True)
-        part = slice(which * PIECE * LANES, (which + 1) * PIECE * LANES)
-        cleaned = clean_rows(rows, commons, member[part], row_good[part])
-        own.append(cleaned)
-        got.append(lax.ppermute(cleaned[:, : SENT[which]], "apa", swap))
-    return deconvolve(own, got, take.astype(jnp.float32)[:, None], wires, filters)[None]
+        own.append(rows)
+        got.append(lax.ppermute(rows[:, : SENT[which]], "apa", swap))
+    early = merge_rows(early_got, place_got, early_own, row_take)
+    early = lax.all_to_all(early, "tick", split_axis=0, concat_axis=0, tiled=True)
+    rows, weight = weigh_rows(early, own, got, row_take, commons, member)
+    spectrum = wire_forward(rows, weight, row_good, commons, member, high, low)
+    return deconvolve(spectrum, filters)[None]
 
 
 def solution(mesh):

time: 370 us -> 364 us (0.984)
  Pallas kernels: 117 us -> 163 us
  waiting for transfers between devices: 129 us -> 84.7 us
  blocking collectives: 37.9 us -> 0 us
  starting transfers between devices: 14.8 us -> 35 us
  local copies, waits for them, and re-layouts: 42.2 us -> 48.9 us
    all_to_all x1 -> x0, blocking collectives: 37.9 us -> none  [shards(): rows = lax.all_to_all(rows, 'tick', split_axis=0, concat_axis=0, tiled=True)]
    pallas_call x4 -> x3, Pallas kernels: 49.6 us -> 81.4 us  [the longest x1 44.4 us: merge_rows(): pl.pallas_call(merge_kernel, grid_spec=pltpu.PrefetchScalarGridSpec(num_s...]
    all_gather x1, waiting for transfers between devices: 27.5 us -> 0.02 us  [shards(): commons = lax.all_gather(jnp.concatenate([first, second], axis=0), 'tick')]
    ppermute x4 -> x7, waiting for transfers between devices: 88.5 us -> 70.2 us  [the longest x3 59.9 us: shards(): got.append(lax.ppermute(rows[:, :SENT[which]], 'apa', swap))]
    pallas_call x1, Pallas kernels: 30 us -> 44.3 us  [pack_rows(): pl.pallas_call(pack_kernel, grid_spec=pltpu.PrefetchScalarGridSpec(num_sc...]
    all_to_all x0 -> x1, starting transfers between devices: none -> 9.37 us  [shards(): lax.all_to_all(early, 'tick', split_axis=0, concat_axis=0, tiled=True)]
    all_to_all x2 -> x3, starting transfers between devices: 10.8 us -> 19.7 us  [shards(): rows = lax.all_to_all(rows, 'tick', split_axis=0, concat_axis=0, tiled=True)]
    unnamed x62 -> x67, local copies, waits for them, and re-layouts: 20.3 us -> 17.2 us
  transfers between devices with their start and end apart: 7 -> 12, of which waited for: 4 -> 5; matrix products, arithmetic and copies ran while one was open for 10% -> 13% of each run, Pallas kernels for 9% -> 12%
where the time goes in v2:
time: 364 us; the launch traced here: 360 us
  Pallas kernels  163 us (45%)
  waiting for transfers between devices  84.7 us (23%)
  local copies, waits for them, and re-layouts  48.9 us (13%)
  starting transfers between devices  35 us (10%)
  between operations  14 us (4%)
  other arithmetic  8.64 us (2%)
  matrix products  6.25 us (2%)
    ppermute x3, waiting for transfers between devices, shards(): got.append(lax.ppermute(rows[:, :SENT[which]], 'apa', swap))  59.9 us
    pallas_call x1, Pallas kernels, merge_rows(): pl.pallas_call(merge_kernel, grid_spec=pltpu.PrefetchScalarGridSpec(num_s...  44.4 us
    pallas_call x1, Pallas kernels, pack_rows(): pl.pallas_call(pack_kernel, grid_spec=pltpu.PrefetchScalarGridSpec(num_sc...  44.3 us
    all_to_all x3, starting transfers between devices, shards(): rows = lax.all_to_all(rows, 'tick', split_axis=0, concat_axis=0, tiled=True)  19.7 us
    pallas_call x1, Pallas kernels, weigh_rows(): pl.pallas_call(weigh_kernel, grid=(SLABS // 2,), in_specs=[slabs(EARLY_RO...  19.2 us
    pallas_call x1, Pallas kernels, wire_forward(): pl.pallas_call(wire_kernel_forward, grid=(SLABS // 2,), in_specs=[pl.Bloc...  17.8 us
    pallas_call x1, Pallas kernels, filter_ticks(): pl.pallas_call(filter_kernel, grid=(SLABS // 2,), in_specs=[some] * 6, ou...  17.5 us
    unnamed x67, local copies, waits for them, and re-layouts  17.2 us
  transfers between devices with their start and end apart: 12, of which 5 were waited for; matrix products, arithmetic and copies ran while one was open for 13% of the time, Pallas kernels for 12%

profile of v2, /device:TPU:1, one launch (start us, length us, event | category | flops | bytes accessed | tf_op | source)
XLA Modules:
  0.0 360.5 jit_solution(12027045702242335232)
XLA Ops:
  6.5 0.8 convert_subtract_fusion
  7.4 0.8 broadcast_subtract_fusion
  8.2 0.8 copy-done.2
  9.0 2.1 rank_rows.1
  11.2 2.8 copy-done.7
  14.0 44.3 %pack_rows.1 = (f32[32,160,128]{2,1,0:T(8,128)S(1)}, f32[32,80,128]{2,1,0:T(8,128)}, f32[32,80,128]{2,1,0:T(8,128)}, f32[32,80,128]{2,1,0:T(8,128)}, f32[120,100]{1,0:T(8,128)S(1)}, /*index=5*/s32[15360]{0:T(1024)S(1)}) custom-call(s32[15360]{0:T(1024)S(1)} %bitcast.44, s32[60,1,256]{2,1,0:T(1,128)S(1)} %bitcast.37, f32[60,1,256]{2,1,0:T(1,128)S(1)} %bitcast.43, ...), custom_call_target="tpu_custom_call" | custom-call | tf_op jit(solution)/shard_map/pack_rows/pallas_call | solution.py:183
  58.3 1.5 copy-done.15
  59.8 9.6 %all-to-all-start.1 = ((f32[32,80,128]{2,1,0:T(8,128)}), f32[32,80,128]{2,1,0:T(8,128)}, u32[]{:S(2)}, u32[]{:S(2)}) async-start(f32[32,80,128]{2,1,0:T(8,128)} %get-tuple-element.19), calls=%async_computation.1 | async-start | bytes 2621440 | tf_op jit(solution)/shard_map/all_to_all | solution.py:601
  69.5 1.3 collective-permute-start.5
  70.8 2.2 collective-permute-done.5
  73.1 0.7 copy.43
  73.9 1.3 collective-permute-start
  75.2 3.3 slice.56
  78.5 0.2 collective-permute-start.1
  78.7 10.0 %all-to-all-done.1.own0 = f32[32,80,128]{2,1,0:T(8,128)} async-done(((f32[32,80,128]{2,1,0:T(8,128)}), f32[32,80,128]{2,1,0:T(8,128)}, u32[]{:S(2)}, u32[]{:S(2)}) %all-to-all-start.1) | async-done | bytes 1310752 | tf_op jit(solution)/shard_map/all_to_all | solution.py:601
  88.7 6.1 %all-to-all-start.2 = ((f32[32,80,128]{2,1,0:T(8,128)}), f32[32,80,128]{2,1,0:T(8,128)}, u32[]{:S(2)}, u32[]{:S(2)}) async-start(f32[32,80,128]{2,1,0:T(8,128)} %get-tuple-element.20), calls=%async_computation.2 | async-start | bytes 2621440 | tf_op jit(solution)/shard_map/all_to_all | solution.py:601
  94.9 3.1 gather_fusion.3
  98.1 3.1 gather_fusion.2
  101.3 3.1 gather_fusion.4
  104.5 3.1 gather_fusion.1
  107.7 0.1 compare_select_fusion.1
  107.8 3.3 gather_fusion
  111.2 1.3 collective-permute-start.6
  112.5 0.1 reshape.50
  112.6 0.1 fusion.24
  112.7 0.1 fusion.23
  112.9 4.4 %all-to-all-done.2.own1 = f32[32,80,128]{2,1,0:T(8,128)} async-done(((f32[32,80,128]{2,1,0:T(8,128)}), f32[32,80,128]{2,1,0:T(8,128)}, u32[]{:S(2)}, u32[]{:S(2)}) %all-to-all-start.2) | async-done | bytes 1310752 | tf_op jit(solution)/shard_map/all_to_all | solution.py:601
  117.3 4.0 %all-to-all-start.3 = ((f32[32,80,128]{2,1,0:T(8,128)}), f32[32,80,128]{2,1,0:T(8,128)S(1)}, u32[]{:S(2)}, u32[]{:S(2)}) async-start(f32[32,80,128]{2,1,0:T(8,128)} %get-tuple-element.21), calls=%async_computation.3 | async-start | bytes 2621440 | tf_op jit(solution)/shard_map/all_to_all | solution.py:601
  121.3 0.2 fusion.12
  121.5 0.2 convolution_add_fusion
  121.7 0.1 reshape.51
  121.8 0.5 slice.35
  122.4 0.6 broadcast_compare_fusion
  123.0 0.1 copy.42.take_ref
  123.1 1.0 fusion.22
  124.2 8.1 %collective-permute-done.1.raw_ref = f32[40,15360]{1,0:T(8,128)} collective-permute-done((f32[40,15360]{1,0:T(8,128)}, f32[40,15360]{1,0:T(8,128)}, u32[]{:S(2)}, u32[]{:S(2)}) %collective-permute-start.1) | collective-permute-done | bytes 2457632 | tf_op jit(solution)/shard_map/ppermute | solution.py:575
  132.3 1.7 copy-done.16
  134.0 44.4 %merge_rows.1 = f32[32,160,128]{2,1,0:T(8,128)S(1)} custom-call(s32[15360]{0:T(1024)S(1)} %collective-permute-done.place_ref, f32[40,15360]{1,0:T(8,128)} %collective-permute-done.1.raw_ref, f32[32,160,128]{2,1,0:T(8,128)S(1)} %copy-done.16, f32[480,1]{1,0:T(8,128)S(1)} %copy.42.take_ref), custom_call_target="tpu_custom_call" | custom-call | tf_op jit(solution)/shard_map/merge_rows/pallas_call | solution.py:230
  178.5 1.5 copy-done.8
  180.0 1.1 copy-done.9
  181.0 9.4 %all-to-all-start = ((f32[32,160,128]{2,1,0:T(8,128)}), f32[32,160,128]{2,1,0:T(8,128)S(1)}, u32[]{:S(2)}, u32[]{:S(2)}) async-start(f32[32,160,128]{2,1,0:T(8,128)} %copy-done.8), calls=%async_computation | async-start | bytes 5242880 | tf_op jit(solution)/shard_map/all_to_all | solution.py:605
  190.4 2.0 fusion
  192.4 4.0 %pad_maximum_fusion.filter_ref = f32[32,256,256]{2,1,0:T(8,128)} fusion(f32[32,256,128]{2,1,0:T(8,128)S(1)} %get-tuple-element.31, f32[32,256,128]{2,1,0:T(8,128)S(1)} %get-tuple-element.30), kind=kLoop, calls=%fused_computation.5 | loop fusion | flops 2097152 | bytes 16777216 | tf_op jit(solution)/shard_map/concatenate | solution.py:547
  196.4 0.2 collective-permute-start.3
  196.6 1.2 collective-permute-start.2
  197.9 0.1 copy.48.good_ref
  198.0 2.2 slice.57
  200.2 0.2 collective-permute-start.4
  200.4 2.3 convolution_convert_fusion
  202.8 2.0 copy.47
  204.8 2.3 convolution_convert_fusion.1
  207.1 2.0 copy.46
  209.1 0.1 fusion.6.member_ref
  209.3 5.2 %copy.45.common_ref = f32[32,240,100]{2,1,0:T(8,128)} copy(f32[32,240,100]{1,2,0:T(8,128)} %all-gather.4.cloned.1.call-done) | data formatting | bytes 6144000 | tf_op jit(solution)/shard_map/all_gather | solution.py:585
  214.5 59.9 %collective-permute-done.4.got2 = f32[32,56,128]{2,1,0:T(8,128)} collective-permute-done((f32[32,56,128]{2,1,0:T(8,128)}, f32[32,56,128]{2,1,0:T(8,128)}, u32[]{:S(2)}, u32[]{:S(2)}) %collective-permute-start.4) | collective-permute-done | bytes 917536 | tf_op jit(solution)/shard_map/ppermute | solution.py:603
  274.4 2.1 copy-done.4
  276.5 1.3 copy-done.10
  277.8 19.2 %weigh_rows.1 = (f32[16,480,256]{2,1,0:T(8,128)S(1)}, f32[480,1]{1,0:T(8,128)S(1)}) custom-call(f32[32,160,128]{2,1,0:T(8,128)S(1)} %all-to-all-done.early, f32[32,80,128]{2,1,0:T(8,128)} %all-to-all-done.1.own0, f32[32,80,128]{2,1,0:T(8,128)} %all-to-all-done.2.own1, f32[32,80,128]{2,1,0:T(8,128)S(1)} %copy-done.10, ...), custom_call_target="tpu_custom_call" | custom-call | tf_op jit(solution)/shard_map/weigh_rows/pallas_call | solution.py:300
  297.0 17.8 %wire_forward.1.in_ref = f32[32,2,256,128]{3,2,1,0:T(8,128)S(1)} custom-call(f32[16,480,256]{2,1,0:T(8,128)S(1)} %get-tuple-element.24.rows_ref, f32[480,1]{1,0:T(8,128)S(1)} %get-tuple-element.25.weight_ref, f32[480,1]{1,0:T(8,128)S(1)} %copy.48.good_ref, f32[32,240,100]{2,1,0:T(8,128)S(1)} %copy-done.5, bf16[480,240]{1,0:T(8,128)(2,1)S(1)} %fusion.6.member_ref, ...), custom_call_target="tpu_custom_call" | custom-call | tf_op jit(solution)/shard_map/wire_forward/pallas_call | solution.py:341
  314.9 4.2 %slab_forward.1.in_ref = f32[32,256,256]{2,1,0:T(8,128)S(1)} custom-call(f32[32,2,256,128]{3,2,1,0:T(8,128)S(1)} %wire_forward.1.in_ref), custom_call_target="tpu_custom_call" | custom-call | tf_op jit(solution)/shard_map/slab_forward/pallas_call | solution.py:461
  319.2 3.4 copy-done.6
  322.6 17.5 %filter_ticks.1.in_ref = f32[32,256,256]{2,1,0:T(8,128)S(1)} custom-call(f32[32,256,256]{2,1,0:T(8,128)} %copy-done.6, bf16[32,256,256]{2,1,0:T(8,128)(2,1)S(1)} %copy-done.14, bf16[32,256,256]{2,1,0:T(8,128)(2,1)S(1)} %copy-done.13, f32[32,256,256]{2,1,0:T(8,128)} %pad_maximum_fusion.filter_ref, bf16[32,256,256]{2,1,0:T(8,128)(2,1)S(1)} %copy-done.12, ...), custom_call_target="tpu_custom_call" | custom-call | tf_op jit(solution)/shard_map/filter_ticks/pallas_call | solution.py:488
  340.2 4.0 %slab_backward.1.in_ref = f32[32,2,256,128]{3,2,1,0:T(8,128)S(1)} custom-call(f32[32,256,256]{2,1,0:T(8,128)S(1)} %filter_ticks.1.in_ref), custom_call_target="tpu_custom_call" | custom-call | tf_op jit(solution)/shard_map/slab_backward/pallas_call | solution.py:461
  344.2 9.4 %wire_backward.1 = f32[480,3200]{1,0:T(8,128)} custom-call(f32[32,2,256,128]{3,2,1,0:T(8,128)S(1)} %slab_backward.1.in_ref, bf16[480,512]{1,0:T(8,128)(2,1)S(1)} %copy-done.20, bf16[480,512]{1,0:T(8,128)(2,1)S(1)} %copy-done.19), custom_call_target="tpu_custom_call" | custom-call | tf_op jit(solution)/shard_map/wire_backward/pallas_call | solution.py:513
  (79 shorter events, 0.5 us)
Async XLA Ops:
  6.5 97.9 %copy-start = (s32[15360]{0:T(1024)S(1)}, s32[15360]{0:T(1024)}, u32[]{:S(2)}) copy-start(s32[15360]{0:T(1024)} %param.29) | copy-start | bytes 184324
  8.2 0.8 copy-start.2
  11.2 2.8 copy-start.7
  58.3 1.5 copy-start.15
  59.8 28.9 %all-to-all-start.1 = ((f32[32,80,128]{2,1,0:T(8,128)}), f32[32,80,128]{2,1,0:T(8,128)}, u32[]{:S(2)}, u32[]{:S(2)}) async-start(f32[32,80,128]{2,1,0:T(8,128)} %get-tuple-element.19), calls=%async_computation.1 | async-start | bytes 2621440 | tf_op jit(solution)/shard_map/all_to_all | solution.py:601
  69.4 139.8 %all-gather.4.cloned.1.call-start = ((), (), s32[]{:S(2)}) async-start(), calls=%async_computation.4 | async-start | bytes 3514368 | tf_op jit(solution)/shard_map/all_gather | solution.py:585
  69.5 3.6 collective-permute-start.5
  73.9 24.2 %copy-start.3 = (s32[15360]{0:T(1024)S(1)}, s32[15360]{0:T(1024)}, u32[]{:S(2)}) copy-start(s32[15360]{0:T(1024)} %param.28) | copy-start | bytes 184324
  73.9 50.3 %collective-permute-start = (s32[15360]{0:T(1024)S(1)}, s32[15360]{0:T(1024)S(1)}, u32[]{:S(2)}, u32[]{:S(2)}) collective-permute-start(s32[15360]{0:T(1024)S(1)} %bitcast.45), channel_id=1, source_target_pairs={{0,32},{32,0},{64,96},{96,64},{1,33},{33,1},{65,97},{97,65},{2,34}... | collective-permute-start | bytes 184328 | tf_op jit(solution)/shard_map/ppermute | solution.py:580
  78.5 22.8 %copy-start.22 = (s32[15360]{0:T(1024)S(1)}, s32[15360]{0:T(1024)}, u32[]{:S(2)}) copy-start(s32[15360]{0:T(1024)} %param.26) | copy-start | bytes 184324
  78.5 53.8 %collective-permute-start.1 = (f32[40,15360]{1,0:T(8,128)}, f32[40,15360]{1,0:T(8,128)}, u32[]{:S(2)}, u32[]{:S(2)}) collective-permute-start(f32[40,15360]{1,0:T(8,128)} %slice.56), channel_id=1, source_target_pairs={{0,32},{32,0},{64,96},{96,64},{1,33},{33,1},{65,97},{97,65},{2,34}... | collective-permute-start | bytes 7372808 | tf_op jit(solution)/shard_map/ppermute | solution.py:575
  88.7 28.6 %all-to-all-start.2 = ((f32[32,80,128]{2,1,0:T(8,128)}), f32[32,80,128]{2,1,0:T(8,128)}, u32[]{:S(2)}, u32[]{:S(2)}) async-start(f32[32,80,128]{2,1,0:T(8,128)} %get-tuple-element.20), calls=%async_computation.2 | async-start | bytes 2621440 | tf_op jit(solution)/shard_map/all_to_all | solution.py:601
  94.9 12.9 %copy-start.21 = (s32[128]{0:T(128)S(1)}, s32[128]{0:T(128)}, u32[]{:S(2)}) copy-start(s32[128]{0:T(128)} %param.30) | copy-start | bytes 1540
  98.1 14.4 %copy-start.30 = (f32[3200]{0:T(1024)S(1)}, f32[3200]{0:T(1024)}, u32[]{:S(2)}) copy-start(f32[3200]{0:T(1024)} %param.32) | copy-start | bytes 38404
  98.1 14.5 %copy-start.29 = (f32[32,32]{1,0:T(8,128)S(1)}, f32[32,32]{1,0:T(8,128)}, u32[]{:S(2)}) copy-start(f32[32,32]{1,0:T(8,128)} %constant.120.clone) | copy-start | bytes 12292
  98.1 14.6 %copy-start.28 = (f32[32,32]{1,0:T(8,128)S(1)}, f32[32,32]{1,0:T(8,128)}, u32[]{:S(2)}) copy-start(f32[32,32]{1,0:T(8,128)} %constant.119.clone) | copy-start | bytes 12292
  101.3 20.0 %copy-start.24 = (f32[100,200]{1,0:T(8,128)S(1)}, f32[100,200]{1,0:T(8,128)}, u32[]{:S(2)}) copy-start(f32[100,200]{1,0:T(8,128)} %constant.133) | copy-start | bytes 240004
  101.3 20.0 %copy-start.26 = (f32[32,100]{1,0:T(8,128)S(1)}, f32[32,100]{1,0:T(8,128)}, u32[]{:S(2)}) copy-start(f32[32,100]{1,0:T(8,128)} %constant.122.clone) | copy-start | bytes 38404
  101.3 20.0 %copy-start.27 = (f32[32,100]{1,0:T(8,128)S(1)}, f32[32,100]{1,0:T(8,128)}, u32[]{:S(2)}) copy-start(f32[32,100]{1,0:T(8,128)} %constant.121.clone) | copy-start | bytes 38404
  101.3 20.2 %copy-start.25 = (f32[100,200]{1,0:T(8,128)S(1)}, f32[100,200]{1,0:T(8,128)}, u32[]{:S(2)}) copy-start(f32[100,200]{1,0:T(8,128)} %constant.134) | copy-start | bytes 240004
  104.5 17.9 %copy-start.32 = (s32[480]{0:T(512)S(1)}, s32[480]{0:T(512)}, u32[]{:S(2)}) copy-start(s32[480]{0:T(512)} %constant.115.clone) | copy-start | bytes 5764
  104.5 18.6 %copy-start.23 = (f32[512,480]{1,0:T(8,128)S(1)}, f32[512,480]{1,0:T(8,128)}, u32[]{:S(2)}) copy-start(f32[512,480]{1,0:T(8,128)} %constant.118.clone) | copy-start | bytes 2949124
  104.5 18.6 %copy-start.31 = (f32[480]{0:T(512)S(1)}, f32[480]{0:T(512)}, u32[]{:S(2)}) copy-start(f32[480]{0:T(512)} %param.31) | copy-start | bytes 5764
  111.2 86.7 %collective-permute-start.6 = (s32[3,480]{1,0:T(4,128)S(1)}, s32[3,480]{1,0:T(4,128)S(1)}, u32[]{:S(2)}, u32[]{:S(2)}) collective-permute-start(s32[3,480]{1,0:T(4,128)S(1)} %pad_add_fusion), channel_id=1, source_target_pairs={{0,32},{32,0},{64,96},{96,64},{1,33},{33,1},{65,97},{97,65},{2,34}... | collective-permute-start | bytes 17288 | tf_op jit(solution)/shard_map/ppermute | solution.py:593
  117.3 62.7 %all-to-all-start.3 = ((f32[32,80,128]{2,1,0:T(8,128)}), f32[32,80,128]{2,1,0:T(8,128)S(1)}, u32[]{:S(2)}, u32[]{:S(2)}) async-start(f32[32,80,128]{2,1,0:T(8,128)} %get-tuple-element.21), calls=%async_computation.3 | async-start | bytes 2621440 | tf_op jit(solution)/shard_map/all_to_all | solution.py:601
  132.3 1.7 copy-start.16
  178.5 1.5 copy-start.8
  179.9 1.1 copy-start.9
  181.0 93.4 %all-to-all-start = ((f32[32,160,128]{2,1,0:T(8,128)}), f32[32,160,128]{2,1,0:T(8,128)S(1)}, u32[]{:S(2)}, u32[]{:S(2)}) async-start(f32[32,160,128]{2,1,0:T(8,128)} %copy-done.8), calls=%async_computation | async-start | bytes 5242880 | tf_op jit(solution)/shard_map/all_to_all | solution.py:605
  196.4 78.0 %collective-permute-start.3 = (f32[32,80,128]{2,1,0:T(8,128)}, f32[32,80,128]{2,1,0:T(8,128)}, u32[]{:S(2)}, u32[]{:S(2)}) collective-permute-start(f32[32,80,128]{2,1,0:T(8,128)} %all-to-all-done.2.own1), channel_id=1, source_target_pairs={{0,32},{32,0},{64,96},{96,64},{1,33},{33,1},{65,97},{97,65},{2,34}... | collective-permute-start | bytes 3932168 | tf_op jit(solution)/shard_map/ppermute | solution.py:603
  196.6 77.8 %collective-permute-start.2 = (f32[32,80,128]{2,1,0:T(8,128)}, f32[32,80,128]{2,1,0:T(8,128)}, u32[]{:S(2)}, u32[]{:S(2)}) collective-permute-start(f32[32,80,128]{2,1,0:T(8,128)} %all-to-all-done.1.own0), channel_id=1, source_target_pairs={{0,32},{32,0},{64,96},{96,64},{1,33},{33,1},{65,97},{97,65},{2,34}... | collective-permute-start | bytes 3932168 | tf_op jit(solution)/shard_map/ppermute | solution.py:603
  200.2 74.2 %collective-permute-start.4 = (f32[32,56,128]{2,1,0:T(8,128)}, f32[32,56,128]{2,1,0:T(8,128)}, u32[]{:S(2)}, u32[]{:S(2)}) collective-permute-start(f32[32,56,128]{2,1,0:T(8,128)} %slice.57), channel_id=1, source_target_pairs={{0,32},{32,0},{64,96},{96,64},{1,33},{33,1},{65,97},{97,65},{2,34}... | collective-permute-start | bytes 2752520 | tf_op jit(solution)/shard_map/ppermute | solution.py:603
  274.4 2.1 copy-start.4
  276.5 1.3 copy-start.10
  277.8 19.2 %copy-start.5 = (f32[32,240,100]{2,1,0:T(8,128)S(1)}, f32[32,240,100]{2,1,0:T(8,128)}, u32[]{:S(2)}) copy-start(f32[32,240,100]{2,1,0:T(8,128)} %copy.45.common_ref) | copy-start | bytes 9216004
  277.8 19.2 %copy-start.17 = (bf16[480,512]{0,1:T(8,128)(2,1)S(1)}, bf16[480,512]{0,1:T(8,128)(2,1)}, u32[]{:S(2)}) copy-start(bf16[480,512]{0,1:T(8,128)(2,1)} %copy.47) | copy-start | bytes 1474564
  277.8 19.2 %copy-start.18 = (bf16[480,512]{0,1:T(8,128)(2,1)S(1)}, bf16[480,512]{0,1:T(8,128)(2,1)}, u32[]{:S(2)}) copy-start(bf16[480,512]{0,1:T(8,128)(2,1)} %copy.46) | copy-start | bytes 1474564
  314.9 7.7 %copy-start.11 = (bf16[32,256,256]{2,1,0:T(8,128)(2,1)S(1)}, bf16[32,256,256]{2,1,0:T(8,128)(2,1)}, u32[]{:S(2)}) copy-start(bf16[32,256,256]{2,1,0:T(8,128)(2,1)} %constant.127.clone.back_low_ref) | copy-start | bytes 12582916
  314.9 7.7 %copy-start.12 = (bf16[32,256,256]{2,1,0:T(8,128)(2,1)S(1)}, bf16[32,256,256]{2,1,0:T(8,128)(2,1)}, u32[]{:S(2)}) copy-start(bf16[32,256,256]{2,1,0:T(8,128)(2,1)} %constant.126.clone.back_high_ref) | copy-start | bytes 12582916
  314.9 7.7 %copy-start.13 = (bf16[32,256,256]{2,1,0:T(8,128)(2,1)S(1)}, bf16[32,256,256]{2,1,0:T(8,128)(2,1)}, u32[]{:S(2)}) copy-start(bf16[32,256,256]{2,1,0:T(8,128)(2,1)} %constant.125.clone.low_ref) | copy-start | bytes 12582916
  314.9 7.7 %copy-start.14 = (bf16[32,256,256]{2,1,0:T(8,128)(2,1)S(1)}, bf16[32,256,256]{2,1,0:T(8,128)(2,1)}, u32[]{:S(2)}) copy-start(bf16[32,256,256]{2,1,0:T(8,128)(2,1)} %constant.124.clone.high_ref) | copy-start | bytes 12582916
  319.1 3.4 copy-start.6
  340.1 4.1 %copy-start.19 = (bf16[480,512]{1,0:T(8,128)(2,1)S(1)}, bf16[480,512]{1,0:T(8,128)(2,1)}, u32[]{:S(2)}) copy-start(bf16[480,512]{1,0:T(8,128)(2,1)} %constant.129.clone.low_ref) | copy-start | bytes 1474564
  340.1 4.1 %copy-start.20 = (bf16[480,512]{1,0:T(8,128)(2,1)S(1)}, bf16[480,512]{1,0:T(8,128)(2,1)}, u32[]{:S(2)}) copy-start(bf16[480,512]{1,0:T(8,128)(2,1)} %constant.128.clone.high_ref) | copy-start | bytes 1474564
  340.1 13.5 %copy-start.1 = (s32[15360]{0:T(1024)S(1)}, s32[15360]{0:T(1024)}, u32[]{:S(2)}) copy-start(s32[15360]{0:T(1024)} %param.29) | copy-start | bytes 184324
Sparse Core Ops, SparseCore 0:
  74.0 51.0 all-gather.3

commit v3 on v1

v3 whole, which is shorter than its diff:
```python
import functools
import math

import jax
import jax.numpy as jnp
import ml_dtypes
import numpy as np
from jax import lax
from jax.experimental import pallas as pl
from jax.experimental.pallas import tpu as pltpu
from jax.sharding import PartitionSpec as P

TICKS = 3200
GROUP = 128
WIRES = 480
SLABS = 32
SLAB = 100
PART = 128
HALF = 256
EARLY = 40
LATE = 60
EARLY_ROWS = 160
LATE_ROWS = 120
BLOCK = 256
WIDE = 512
SENT = (120, 96)

highest = lax.Precision.HIGHEST
epsilon_power = 1e-06
regular_term = 0.25
mega = 1024 * 1024


def roomy(size):
    return pltpu.CompilerParams(vmem_limit_bytes=size * mega)


def two_halves(table):
    high = table.astype(ml_dtypes.bfloat16)
    low = (table - high.astype(np.float64)).astype(ml_dtypes.bfloat16)
    return high, low


def split(value):
    high = value.astype(jnp.bfloat16)
    low = (value - high.astype(jnp.float32)).astype(jnp.bfloat16)
    return high, low


def dot(left, right):
    return jnp.dot(left, right, preferred_element_type=jnp.float32)


def three_dot(left_high, left_low, right_high, right_low):
    return dot(left_high, right_high) + (dot(left_high, right_low) + dot(left_low, right_high))


def wire_tables():
    spread = np.outer(np.arange(WIRES // 2 + 1), np.arange(WIRES)) % WIRES
    angle = 2.0 * np.pi * spread / WIRES
    forward = np.zeros((2, HALF, WIRES))
    forward[0, : WIRES // 2 + 1] = np.cos(angle)
    forward[1, : WIRES // 2 + 1] = -np.sin(angle)
    weight = np.full((WIRES // 2 + 1, 1), 2.0)
    weight[0] = weight[-1] = 1.0
    weight /= WIRES * TICKS
    backward = np.zeros((2, HALF, WIRES))
    backward[0, : WIRES // 2 + 1] = weight * np.cos(angle)
    backward[1, : WIRES // 2 + 1] = -weight * np.sin(angle)
    return forward.reshape(2 * HALF, WIRES), backward.reshape(2 * HALF, WIRES).T.copy()


def tick_tables():
    angle = 2.0 * np.pi * (np.outer(np.arange(SLAB), np.arange(SLAB)) % SLAB) / SLAB
    table = np.zeros((2, PART, 2, PART))
    table[0, :SLAB, 0, :SLAB] = table[1, :SLAB, 1, :SLAB] = np.cos(angle)
    table[0, :SLAB, 1, :SLAB] = -np.sin(angle)
    table[1, :SLAB, 0, :SLAB] = np.sin(angle)
    table = table.reshape(HALF, HALF)
    twist = 2.0 * np.pi * np.outer(np.arange(SLABS), np.arange(PART)) / TICKS
    return table, table.T.copy(), np.stack([np.cos(twist), np.sin(twist)], axis=1).astype(np.float32)[:, :, None, :]


def row_order():
    row = np.arange(WIRES)
    piece = (row >= 360).astype(np.int32)
    place = row - 240 - 120 * piece
    late = np.where(place < 90, 240 + 90 * piece + place, 420 + 30 * piece + place - 90)
    return np.where(row < 240, row, late).astype(np.int32)


def rank_kernel(plane_ref, base_ref, cross_ref, place_ref, count_ref):
    tri_row = lax.broadcasted_iota(jnp.int32, (BLOCK, BLOCK), 0)
    tri_col = lax.broadcasted_iota(jnp.int32, (BLOCK, BLOCK), 1)
    earlier = (tri_row < tri_col).astype(jnp.float32).astype(jnp.bfloat16)
    names = lax.broadcasted_iota(jnp.int32, (2 * SLABS, BLOCK), 0)
    pair_base = base_ref[0]
    cross_side = cross_ref[0]
    chan_count = plane_ref.shape[1]
    local = plane_ref[...] - pair_base
    is_cross = (local // SLABS == cross_side).astype(jnp.float32)
    cross_count = jnp.sum(is_cross, axis=1, keepdims=True) * (1.0 / SLABS)
    before = jnp.zeros((2 * SLABS, 1), jnp.float32)
    for block in range(chan_count // BLOCK):
        part = slice(block * BLOCK, (block + 1) * BLOCK)
        member = (names == local[:, part]).astype(jnp.float32)
        prefix = dot(member.astype(jnp.bfloat16), earlier) + before
        rank = jnp.sum(member * prefix, axis=0, keepdims=True)
        before = before + jnp.sum(member, axis=1, keepdims=True)
        order = (rank + (1.0 - is_cross[:, part]) * cross_count).astype(jnp.int32)
        near_row = order + jnp.where(order >= 330, 30, 0)
        far_row = order - 90 + jnp.where(order >= 450, 90, 0)
        row = jnp.where(order < 240, order, jnp.where(order < 420, near_row, far_row))
        place_ref[:, part] = (local[:, part] % SLABS) * WIRES + row
    count_ref[...] = jnp.broadcast_to(cross_count.astype(jnp.int32), count_ref.shape)


def rank_rows(chan_plane, pair_base, cross_side):
    chan_count = chan_plane.shape[0]
    scalar = pl.BlockSpec(memory_space=pltpu.SMEM)
    whole = pl.BlockSpec(memory_space=pltpu.VMEM)
    place, count = pl.pallas_call(
        rank_kernel,
        in_specs=[whole, scalar, scalar],
        out_specs=[whole, whole],
        out_shape=[
            jax.ShapeDtypeStruct((1, chan_count), jnp.int32),
            jax.ShapeDtypeStruct((8, 128), jnp.int32),
        ],
        compiler_params=roomy(16),
        name="rank_rows",
    )(chan_plane[None, :], pair_base[None], cross_side[None])
    return place[0], count[0, 0]


def whole(count):
    return [pl.BlockSpec(memory_space=pltpu.VMEM)] * count


def turned_scatter(place_ref, raw_ref, rows_ref, even_ref, odd_ref):
    ticks, chan_count = raw_ref.shape
    steps = chan_count // WIDE

    def turn_block(step, to_ref):
        at = pl.multiple_of(step * WIDE, WIDE)
        to_ref[:, 0:ticks] = raw_ref[:, pl.ds(at, WIDE)].T

    def move(step, from_ref):
        first = step * WIDE
        for row in range(WIDE):
            rows_ref[pl.ds(place_ref[first + row], 1), :] = from_ref[pl.ds(row, 1), :]

    turn_block(0, even_ref)

    def both(half, carry):
        turn_block(2 * half + 1, odd_ref)
        move(2 * half, even_ref)
        turn_block(jnp.minimum(2 * half + 2, steps - 2), even_ref)
        move(2 * half + 1, odd_ref)
        return carry

    lax.fori_loop(0, steps // 2, both, 0)


def pack_kernel(place_ref, raw_ref, rows_ref, even_ref, odd_ref):
    turned_scatter(place_ref, raw_ref, rows_ref, even_ref, odd_ref)


def pack_rows(place, raw_turned):
    chan_count = raw_turned.shape[1]
    return pl.pallas_call(
        pack_kernel,
        in_specs=[pl.BlockSpec(memory_space=pltpu.SMEM)] + whole(1),
        out_specs=whole(1)[0],
        out_shape=jax.ShapeDtypeStruct((chan_count, PART), jnp.float32),
        scratch_shapes=[pltpu.VMEM((WIDE, PART), jnp.float32)] * 2,
        compiler_params=roomy(32),
        name="pack_rows",
    )(place, raw_turned)


def late_kernel(which, rows_ref, out_ref):
    def one_slot(slot, carry):
        start = pl.multiple_of(slot * WIRES, 8)
        for piece in range(2):
            at = start + (which * 2 + piece) * LATE_ROWS
            out_ref[slot, :, piece * LATE : (piece + 1) * LATE] = rows_ref[pl.ds(at, LATE_ROWS), EARLY:SLAB]
        return carry

    lax.fori_loop(0, SLABS, one_slot, 0)


def lay_late(rows, which):
    return pl.pallas_call(
        functools.partial(late_kernel, which),
        in_specs=whole(1),
        out_specs=whole(1)[0],
        out_shape=jax.ShapeDtypeStruct((SLABS, LATE_ROWS, PART), jnp.float32),
        compiler_params=roomy(24),
        name="lay_late",
    )(rows)


def merge_kernel(place_ref, raw_ref, own_ref, take_ref, out_ref, rows_ref, even_ref, odd_ref):
    turned_scatter(place_ref, raw_ref, rows_ref, even_ref, odd_ref)

    def one_slot(slot, carry):
        start = pl.multiple_of(slot * WIRES, 8)
        for piece in range(3):
            rows = pl.ds(start + piece * EARLY_ROWS, EARLY_ROWS)
            take = take_ref[piece * EARLY_ROWS : (piece + 1) * EARLY_ROWS, :] > 0.5
            value = jnp.where(take, rows_ref[rows, 0:EARLY], own_ref[rows, 0:EARLY])
            out_ref[slot, :, piece * EARLY : (piece + 1) * EARLY] = value
        return carry

    lax.fori_loop(0, SLABS, one_slot, 0)


def merge_rows(place, raw_turned, own, take):
    chan_count = raw_turned.shape[1]
    return pl.pallas_call(
        merge_kernel,
        in_specs=[pl.BlockSpec(memory_space=pltpu.SMEM)] + whole(3),
        out_specs=whole(1)[0],
        out_shape=jax.ShapeDtypeStruct((SLABS, EARLY_ROWS, PART), jnp.float32),
        scratch_shapes=[pltpu.VMEM((chan_count, PART), jnp.float32)] + [pltpu.VMEM((WIDE, PART), jnp.float32)] * 2,
        compiler_params=roomy(40),
        name="merge_rows",
    )(place, raw_turned, own, take)


def across(left, right):
    return lax.dot_general(left, right, (((1,), (1,)), ((), ())), preferred_element_type=jnp.float32)


def group_kernel(raw_ref, group_ref, good_ref, out_ref):
    group_count = out_ref.shape[0]
    names = lax.broadcasted_iota(jnp.int32, (group_count, WIDE), 0)

    def some(step, total):
        part = pl.ds(pl.multiple_of(step * WIDE, WIDE), WIDE)
        member = jnp.where(names == group_ref[:, part], good_ref[:, part], 0.0).astype(jnp.bfloat16)
        high, low = split(raw_ref[:, part])
        return total + (across(member, high) + across(member, low))

    out_ref[...] = lax.fori_loop(0, raw_ref.shape[1] // WIDE, some, jnp.zeros(out_ref.shape, jnp.float32))


def sum_groups(raw_turned, local_group, good_mask):
    group_count = raw_turned.shape[1] // GROUP
    return pl.pallas_call(
        group_kernel,
        in_specs=whole(3),
        out_specs=whole(1)[0],
        out_shape=jax.ShapeDtypeStruct((group_count, SLAB), jnp.float32),
        compiler_params=roomy(24),
        name="sum_groups",
    )(raw_turned, local_group[None, :], good_mask[None, :])


def facts_kernel(place_ref, facts_ref, out_ref):
    names = lax.broadcasted_iota(jnp.int32, (WIRES, BLOCK), 0)

    def some(step, total):
        part = pl.ds(pl.multiple_of(step * BLOCK, BLOCK), BLOCK)
        member = (names == place_ref[:, part]).astype(jnp.float32).astype(jnp.bfloat16)
        return total + across(facts_ref[:, part].astype(jnp.bfloat16), member)

    out_ref[...] = lax.fori_loop(0, place_ref.shape[1] // BLOCK, some, jnp.zeros(out_ref.shape, jnp.float32))


def pick_facts(place, facts):
    return pl.pallas_call(
        facts_kernel,
        in_specs=whole(2),
        out_specs=whole(1)[0],
        out_shape=jax.ShapeDtypeStruct((facts.shape[0], WIRES), jnp.float32),
        compiler_params=roomy(16),
        name="pick_facts",
    )(place[None, :], facts)


def add(first, second):
    return (first[0] + second[0], first[1] + second[1])


def sub(first, second):
    return (first[0] - second[0], first[1] - second[1])


def turn(value, sign):
    if sign < 0:
        return (value[1], -value[0])
    return (-value[1], value[0])


def scaled(value, angle):
    real, imag = math.cos(angle), math.sin(angle)
    if abs(angle) < 1e-12:
        return value
    return (value[0] * real - value[1] * imag, value[0] * imag + value[1] * real)


def four_point(items, sign):
    even_sum, even_diff = add(items[0], items[2]), sub(items[0], items[2])
    odd_sum, odd_diff = add(items[1], items[3]), turn(sub(items[1], items[3]), sign)
    return [add(even_sum, odd_sum), add(even_diff, odd_diff), sub(even_sum, odd_sum), sub(even_diff, odd_diff)]


def eighth(value, count, sign):
    root = math.sqrt(0.5)
    if count == 0:
        return value
    if count == 2:
        return turn(value, sign)
    real, imag = value
    if count == 1:
        return ((real - sign * imag) * root, (imag + sign * real) * root)
    return ((-real - sign * imag) * root, (sign * real - imag) * root)


def eight_point(items, sign):
    even = four_point(items[0::2], sign)
    odd = four_point(items[1::2], sign)
    odd = [eighth(value, count, sign) for count, value in enumerate(odd)]
    return [add(even[k], odd[k]) for k in range(4)] + [sub(even[k], odd[k]) for k in range(4)]


def slab_points(load, store, middle_ref, sign):
    for low in range(8):
        outs = four_point([load(8 * high + low) for high in range(4)], sign)
        for k, value in enumerate(outs):
            value = scaled(value, sign * 2.0 * math.pi * low * k / 32)
            middle_ref[8 * k + low, 0] = value[0]
            middle_ref[8 * k + low, 1] = value[1]
    for k in range(4):
        outs = eight_point([(middle_ref[8 * k + low, 0], middle_ref[8 * k + low, 1]) for low in range(8)], sign)
        for big, value in enumerate(outs):
            store(k + 4 * big, value)


def tail_kernel(
    early,
    own0,
    own1,
    got0,
    got1,
    take_ref,
    good_ref,
    common_ref,
    member_ref,
    high_ref,
    low_ref,
    filter_ref,
    twist_ref,
    tick_high_ref,
    tick_low_ref,
    untick_high_ref,
    untick_low_ref,
    back_high_ref,
    back_low_ref,
    out_ref,
    rows_ref,
    plane_ref,
    both_ref,
    covar_ref,
    power_ref,
    middle_ref,
):
    both_ref[...] = jnp.zeros_like(both_ref)
    covar_ref[...] = jnp.zeros_like(covar_ref)
    power_ref[...] = jnp.zeros_like(power_ref)

    def spread_common(pair):
        for slab in range(2):
            both_ref[:, slab * PART : slab * PART + SLAB] = common_ref[2 * pair + slab]
        high, low = split(both_ref[...])
        return dot(member_ref[...], high) + dot(member_ref[...], low)

    def assemble(pair, carry):
        for half in range(2):
            slab = 2 * pair + half
            base = half * PART
            rows_ref[pair, :, base + SLAB : base + PART] = jnp.zeros((WIRES, PART - SLAB), jnp.float32)
            for piece in range(3):
                rows = slice(piece * EARLY_ROWS, (piece + 1) * EARLY_ROWS)
                rows_ref[pair, rows, base : base + EARLY] = early[slab, :, piece * EARLY : (piece + 1) * EARLY]
            for which, (own, got) in enumerate(((own0, got0), (own1, got1))):
                sent = SENT[which]
                for piece in range(2):
                    part = slice(piece * LATE, (piece + 1) * LATE)
                    at = (which * 2 + piece) * LATE_ROWS
                    take = take_ref[at : at + sent, :] > 0.5
                    lanes = slice(base + EARLY, base + SLAB)
                    rows_ref[pair, at : at + sent, lanes] = jnp.where(take, got[slab, :, part], own[slab, 0:sent, part])
                    if sent < LATE_ROWS:
                        rows_ref[pair, at + sent : at + LATE_ROWS, lanes] = own[slab, sent:LATE_ROWS, part]
        spread = spread_common(pair)
        covar_ref[...] += rows_ref[pair] * spread
        power_ref[...] += spread * spread
        return carry

    lax.fori_loop(0, SLABS // 2, assemble, 0)
    covar = jnp.sum(covar_ref[...], axis=1, keepdims=True) / TICKS
    power = jnp.sum(power_ref[...], axis=1, keepdims=True) / TICKS
    weight = covar / (power + epsilon_power)

    def to_wires(pair, carry):
        cleaned = good_ref[...] * (rows_ref[pair] - weight * spread_common(pair))
        row_high, row_low = split(cleaned)
        result = three_dot(high_ref[...], low_ref[...], row_high, row_low)
        for slab in range(2):
            for part in range(2):
                plane_ref[2 * pair + slab, part] = result[
                    part * HALF : (part + 1) * HALF, slab * PART : (slab + 1) * PART
                ]
        return carry

    lax.fori_loop(0, SLABS // 2, to_wires, 0)

    def slabs_over(index, carry, sign):
        rows = pl.ds(pl.multiple_of(index * 8, 8), 8)

        def load(item):
            real, imag = plane_ref[item, 0, rows, :], plane_ref[item, 1, rows, :]
            if sign < 0:
                return (real, imag)
            cosine, sine = twist_ref[item, 0], twist_ref[item, 1]
            return (real * cosine - imag * sine, real * sine + imag * cosine)

        def store(item, value):
            real, imag = value
            if sign < 0:
                cosine, sine = twist_ref[item, 0], twist_ref[item, 1]
                real, imag = real * cosine + imag * sine, imag * cosine - real * sine
            plane_ref[item, 0, rows, :] = real
            plane_ref[item, 1, rows, :] = imag

        slab_points(load, store, middle_ref, sign)
        return carry

    lax.fori_loop(0, HALF // 8, functools.partial(slabs_over, sign=-1), 0)

    def filtered(item, carry):
        data_high, data_low = split(jnp.concatenate([plane_ref[item, 0], plane_ref[item, 1]], axis=1))
        spectrum = three_dot(data_high, data_low, tick_high_ref[...], tick_low_ref[...])
        real, imag = spectrum[:, :PART], spectrum[:, PART:]
        filter_real, filter_imag = filter_ref[item, :, :PART], filter_ref[item, :, PART:]
        mixed = jnp.concatenate(
            [real * filter_real - imag * filter_imag, real * filter_imag + imag * filter_real], axis=1
        )
        mixed_high, mixed_low = split(mixed)
        result = three_dot(mixed_high, mixed_low, untick_high_ref[...], untick_low_ref[...])
        plane_ref[item, 0] = result[:, :PART]
        plane_ref[item, 1] = result[:, PART:]
        return carry

    lax.fori_loop(0, SLABS, filtered, 0)
    lax.fori_loop(0, HALF // 8, functools.partial(slabs_over, sign=1), 0)
    for pair in range(SLABS // 2):
        both = jnp.concatenate(
            [plane_ref[2 * pair + slab].reshape(2 * HALF, PART) for slab in range(2)], axis=1
        )
        data_high, data_low = split(both)
        result = three_dot(back_high_ref[...], back_low_ref[...], data_high, data_low)
        for slab in range(2):
            at = (2 * pair + slab) * SLAB
            out_ref[:, at : at + SLAB] = result[:, slab * PART : slab * PART + SLAB]


def tail(early, own, got, take, good, commons, member, high, low, filters):
    back_high, back_low = two_halves(wire_tables()[1])
    tick, untick, twist = tick_tables()
    tables = (twist, *two_halves(tick), *two_halves(untick), back_high, back_low)
    operands = (early, *own, *got, take, good, commons, member, high, low, filters, *tables)
    return pl.pallas_call(
        tail_kernel,
        in_specs=whole(len(operands)),
        out_specs=whole(1)[0],
        out_shape=jax.ShapeDtypeStruct((WIRES, TICKS), jnp.float32),
        scratch_shapes=[
            pltpu.VMEM((SLABS // 2, WIRES, HALF), jnp.float32),
            pltpu.VMEM((SLABS, 2, HALF, PART), jnp.float32),
            pltpu.VMEM((commons.shape[1], HALF), jnp.float32),
            pltpu.VMEM((WIRES, HALF), jnp.float32),
            pltpu.VMEM((WIRES, HALF), jnp.float32),
            pltpu.VMEM((SLABS, 2, 8, PART), jnp.float32),
        ],
        compiler_params=roomy(60),
        name="deconvolve",
    )(*operands)


def make_filter(wire_kernel, time_kernel):
    forward, _ = wire_tables()
    wire_resp = jnp.dot(forward.astype(np.float32), wire_kernel, precision=highest).reshape(2, 1, HALF, 1)
    first = np.arange(SLABS)
    angle = 2.0 * np.pi * (np.outer(first, first) % SLABS) / SLABS
    slabs = time_kernel.reshape(SLABS, SLAB)
    real = jnp.dot(np.cos(angle).astype(np.float32), slabs, precision=highest)
    imag = jnp.dot(-np.sin(angle).astype(np.float32), slabs, precision=highest)
    twist = 2.0 * np.pi * np.outer(first, np.arange(SLAB)) / TICKS
    cosine, sine = np.cos(twist).astype(np.float32), np.sin(twist).astype(np.float32)
    real, imag = real * cosine + imag * sine, imag * cosine - real * sine
    inner = np.arange(SLAB)
    angle = 2.0 * np.pi * (np.outer(inner, inner) % SLAB) / SLAB
    cosine, sine = np.cos(angle).astype(np.float32), np.sin(angle).astype(np.float32)
    both = jnp.dot(
        jnp.concatenate([real, imag], axis=1),
        np.block([[cosine, -sine], [sine, cosine]]).astype(np.float32),
        precision=highest,
    )
    time_resp = jnp.pad(both.reshape(SLABS, 2, SLAB), ((0, 0), (0, 0), (0, PART - SLAB)))
    time_real, time_imag = time_resp[:, 0][:, None, :], time_resp[:, 1][:, None, :]
    real = wire_resp[0] * time_real - wire_resp[1] * time_imag
    imag = wire_resp[0] * time_imag + wire_resp[1] * time_real
    denominator = real * real + imag * imag + regular_term
    return jnp.concatenate([real / denominator, -imag / denominator], axis=2)


def picked_tables(wires):
    wire_high, wire_low = two_halves(wire_tables()[0])
    picked = (jnp.arange(WIRES, dtype=jnp.int32)[:, None] == wires[None, :]).astype(jnp.bfloat16)
    return dot(jnp.asarray(wire_high), picked).astype(jnp.bfloat16), dot(jnp.asarray(wire_low), picked).astype(
        jnp.bfloat16
    )


def shards(raw, bad, group_id, chan_plane, chan_wire, plane_offset, wire_kernel, time_kernel):
    chan_count = raw.shape[0]
    group_count = chan_count // GROUP
    apa_index = lax.axis_index("apa")
    tick_index = lax.axis_index("tick")
    parity = apa_index % 2
    swap = [(i, i ^ 1) for i in range(lax.axis_size("apa"))]
    raw_turned = raw.T
    early_got = lax.ppermute(raw_turned[:EARLY], "apa", swap)
    local_group = group_id - apa_index * group_count
    good_mask = 1.0 - bad.astype(jnp.float32)
    pair_base = (apa_index // 2 * 2 * SLABS).astype(jnp.int32)
    place, cross_count = rank_rows(chan_plane, pair_base, (1 - parity).astype(jnp.int32))
    place_got = lax.ppermute(place, "apa", swap)
    rows = pack_rows(place, raw_turned)
    late0, late1 = lay_late(rows, 0), lay_late(rows, 1)
    common = sum_groups(raw_turned, local_group, good_mask)
    common_got = lax.ppermute(common, "apa", swap)
    first = jnp.where(parity == 0, common, common_got)
    second = jnp.where(parity == 0, common_got, common)
    commons = lax.all_gather(jnp.concatenate([first, second], axis=0), "tick")
    blank = jnp.zeros_like(bad)
    facts = jnp.stack([chan_wire >> 5, chan_wire & 31, local_group, bad, chan_plane - pair_base, blank, blank, blank])
    facts = pick_facts(place - tick_index * WIRES, facts.astype(jnp.float32)).astype(jnp.int32)
    row_offset = jnp.take(plane_offset, facts[4] + pair_base)
    row_wire = (facts[0] * 32 + facts[1] + row_offset) % WIRES
    facts = jnp.stack([row_wire, facts[2] + parity * group_count, facts[3]])
    take = jnp.asarray(row_order()) < cross_count
    facts = jnp.where(take[None, :], lax.ppermute(facts, "apa", swap), facts)
    row_take = take.astype(jnp.float32)[:, None]
    row_good = 1.0 - facts[2].astype(jnp.float32)[:, None]
    member = (facts[1][:, None] == jnp.arange(2 * group_count, dtype=jnp.int32)[None, :]).astype(jnp.bfloat16)
    high, low = picked_tables(facts[0])
    filters = make_filter(wire_kernel, time_kernel)

    def over_ticks(value):
        return lax.all_to_all(value, "tick", split_axis=0, concat_axis=0, tiled=True)

    own0 = over_ticks(late0)
    late1, early_got = lax.optimization_barrier((late1, early_got))
    own1 = over_ticks(late1)
    got0 = lax.ppermute(own0[:, : SENT[0]], "apa", swap)
    early = merge_rows(place_got, early_got, rows, row_take)
    early, got0 = lax.optimization_barrier((early, got0))
    early = over_ticks(early)
    got1 = lax.ppermute(own1[:, : SENT[1]], "apa", swap)
    return tail(early, (own0, own1), (got0, got1), row_take, row_good, commons, member, high, low, filters)[None]


def solution(mesh):
    placed = (P("apa", "tick"), P("apa"), P("apa"), P("apa"), P("apa"), P(), P(), P())
    return jax.shard_map(
        shards,
        mesh=mesh,
        in_specs=placed,
        out_specs=P(("apa", "tick"), None, None),
        check_vma=False,
    )
```

time: 370 us -> 262 us (0.71)
  waiting for transfers between devices: 129 us -> 22.9 us
  blocking collectives: 37.9 us -> 0 us
  Pallas kernels: 117 us -> 143 us
  starting transfers between devices: 14.8 us -> 31.8 us
  local copies, waits for them, and re-layouts: 42.2 us -> 34.4 us
    ppermute x4 -> x6, waiting for transfers between devices: 88.5 us -> 22.1 us  [the longest x1 19.5 us: shards(): got1 = lax.ppermute(own1[:, :SENT[1]], 'apa', swap)]
    all_to_all x1 -> x0, blocking collectives: 37.9 us -> none  [shards(): rows = lax.all_to_all(rows, 'tick', split_axis=0, concat_axis=0, tiled=True)]
    all_gather x1, waiting for transfers between devices: 27.5 us -> 0.01 us  [shards(): commons = lax.all_gather(jnp.concatenate([first, second], axis=0), 'tick')]
    pallas_call x9 -> x7, Pallas kernels: 114 us -> 140 us  [the longest x1 76.1 us: tail(): pl.pallas_call(tail_kernel, in_specs=whole(len(operands)), out_specs=whol...]
    all_to_all x2 -> x3, starting transfers between devices: 10.8 us -> 26.1 us  [over_ticks(): lax.all_to_all(value, 'tick', split_axis=0, concat_axis=0, tiled=True)]
    gather x5 -> x1, local copies, waits for them, and re-layouts: 15.9 us -> 3.35 us  [shards(): row_offset = jnp.take(plane_offset, facts[4] + pair_base)]
    all_to_all x2 -> x3, waiting for transfers between devices: 12.9 us -> 0.82 us  [over_ticks(): lax.all_to_all(value, 'tick', split_axis=0, concat_axis=0, tiled=True)]
    unnamed x62 -> x45, local copies, waits for them, and re-layouts: 20.3 us -> 15.5 us
  transfers between devices with their start and end apart: 7 -> 10, of which waited for: 4 -> 3; matrix products, arithmetic and copies ran while one was open for 10% -> 14% of each run, Pallas kernels for 9% -> 25%
where the time goes in v3:
time: 262 us; the launch traced here: 261 us
  Pallas kernels  143 us (55%)
  local copies, waits for them, and re-layouts  34.4 us (13%)
  starting transfers between devices  31.8 us (12%)
  waiting for transfers between devices  22.9 us (9%)
  between operations  13.8 us (5%)
  other arithmetic  9.9 us (4%)
  matrix products  5.97 us (2%)
    pallas_call x1, Pallas kernels, tail(): pl.pallas_call(tail_kernel, in_specs=whole(len(operands)), out_specs=whol...  76.1 us
    all_to_all x3, starting transfers between devices, over_ticks(): lax.all_to_all(value, 'tick', split_axis=0, concat_axis=0, tiled=True)  26.1 us
    pallas_call x1, Pallas kernels, merge_rows(): pl.pallas_call(merge_kernel, in_specs=[pl.BlockSpec(memory_space=pltpu.SM...  23.3 us
    ppermute x1, waiting for transfers between devices, shards(): got1 = lax.ppermute(own1[:, :SENT[1]], 'apa', swap)  19.5 us
    unnamed x45, local copies, waits for them, and re-layouts  15.5 us
    pallas_call x1, Pallas kernels, pack_rows(): pl.pallas_call(pack_kernel, in_specs=[pl.BlockSpec(memory_space=pltpu.SME...  13.9 us
    pallas_call x1, Pallas kernels, pick_facts(): pl.pallas_call(facts_kernel, in_specs=whole(2), out_specs=whole(1)[0], ou...  11.1 us
    pallas_call x2, Pallas kernels, lay_late(): pl.pallas_call(functools.partial(late_kernel, which), in_specs=whole(1),...  8.89 us
  transfers between devices with their start and end apart: 10, of which 3 were waited for; matrix products, arithmetic and copies ran while one was open for 14% of the time, Pallas kernels for 25%

profile of v3, /device:TPU:1, one launch (start us, length us, event | category | flops | bytes accessed | tf_op | source)
XLA Modules:
  0.0 261.4 jit_solution(5447893474152859412)
XLA Ops:
  6.5 0.8 copy-done.8
  7.4 2.1 rank_rows.1
  9.5 2.1 collective-permute-start
  11.6 0.8 convert_subtract_fusion
  12.5 0.8 broadcast_subtract_fusion.1
  13.3 2.8 %copy-done.5 = f32[15360,100]{0,1:T(8,128)S(1)} copy-done((f32[15360,100]{0,1:T(8,128)S(1)}, f32[15360,100]{0,1:T(8,128)}, u32[]{:S(2)}) %copy-start.5) | copy-done | bytes 6144024
  16.1 7.1 %sum_groups.1 = f32[120,100]{1,0:T(8,128)S(1)} custom-call(f32[100,15360]{1,0:T(8,128)S(1)} %bitcast.43, s32[1,15360]{1,0:T(1,128)S(1)} %bitcast.46, f32[1,15360]{1,0:T(1,128)S(1)} %bitcast.51), custom_call_target="tpu_custom_call" | custom-call | tf_op jit(solution)/shard_map/sum_groups/pallas_call | solution.py:251
  23.2 0.1 collective-permute-start.5
  23.3 1.6 slice.68
  24.9 1.4 collective-permute-start.1
  26.4 13.9 %pack_rows.1.rows_ref.own_ref = f32[15360,128]{1,0:T(8,128)S(1)} custom-call(s32[15360]{0:T(1024)S(1)} %bitcast.49, f32[100,15360]{1,0:T(8,128)S(1)} %bitcast.45), custom_call_target="tpu_custom_call" | custom-call | tf_op jit(solution)/shard_map/pack_rows/pallas_call | solution.py:171
  40.3 4.4 %lay_late.3 = f32[32,120,128]{2,1,0:T(8,128)} custom-call(f32[15360,128]{1,0:T(8,128)S(1)} %pack_rows.1.rows_ref.own_ref), custom_call_target="tpu_custom_call" | custom-call | tf_op jit(solution)/shard_map/lay_late/pallas_call | solution.py:194
  44.7 3.1 %copy-done.2 = f32[15360,128]{1,0:T(8,128)} copy-done((f32[15360,128]{1,0:T(8,128)}, f32[15360,128]{1,0:T(8,128)S(1)}, u32[]{:S(2)}) %copy-start.2) | copy-done | bytes 7864344
  47.8 9.7 %all-to-all-start = ((f32[32,120,128]{2,1,0:T(8,128)}), f32[32,120,128]{2,1,0:T(8,128)}, u32[]{:S(2)}, u32[]{:S(2)}) async-start(f32[32,120,128]{2,1,0:T(8,128)} %lay_late.3), calls=%async_computation | async-start | bytes 3932160 | tf_op jit(solution)/shard_map/all_to_all | solution.py:565
  57.4 0.0 all-gather.4.cloned.1.call-start
  57.6 3.2 %copy-done.3 = f32[15360,128]{1,0:T(8,128)S(1)} copy-done((f32[15360,128]{1,0:T(8,128)S(1)}, f32[15360,128]{1,0:T(8,128)}, u32[]{:S(2)}) %copy-start.3) | copy-done | bytes 7864344
  60.8 4.5 %lay_late.2 = f32[32,120,128]{2,1,0:T(8,128)} custom-call(f32[15360,128]{1,0:T(8,128)S(1)} %copy-done.3), custom_call_target="tpu_custom_call" | custom-call | tf_op jit(solution)/shard_map/lay_late/pallas_call | solution.py:194
  65.3 0.7 copy.43
  66.0 0.0 all-gather.4.cloned.1.call-update
  66.1 0.6 broadcast_and_fusion
  66.7 0.7 stack_broadcast_in_dim.3
  67.4 0.0 copy-start.15
  67.4 0.0 copy-start.16
  67.5 1.4 stack.32
  68.9 0.0 copy-start.19
  68.9 0.0 copy-start.18
  68.9 0.0 copy-start.13
  68.9 0.0 copy-start.14
  69.0 11.1 %pick_facts.1 = f32[8,480]{1,0:T(8,128)S(1)} custom-call(s32[1,15360]{1,0:T(1,128)S(1)} %broadcast_subtract_fusion.2.place_ref, f32[8,15360]{1,0:T(8,128)S(1)} %convert_element_type.37.facts_ref), custom_call_target="tpu_custom_call" | custom-call | tf_op jit(solution)/shard_map/pick_facts/pallas_call | solution.py:273
  80.2 3.3 %gather_fusion = s32[480]{0:T(512)S(1)} fusion(s32[128]{0:T(128)S(1)} %copy-done.10, s32[1024]{0:T(1024)S(1)} %pad_clamp_fusion), kind=kCustom, calls=%fused_computation | custom fusion | bytes 5760 | tf_op jit(solution)/shard_map/jit(_take)/gather | solution.py:553
  83.6 0.8 all-to-all-done.own0
  84.4 0.5 collective-permute-start.2
  84.9 6.7 %all-to-all-start.2 = ((f32[32,120,128]{2,1,0:T(8,128)}), f32[32,120,128]{2,1,0:T(8,128)}, u32[]{:S(2)}, u32[]{:S(2)}) async-start(f32[32,120,128]{2,1,0:T(8,128)} %lay_late.2), calls=%async_computation.2 | async-start | bytes 3932160 | tf_op jit(solution)/shard_map/all_to_all | solution.py:565
  91.7 1.3 collective-permute-start.4
  93.0 0.1 reshape.60
  93.1 0.1 fusion.24
  93.2 0.0 copy-done.18
  93.3 0.1 fusion.23
  93.4 0.0 copy-done.15
  93.4 0.2 fusion.12
  93.6 0.2 convolution_add_fusion
  93.8 0.1 reshape.61
  93.9 0.5 slice.50
  94.4 0.6 broadcast_compare_fusion
  95.1 0.1 copy.42.take_ref
  95.2 2.3 fusion.22
  97.6 3.2 %copy-done.4 = f32[15360,128]{1,0:T(8,128)S(1)} copy-done((f32[15360,128]{1,0:T(8,128)S(1)}, f32[15360,128]{1,0:T(8,128)}, u32[]{:S(2)}) %copy-start.4) | copy-done | bytes 7864344
  100.8 23.3 %merge_rows.1 = f32[32,160,128]{2,1,0:T(8,128)} custom-call(s32[15360]{0:T(1024)S(1)} %collective-permute-done.place_ref, f32[40,15360]{1,0:T(8,128)S(1)} %collective-permute-done.1.raw_ref, f32[15360,128]{1,0:T(8,128)S(1)} %copy-done.4, f32[480,1]{1,0:T(8,128)S(1)} %copy.42.take_ref), custom_call_target="tpu_custom_call" | custom-call | tf_op jit(solution)/shard_map/merge_rows/pallas_call | solution.py:221
  124.1 2.5 collective-permute-done.2.got0
  126.7 9.6 %all-to-all-start.1 = ((f32[32,160,128]{2,1,0:T(8,128)}), f32[32,160,128]{2,1,0:T(8,128)S(1)}, u32[]{:S(2)}, u32[]{:S(2)}) async-start(f32[32,160,128]{2,1,0:T(8,128)} %merge_rows.1), calls=%async_computation.1 | async-start | bytes 5242880 | tf_op jit(solution)/shard_map/all_to_all | solution.py:565
  136.3 2.0 fusion
  138.3 2.7 %slice.69 = f32[32,96,128]{2,1,0:T(8,128)} slice(f32[32,120,128]{2,1,0:T(8,128)} %all-to-all-done.2.own1), slice={[0:32], [0:96], [0:128]} | slice | bytes 3145728 | tf_op jit(solution)/shard_map/slice | solution.py:574
  141.0 0.3 collective-permute-start.3
  141.3 4.0 %pad_maximum_fusion.filter_ref = f32[32,256,256]{2,1,0:T(8,128)} fusion(f32[32,256,128]{2,1,0:T(8,128)S(1)} %get-tuple-element.22, f32[32,256,128]{2,1,0:T(8,128)S(1)} %get-tuple-element.21), kind=kLoop, calls=%fused_computation.1 | loop fusion | flops 2097152 | bytes 16777216 | tf_op jit(solution)/shard_map/concatenate | solution.py:518
  145.3 0.9 copy.48.good_ref
  146.2 1.5 convolution_convert_fusion
  147.7 1.0 copy.45
  148.7 1.5 convolution_convert_fusion.1
  150.3 1.1 copy.44
  151.3 0.8 fusion.6.member_ref
  152.1 5.3 %copy.49.common_ref = f32[32,240,100]{2,1,0:T(8,128)} copy(f32[32,240,100]{1,2,0:T(8,128)} %all-gather.4.cloned.1.call-done) | data formatting | bytes 6144000 | tf_op jit(solution)/shard_map/all_gather | solution.py:549
  157.4 19.5 %collective-permute-done.3.got1 = f32[32,96,128]{2,1,0:T(8,128)} collective-permute-done((f32[32,96,128]{2,1,0:T(8,128)}, f32[32,96,128]{2,1,0:T(8,128)}, u32[]{:S(2)}, u32[]{:S(2)}) %collective-permute-start.3) | collective-permute-done | bytes 1572896 | tf_op jit(solution)/shard_map/ppermute | solution.py:574
  176.9 1.5 copy-done.11
  178.4 76.1 %deconvolve.1 = f32[480,3200]{1,0:T(8,128)} custom-call(f32[32,160,128]{2,1,0:T(8,128)} %copy-done.11, f32[32,120,128]{2,1,0:T(8,128)} %all-to-all-done.own0, f32[32,120,128]{2,1,0:T(8,128)} %all-to-all-done.2.own1, f32[32,120,128]{2,1,0:T(8,128)} %collective-permute-done.2.got0, f32[32,96,128]{2,1,0:T(8,128)} %collective-permute-done.3.got1, ...), custom_call_target="tpu_custom_call" | custom-call | tf_op jit(solution)/shard_map/deconvolve/pallas_call | solution.py:476
  (54 shorter events, 0.3 us)
Async XLA Ops:
  6.5 88.7 %copy-start = (f32[480]{0:T(512)S(1)}, f32[480]{0:T(512)}, u32[]{:S(2)}) copy-start(f32[480]{0:T(512)} %param.30) | copy-start | bytes 5764
  6.5 0.8 copy-start.8
  9.5 88.0 %collective-permute-start = (s32[15360]{0:T(1024)S(1)}, s32[15360]{0:T(1024)S(1)}, u32[]{:S(2)}, u32[]{:S(2)}) collective-permute-start(s32[15360]{0:T(1024)S(1)} %bitcast.48), channel_id=1, source_target_pairs={{0,32},{32,0},{64,96},{96,64},{1,33},{33,1},{65,97},{97,65},{2,34}... | collective-permute-start | bytes 184328 | tf_op jit(solution)/shard_map/ppermute | solution.py:542
  13.3 2.8 %copy-start.5 = (f32[15360,100]{0,1:T(8,128)S(1)}, f32[15360,100]{0,1:T(8,128)}, u32[]{:S(2)}) copy-start(f32[15360,100]{0,1:T(8,128)} %param.24) | copy-start | bytes 18432004
  16.1 10.2 %copy-start.6 = (f32[15360,100]{0,1:T(8,128)S(1)}, f32[15360,100]{0,1:T(8,128)}, u32[]{:S(2)}) copy-start(f32[15360,100]{0,1:T(8,128)} %param.24) | copy-start | bytes 18432004
  23.2 42.1 %collective-permute-start.5 = (f32[120,100]{1,0:T(8,128)S(1)}, f32[120,100]{1,0:T(8,128)S(1)}, u32[]{:S(2)}, u32[]{:S(2)}) collective-permute-start(f32[120,100]{1,0:T(8,128)S(1)} %sum_groups.1), channel_id=1, source_target_pairs={{0,32},{32,0},{64,96},{96,64},{1,33},{33,1},{65,97},{97,65},{2,34}... | collective-permute-start | bytes 144008 | tf_op jit(solution)/shard_map/ppermute | solution.py:546
  24.9 60.0 %collective-permute-start.1 = (f32[40,15360]{1,0:T(8,128)}, f32[40,15360]{1,0:T(8,128)S(1)}, u32[]{:S(2)}, u32[]{:S(2)}) collective-permute-start(f32[40,15360]{1,0:T(8,128)} %slice.68), channel_id=1, source_target_pairs={{0,32},{32,0},{64,96},{96,64},{1,33},{33,1},{65,97},{97,65},{2,34}... | collective-permute-start | bytes 7372808 | tf_op jit(solution)/shard_map/ppermute | solution.py:537
  44.7 3.1 %copy-start.2 = (f32[15360,128]{1,0:T(8,128)}, f32[15360,128]{1,0:T(8,128)S(1)}, u32[]{:S(2)}) copy-start(f32[15360,128]{1,0:T(8,128)S(1)} %pack_rows.1.rows_ref.own_ref) | copy-start | bytes 23592964
  47.8 36.6 %all-to-all-start = ((f32[32,120,128]{2,1,0:T(8,128)}), f32[32,120,128]{2,1,0:T(8,128)}, u32[]{:S(2)}, u32[]{:S(2)}) async-start(f32[32,120,128]{2,1,0:T(8,128)} %lay_late.3), calls=%async_computation | async-start | bytes 3932160 | tf_op jit(solution)/shard_map/all_to_all | solution.py:565
  57.4 94.7 %all-gather.4.cloned.1.call-start = ((), (), s32[]{:S(2)}) async-start(), calls=%async_computation.3 | async-start | bytes 3514368 | tf_op jit(solution)/shard_map/all_gather | solution.py:549
  57.5 3.2 %copy-start.3 = (f32[15360,128]{1,0:T(8,128)S(1)}, f32[15360,128]{1,0:T(8,128)}, u32[]{:S(2)}) copy-start(f32[15360,128]{1,0:T(8,128)} %copy-done.2) | copy-start | bytes 23592964
  60.8 5.3 %copy-start.9 = (s32[15360]{0:T(1024)S(1)}, s32[15360]{0:T(1024)}, u32[]{:S(2)}) copy-start(s32[15360]{0:T(1024)} %param.27) | copy-start | bytes 184324
  60.8 5.3 %copy-start.17 = (s32[15360]{0:T(1024)S(1)}, s32[15360]{0:T(1024)}, u32[]{:S(2)}) copy-start(s32[15360]{0:T(1024)} %param.28) | copy-start | bytes 184324
  60.8 6.6 %copy-start.12 = (s32[15360]{0:T(1024)S(1)}, s32[15360]{0:T(1024)}, u32[]{:S(2)}) copy-start(s32[15360]{0:T(1024)} %param.25) | copy-start | bytes 184324
  65.3 15.0 %copy-start.10 = (s32[128]{0:T(128)S(1)}, s32[128]{0:T(128)}, u32[]{:S(2)}) copy-start(s32[128]{0:T(128)} %param.29) | copy-start | bytes 1540
  67.4 26.0 %copy-start.15 = (f32[32,100]{1,0:T(8,128)S(1)}, f32[32,100]{1,0:T(8,128)}, u32[]{:S(2)}) copy-start(f32[32,100]{1,0:T(8,128)} %constant.120.clone) | copy-start | bytes 38404
  67.4 26.0 %copy-start.16 = (f32[32,100]{1,0:T(8,128)S(1)}, f32[32,100]{1,0:T(8,128)}, u32[]{:S(2)}) copy-start(f32[32,100]{1,0:T(8,128)} %constant.119.clone) | copy-start | bytes 38404
  68.9 24.1 %copy-start.20 = (f32[3200]{0:T(1024)S(1)}, f32[3200]{0:T(1024)}, u32[]{:S(2)}) copy-start(f32[3200]{0:T(1024)} %param.31) | copy-start | bytes 38404
  68.9 24.2 %copy-start.19 = (f32[32,32]{1,0:T(8,128)S(1)}, f32[32,32]{1,0:T(8,128)}, u32[]{:S(2)}) copy-start(f32[32,32]{1,0:T(8,128)} %constant.118.clone) | copy-start | bytes 12292
  68.9 24.3 %copy-start.18 = (f32[32,32]{1,0:T(8,128)S(1)}, f32[32,32]{1,0:T(8,128)}, u32[]{:S(2)}) copy-start(f32[32,32]{1,0:T(8,128)} %constant.117.clone) | copy-start | bytes 12292
  68.9 24.5 %copy-start.13 = (f32[100,200]{1,0:T(8,128)S(1)}, f32[100,200]{1,0:T(8,128)}, u32[]{:S(2)}) copy-start(f32[100,200]{1,0:T(8,128)} %constant.132) | copy-start | bytes 240004
  68.9 24.7 %copy-start.14 = (f32[100,200]{1,0:T(8,128)S(1)}, f32[100,200]{1,0:T(8,128)}, u32[]{:S(2)}) copy-start(f32[100,200]{1,0:T(8,128)} %constant.133) | copy-start | bytes 240004
  69.0 25.5 %copy-start.21 = (s32[480]{0:T(512)S(1)}, s32[480]{0:T(512)}, u32[]{:S(2)}) copy-start(s32[480]{0:T(512)} %constant.113.clone) | copy-start | bytes 5764
  84.4 42.3 %collective-permute-start.2 = (f32[32,120,128]{2,1,0:T(8,128)}, f32[32,120,128]{2,1,0:T(8,128)}, u32[]{:S(2)}, u32[]{:S(2)}) collective-permute-start(f32[32,120,128]{2,1,0:T(8,128)} %all-to-all-done.own0), channel_id=1, source_target_pairs={{0,32},{32,0},{64,96},{96,64},{1,33},{33,1},{65,97},{97,65},{2,34}... | collective-permute-start | bytes 5898248 | tf_op jit(solution)/shard_map/ppermute | solution.py:570
  84.9 41.8 %all-to-all-start.2 = ((f32[32,120,128]{2,1,0:T(8,128)}), f32[32,120,128]{2,1,0:T(8,128)}, u32[]{:S(2)}, u32[]{:S(2)}) async-start(f32[32,120,128]{2,1,0:T(8,128)} %lay_late.2), calls=%async_computation.2 | async-start | bytes 3932160 | tf_op jit(solution)/shard_map/all_to_all | solution.py:565
  91.7 53.6 %collective-permute-start.4 = (s32[3,480]{1,0:T(4,128)S(1)}, s32[3,480]{1,0:T(4,128)S(1)}, u32[]{:S(2)}, u32[]{:S(2)}) collective-permute-start(s32[3,480]{1,0:T(4,128)S(1)} %pad_add_fusion), channel_id=1, source_target_pairs={{0,32},{32,0},{64,96},{96,64},{1,33},{33,1},{65,97},{97,65},{2,34}... | collective-permute-start | bytes 17288 | tf_op jit(solution)/shard_map/ppermute | solution.py:557
  95.2 28.9 %copy-start.7 = (f32[480,1]{1,0:T(8,128)}, f32[480,1]{1,0:T(8,128)S(1)}, u32[]{:S(2)}) copy-start(f32[480,1]{1,0:T(8,128)S(1)} %copy.42.take_ref) | copy-start | bytes 5764
  97.6 3.3 %copy-start.4 = (f32[15360,128]{1,0:T(8,128)S(1)}, f32[15360,128]{1,0:T(8,128)}, u32[]{:S(2)}) copy-start(f32[15360,128]{1,0:T(8,128)} %copy-done.2) | copy-start | bytes 23592964
  126.7 50.2 %all-to-all-start.1 = ((f32[32,160,128]{2,1,0:T(8,128)}), f32[32,160,128]{2,1,0:T(8,128)S(1)}, u32[]{:S(2)}, u32[]{:S(2)}) async-start(f32[32,160,128]{2,1,0:T(8,128)} %merge_rows.1), calls=%async_computation.1 | async-start | bytes 5242880 | tf_op jit(solution)/shard_map/all_to_all | solution.py:565
  141.0 35.9 %collective-permute-start.3 = (f32[32,96,128]{2,1,0:T(8,128)}, f32[32,96,128]{2,1,0:T(8,128)}, u32[]{:S(2)}, u32[]{:S(2)}) collective-permute-start(f32[32,96,128]{2,1,0:T(8,128)} %slice.69), channel_id=1, source_target_pairs={{0,32},{32,0},{64,96},{96,64},{1,33},{33,1},{65,97},{97,65},{2,34}... | collective-permute-start | bytes 4718600 | tf_op jit(solution)/shard_map/ppermute | solution.py:574
  176.9 1.5 copy-start.11
  178.4 76.1 %copy-start.1 = (f32[480]{0:T(512)S(1)}, f32[480]{0:T(512)}, u32[]{:S(2)}) copy-start(f32[480]{0:T(512)} %param.30) | copy-start | bytes 5764
Sparse Core Ops, SparseCore 0:
  66.2 60.3 all-gather.3

commit v4 on v3

--- a/solution.py
+++ b/solution.py
@@ -20,15 +20,19 @@
 EARLY = 40
 LATE = 60
 EARLY_ROWS = 160
-LATE_ROWS = 120
+LATE_ROWS = (96, 144)
+LATE_BASE = (0, 192)
 BLOCK = 256
 WIDE = 512
-SENT = (120, 96)
+SENT = (96, 120)
 
 highest = lax.Precision.HIGHEST
 epsilon_power = 1e-06
 regular_term = 0.25
 mega = 1024 * 1024
+
+
+light = pl.CostEstimate(flops=1, bytes_accessed=1, transcendentals=0)
 
 
 def roomy(size):
@@ -83,10 +87,10 @@
 
 def row_order():
     row = np.arange(WIRES)
-    piece = (row >= 360).astype(np.int32)
-    place = row - 240 - 120 * piece
-    late = np.where(place < 90, 240 + 90 * piece + place, 420 + 30 * piece + place - 90)
-    return np.where(row < 240, row, late).astype(np.int32)
+    piece = (row >= 336).astype(np.int32)
+    place = row - 192 - 144 * piece
+    late = np.where(place < 114, 192 + 114 * piece + place, 420 + 30 * piece + place - 114)
+    return np.where(row < 192, row, late).astype(np.int32)
 
 
 def rank_kernel(plane_ref, base_ref, cross_ref, place_ref, count_ref):
@@ -108,9 +112,9 @@
         rank = jnp.sum(member * prefix, axis=0, keepdims=True)
         before = before + jnp.sum(member, axis=1, keepdims=True)
         order = (rank + (1.0 - is_cross[:, part]) * cross_count).astype(jnp.int32)
-        near_row = order + jnp.where(order >= 330, 30, 0)
-        far_row = order - 90 + jnp.where(order >= 450, 90, 0)
-        row = jnp.where(order < 240, order, jnp.where(order < 420, near_row, far_row))
+        near_row = order + jnp.where(order >= 306, 30, 0)
+        far_row = order - 114 + jnp.where(order >= 450, 114, 0)
+        row = jnp.where(order < 192, order, jnp.where(order < 420, near_row, far_row))
         place_ref[:, part] = (local[:, part] % SLABS) * WIRES + row
     count_ref[...] = jnp.broadcast_to(cross_count.astype(jnp.int32), count_ref.shape)
 
@@ -162,8 +166,29 @@
     lax.fori_loop(0, steps // 2, both, 0)
 
 
-def pack_kernel(place_ref, raw_ref, rows_ref, even_ref, odd_ref):
+def late_kernel(which, rows_ref, out_ref):
+    size = LATE_ROWS[which]
+
+    def one_slot(slot, carry):
+        start = pl.multiple_of(slot * WIRES, 8)
+        for piece in range(2):
+            at = start + LATE_BASE[which] + piece * size
+            out_ref[slot, :, piece * LATE : (piece + 1) * LATE] = rows_ref[pl.ds(at, size), EARLY:SLAB]
+        return carry
+
+    lax.fori_loop(0, SLABS, one_slot, 0)
+
+
+def late_shape(which):
+    return jax.ShapeDtypeStruct((SLABS, LATE_ROWS[which], PART), jnp.float32)
+
+
+def pack_kernel(place_ref, raw_ref, late_ref, rows_out, rows_ref, even_ref, odd_ref, rows_done):
     turned_scatter(place_ref, raw_ref, rows_ref, even_ref, odd_ref)
+    keep = pltpu.make_async_copy(rows_ref, rows_out, rows_done)
+    keep.start()
+    late_kernel(0, rows_ref, late_ref)
+    keep.wait()
 
 
 def pack_rows(place, raw_turned):
@@ -171,23 +196,14 @@
     return pl.pallas_call(
         pack_kernel,
         in_specs=[pl.BlockSpec(memory_space=pltpu.SMEM)] + whole(1),
-        out_specs=whole(1)[0],
-        out_shape=jax.ShapeDtypeStruct((chan_count, PART), jnp.float32),
-        scratch_shapes=[pltpu.VMEM((WIDE, PART), jnp.float32)] * 2,
+        out_specs=whole(1) + [pl.BlockSpec(memory_space=pl.ANY)],
+        out_shape=[late_shape(0), jax.ShapeDtypeStruct((chan_count, PART), jnp.float32)],
+        scratch_shapes=[pltpu.VMEM((chan_count, PART), jnp.float32)]
+        + [pltpu.VMEM((WIDE, PART), jnp.float32)] * 2
+        + [pltpu.SemaphoreType.DMA],
         compiler_params=roomy(32),
         name="pack_rows",
     )(place, raw_turned)
-
-
-def late_kernel(which, rows_ref, out_ref):
-    def one_slot(slot, carry):
-        start = pl.multiple_of(slot * WIRES, 8)
-        for piece in range(2):
-            at = start + (which * 2 + piece) * LATE_ROWS
-            out_ref[slot, :, piece * LATE : (piece + 1) * LATE] = rows_ref[pl.ds(at, LATE_ROWS), EARLY:SLAB]
-        return carry
-
-    lax.fori_loop(0, SLABS, one_slot, 0)
 
 
 def lay_late(rows, which):
@@ -195,9 +211,10 @@
         functools.partial(late_kernel, which),
         in_specs=whole(1),
         out_specs=whole(1)[0],
-        out_shape=jax.ShapeDtypeStruct((SLABS, LATE_ROWS, PART), jnp.float32),
-        compiler_params=roomy(24),
+        out_shape=late_shape(which),
+        compiler_params=roomy(20),
         name="lay_late",
+        cost_estimate=light,
     )(rows)
 
 
@@ -211,6 +228,7 @@
             take = take_ref[piece * EARLY_ROWS : (piece + 1) * EARLY_ROWS, :] > 0.5
             value = jnp.where(take, rows_ref[rows, 0:EARLY], own_ref[rows, 0:EARLY])
             out_ref[slot, :, piece * EARLY : (piece + 1) * EARLY] = value
+        out_ref[slot, :, 3 * EARLY : PART] = jnp.zeros((EARLY_ROWS, PART - 3 * EARLY), jnp.float32)
         return carry
 
     lax.fori_loop(0, SLABS, one_slot, 0)
@@ -255,29 +273,37 @@
         out_shape=jax.ShapeDtypeStruct((group_count, SLAB), jnp.float32),
         compiler_params=roomy(24),
         name="sum_groups",
+        cost_estimate=light,
     )(raw_turned, local_group[None, :], good_mask[None, :])
 
 
 def facts_kernel(place_ref, facts_ref, out_ref):
-    names = lax.broadcasted_iota(jnp.int32, (WIRES, BLOCK), 0)
+    names = lax.broadcasted_iota(jnp.int32, (32, WIDE), 0)
+    tops = lax.broadcasted_iota(jnp.int32, (16, WIDE), 0)
 
     def some(step, total):
-        part = pl.ds(pl.multiple_of(step * BLOCK, BLOCK), BLOCK)
-        member = (names == place_ref[:, part]).astype(jnp.float32).astype(jnp.bfloat16)
-        return total + across(facts_ref[:, part].astype(jnp.bfloat16), member)
-
-    out_ref[...] = lax.fori_loop(0, place_ref.shape[1] // BLOCK, some, jnp.zeros(out_ref.shape, jnp.float32))
+        part = pl.ds(pl.multiple_of(step * WIDE, WIDE), WIDE)
+        place = place_ref[:, part]
+        top = tops == place >> 5
+        picked = [jnp.where(top, facts_ref[fact : fact + 1, part], 0.0) for fact in range(facts_ref.shape[0])]
+        member = (names == place & 31).astype(jnp.float32).astype(jnp.bfloat16)
+        return total + across(jnp.concatenate(picked, axis=0).astype(jnp.bfloat16), member)
+
+    out_ref[...] = lax.fori_loop(0, place_ref.shape[1] // WIDE, some, jnp.zeros(out_ref.shape, jnp.float32))
 
 
 def pick_facts(place, facts):
-    return pl.pallas_call(
+    count = facts.shape[0]
+    picked = pl.pallas_call(
         facts_kernel,
         in_specs=whole(2),
         out_specs=whole(1)[0],
-        out_shape=jax.ShapeDtypeStruct((facts.shape[0], WIRES), jnp.float32),
+        out_shape=jax.ShapeDtypeStruct((count * 16, 32), jnp.float32),
         compiler_params=roomy(16),
         name="pick_facts",
+        cost_estimate=light,
     )(place[None, :], facts)
+    return picked.reshape(count, 16 * 32)[:, :WIRES]
 
 
 def add(first, second):
@@ -351,7 +377,7 @@
     member_ref,
     high_ref,
     low_ref,
-    filter_ref,
+    filter_hbm,
     twist_ref,
     tick_high_ref,
     tick_low_ref,
@@ -366,7 +392,11 @@
     covar_ref,
     power_ref,
     middle_ref,
+    filter_ref,
+    filter_done,
 ):
+    fetch = pltpu.make_async_copy(filter_hbm, filter_ref, filter_done)
+    fetch.start()
     both_ref[...] = jnp.zeros_like(both_ref)
     covar_ref[...] = jnp.zeros_like(covar_ref)
     power_ref[...] = jnp.zeros_like(power_ref)
@@ -377,32 +407,41 @@
         high, low = split(both_ref[...])
         return dot(member_ref[...], high) + dot(member_ref[...], low)
 
+    def spread_power(power):
+        high, rest = split(power)
+        middle = (power - high.astype(jnp.float32) - rest.astype(jnp.float32)).astype(jnp.bfloat16)
+        return dot(member_ref[...], high) + (dot(member_ref[...], rest) + dot(member_ref[...], middle))
+
     def assemble(pair, carry):
         for half in range(2):
             slab = 2 * pair + half
             base = half * PART
-            rows_ref[pair, :, base + SLAB : base + PART] = jnp.zeros((WIRES, PART - SLAB), jnp.float32)
             for piece in range(3):
                 rows = slice(piece * EARLY_ROWS, (piece + 1) * EARLY_ROWS)
-                rows_ref[pair, rows, base : base + EARLY] = early[slab, :, piece * EARLY : (piece + 1) * EARLY]
+                value = early[slab]
+                if piece:
+                    value = pltpu.roll(value, PART - piece * EARLY, 1)
+                rows_ref[pair, rows, base : base + PART] = value
             for which, (own, got) in enumerate(((own0, got0), (own1, got1))):
                 sent = SENT[which]
                 for piece in range(2):
                     part = slice(piece * LATE, (piece + 1) * LATE)
-                    at = (which * 2 + piece) * LATE_ROWS
+                    at = LATE_BASE[which] + piece * LATE_ROWS[which]
                     take = take_ref[at : at + sent, :] > 0.5
                     lanes = slice(base + EARLY, base + SLAB)
                     rows_ref[pair, at : at + sent, lanes] = jnp.where(take, got[slab, :, part], own[slab, 0:sent, part])
-                    if sent < LATE_ROWS:
-                        rows_ref[pair, at + sent : at + LATE_ROWS, lanes] = own[slab, sent:LATE_ROWS, part]
+                    if sent < LATE_ROWS[which]:
+                        rest = slice(at + sent, at + LATE_ROWS[which])
+                        rows_ref[pair, rest, lanes] = own[slab, sent : LATE_ROWS[which], part]
         spread = spread_common(pair)
         covar_ref[...] += rows_ref[pair] * spread
-        power_ref[...] += spread * spread
+        power_ref[...] += both_ref[...] * both_ref[...]
         return carry
 
     lax.fori_loop(0, SLABS // 2, assemble, 0)
     covar = jnp.sum(covar_ref[...], axis=1, keepdims=True) / TICKS
     power = jnp.sum(power_ref[...], axis=1, keepdims=True) / TICKS
+    power = spread_power(jnp.broadcast_to(power, (power.shape[0], PART)))[:, 0:1]
     weight = covar / (power + epsilon_power)
 
     def to_wires(pair, carry):
@@ -416,7 +455,8 @@
                 ]
         return carry
 
-    lax.fori_loop(0, SLABS // 2, to_wires, 0)
+    for pair in range(SLABS // 2):
+        to_wires(pair, 0)
 
     def slabs_over(index, carry, sign):
         rows = pl.ds(pl.multiple_of(index * 8, 8), 8)
@@ -455,7 +495,8 @@
         plane_ref[item, 1] = result[:, PART:]
         return carry
 
-    lax.fori_loop(0, SLABS, filtered, 0)
+    fetch.wait()
+    lax.fori_loop(0, SLABS, filtered, 0, unroll=8)
     lax.fori_loop(0, HALF // 8, functools.partial(slabs_over, sign=1), 0)
     for pair in range(SLABS // 2):
         both = jnp.concatenate(
@@ -475,7 +516,7 @@
     operands = (early, *own, *got, take, good, commons, member, high, low, filters, *tables)
     return pl.pallas_call(
         tail_kernel,
-        in_specs=whole(len(operands)),
+        in_specs=whole(11) + [pl.BlockSpec(memory_space=pl.ANY)] + whole(len(operands) - 12),
         out_specs=whole(1)[0],
         out_shape=jax.ShapeDtypeStruct((WIRES, TICKS), jnp.float32),
         scratch_shapes=[
@@ -483,8 +524,10 @@
             pltpu.VMEM((SLABS, 2, HALF, PART), jnp.float32),
             pltpu.VMEM((commons.shape[1], HALF), jnp.float32),
             pltpu.VMEM((WIRES, HALF), jnp.float32),
-            pltpu.VMEM((WIRES, HALF), jnp.float32),
+            pltpu.VMEM((commons.shape[1], HALF), jnp.float32),
             pltpu.VMEM((SLABS, 2, 8, PART), jnp.float32),
+            pltpu.VMEM((SLABS, HALF, HALF), jnp.float32),
+            pltpu.SemaphoreType.DMA,
         ],
         compiler_params=roomy(60),
         name="deconvolve",
@@ -540,16 +583,21 @@
     pair_base = (apa_index // 2 * 2 * SLABS).astype(jnp.int32)
     place, cross_count = rank_rows(chan_plane, pair_base, (1 - parity).astype(jnp.int32))
     place_got = lax.ppermute(place, "apa", swap)
-    rows = pack_rows(place, raw_turned)
-    late0, late1 = lay_late(rows, 0), lay_late(rows, 1)
-    common = sum_groups(raw_turned, local_group, good_mask)
+    late0, rows = pack_rows(place, raw_turned)
+    late0, later_place, later_raw = lax.optimization_barrier((late0, place, raw_turned))
+    common = sum_groups(later_raw, local_group, good_mask)
+    late1 = lay_late(rows, 1)
+
+    def over_ticks(value):
+        return lax.all_to_all(value, "tick", split_axis=0, concat_axis=0, tiled=True)
+
+    own0 = over_ticks(late0)
     common_got = lax.ppermute(common, "apa", swap)
     first = jnp.where(parity == 0, common, common_got)
     second = jnp.where(parity == 0, common_got, common)
     commons = lax.all_gather(jnp.concatenate([first, second], axis=0), "tick")
-    blank = jnp.zeros_like(bad)
-    facts = jnp.stack([chan_wire >> 5, chan_wire & 31, local_group, bad, chan_plane - pair_base, blank, blank, blank])
-    facts = pick_facts(place - tick_index * WIRES, facts.astype(jnp.float32)).astype(jnp.int32)
+    facts = jnp.stack([chan_wire >> 5, chan_wire & 31, local_group, bad, chan_plane - pair_base])
+    facts = pick_facts(later_place - tick_index * WIRES, facts.astype(jnp.float32)).astype(jnp.int32)
     row_offset = jnp.take(plane_offset, facts[4] + pair_base)
     row_wire = (facts[0] * 32 + facts[1] + row_offset) % WIRES
     facts = jnp.stack([row_wire, facts[2] + parity * group_count, facts[3]])
@@ -560,12 +608,7 @@
     member = (facts[1][:, None] == jnp.arange(2 * group_count, dtype=jnp.int32)[None, :]).astype(jnp.bfloat16)
     high, low = picked_tables(facts[0])
     filters = make_filter(wire_kernel, time_kernel)
-
-    def over_ticks(value):
-        return lax.all_to_all(value, "tick", split_axis=0, concat_axis=0, tiled=True)
-
-    own0 = over_ticks(late0)
-    late1, early_got = lax.optimization_barrier((late1, early_got))
+    own0, late1, early_got = lax.optimization_barrier((own0, late1, early_got))
     own1 = over_ticks(late1)
     got0 = lax.ppermute(own0[:, : SENT[0]], "apa", swap)
     early = merge_rows(place_got, early_got, rows, row_take)

time: 262 us -> 254 us (0.969)
  Pallas kernels: 143 us -> 114 us
  waiting for transfers between devices: 22.9 us -> 38.6 us
  local copies, waits for them, and re-layouts: 34.4 us -> 37.9 us
    pallas_call x1, Pallas kernels: 76.1 us -> 54.5 us  [tail(): pl.pallas_call(tail_kernel, in_specs=whole(11) + [pl.BlockSpec(memory_spa...]
    all_to_all x3, waiting for transfers between devices: 0.82 us -> 11.3 us  [over_ticks(): lax.all_to_all(value, 'tick', split_axis=0, concat_axis=0, tiled=True)]
    ppermute x1, waiting for transfers between devices: 0.01 us -> 9.96 us  [shards(): common_got = lax.ppermute(common, 'apa', swap)]
    pallas_call x1, Pallas kernels: 11.1 us -> 4.73 us  [pick_facts(): pl.pallas_call(facts_kernel, in_specs=whole(2), out_specs=whole(1)[0], ou...]
    ppermute x1, waiting for transfers between devices: 19.5 us -> 13.9 us  [shards(): got1 = lax.ppermute(own1[:, :SENT[1]], 'apa', swap)]
    pallas_call x2 -> x1, Pallas kernels: 8.89 us -> 4.82 us  [lay_late(): pl.pallas_call(functools.partial(late_kernel, which), in_specs=whole(1),...]
    pallas_call x1, Pallas kernels: 13.9 us -> 17.4 us  [pack_rows(): pl.pallas_call(pack_kernel, in_specs=[pl.BlockSpec(memory_space=pltpu.SME...]
    unnamed x45 -> x49, local copies, waits for them, and re-layouts: 15.5 us -> 18 us
  transfers between devices with their start and end apart: 10 -> 10, of which waited for: 3 -> 4; matrix products, arithmetic and copies ran while one was open for 14% -> 14% of each run, Pallas kernels for 25% -> 23%
where the time goes in v4:
time: 254 us
  Pallas kernels  114 us (45%)
  waiting for transfers between devices  38.6 us (15%)
  local copies, waits for them, and re-layouts  37.9 us (15%)
  starting transfers between devices  34.3 us (14%)
  between operations  13.9 us (5%)
  other arithmetic  8.75 us (3%)
  matrix products  6.18 us (2%)
    pallas_call x1, Pallas kernels, tail(): pl.pallas_call(tail_kernel, in_specs=whole(11) + [pl.BlockSpec(memory_spa...  54.5 us
    all_to_all x3, starting transfers between devices, over_ticks(): lax.all_to_all(value, 'tick', split_axis=0, concat_axis=0, tiled=True)  28 us
    pallas_call x1, Pallas kernels, merge_rows(): pl.pallas_call(merge_kernel, in_specs=[pl.BlockSpec(memory_space=pltpu.SM...  23.4 us
    unnamed x49, local copies, waits for them, and re-layouts  18 us
    pallas_call x1, Pallas kernels, pack_rows(): pl.pallas_call(pack_kernel, in_specs=[pl.BlockSpec(memory_space=pltpu.SME...  17.4 us
    ppermute x1, waiting for transfers between devices, shards(): got1 = lax.ppermute(own1[:, :SENT[1]], 'apa', swap)  13.9 us
    all_to_all x3, waiting for transfers between devices, over_ticks(): lax.all_to_all(value, 'tick', split_axis=0, concat_axis=0, tiled=True)  11.3 us
    ppermute x1, waiting for transfers between devices, shards(): common_got = lax.ppermute(common, 'apa', swap)  9.96 us
  transfers between devices with their start and end apart: 10, of which 4 were waited for; matrix products, arithmetic and copies ran while one was open for 14% of the time, Pallas kernels for 23%

profile of v4, /device:TPU:1, one launch (start us, length us, event | category | flops | bytes accessed | tf_op | source)
XLA Modules:
  0.0 253.6 jit_solution(1271999355038982381)
XLA Ops:
  6.5 0.8 copy-done.9
  7.4 2.1 rank_rows.1
  9.5 2.1 collective-permute-start
  11.6 3.3 %slice.72 = f32[40,15360]{1,0:T(8,128)} slice(f32[100,15360]{1,0:T(8,128)} %bitcast.44), slice={[0:40], [0:15360]} | slice | bytes 4915200 | tf_op jit(solution)/shard_map/slice | solution.py:580
  14.9 0.0 collective-permute-start.1
  15.0 2.8 %copy-done.2 = f32[15360,100]{0,1:T(8,128)S(1)} copy-done((f32[15360,100]{0,1:T(8,128)S(1)}, f32[15360,100]{0,1:T(8,128)}, u32[]{:S(2)}) %copy-start.2) | copy-done | bytes 6144024
  17.8 17.4 %pack_rows.1 = (f32[32,96,128]{2,1,0:T(8,128)S(1)}, f32[15360,128]{1,0:T(8,128)S(1)}) custom-call(s32[15360]{0:T(1024)S(1)} %bitcast.52, f32[100,15360]{1,0:T(8,128)S(1)} %bitcast.45), custom_call_target="tpu_custom_call" | custom-call | tf_op jit(solution)/shard_map/pack_rows/pallas_call | solution.py:196
  35.2 3.1 %copy-done.4 = f32[15360,128]{1,0:T(8,128)} copy-done((f32[15360,128]{1,0:T(8,128)}, f32[15360,128]{1,0:T(8,128)S(1)}, u32[]{:S(2)}) %copy-start.4) | copy-done | bytes 7864344
  38.3 1.1 copy-done.8
  39.4 9.6 %all-to-all-start = ((f32[32,96,128]{2,1,0:T(8,128)}), f32[32,96,128]{2,1,0:T(8,128)}, u32[]{:S(2)}, u32[]{:S(2)}) async-start(f32[32,96,128]{2,1,0:T(8,128)} %copy-done.8), calls=%async_computation | async-start | bytes 3145728 | tf_op jit(solution)/shard_map/all_to_all | solution.py:592
  49.1 0.0 copy-start.19
  49.1 0.0 copy-start.10
  49.1 0.0 all-gather.4.cloned.1.call-start
  49.2 0.0 copy-start.3
  49.2 2.8 %copy-done.3 = f32[15360,100]{0,1:T(8,128)S(1)} copy-done((f32[15360,100]{0,1:T(8,128)S(1)}, f32[15360,100]{0,1:T(8,128)}, u32[]{:S(2)}) %copy-start.3) | copy-done | bytes 6144024
  52.0 7.1 %sum_groups.1 = f32[120,100]{1,0:T(8,128)S(1)} custom-call(f32[100,15360]{1,0:T(8,128)S(1)} %bitcast.46, s32[1,15360]{1,0:T(1,128)S(1)} %bitcast.47, f32[1,15360]{1,0:T(1,128)S(1)} %bitcast.54), custom_call_target="tpu_custom_call" | custom-call | flops 1 | bytes 1 | tf_op jit(solution)/shard_map/sum_groups/pallas_call | solution.py:269
  59.1 1.3 collective-permute-start.5
  60.4 10.0 %collective-permute-done.5 = f32[120,100]{1,0:T(8,128)S(1)} collective-permute-done((f32[120,100]{1,0:T(8,128)S(1)}, f32[120,100]{1,0:T(8,128)S(1)}, u32[]{:S(2)}, u32[]{:S(2)}) %collective-permute-start.5) | collective-permute-done | bytes 48032 | tf_op jit(solution)/shard_map/ppermute | solution.py:595
  70.4 0.7 copy.43
  71.1 0.0 all-gather.4.cloned.1.call-update
  71.2 3.2 %copy-done.5 = f32[15360,128]{1,0:T(8,128)S(1)} copy-done((f32[15360,128]{1,0:T(8,128)S(1)}, f32[15360,128]{1,0:T(8,128)}, u32[]{:S(2)}) %copy-start.5) | copy-done | bytes 7864344
  74.4 4.8 %lay_late.1 = f32[32,144,128]{2,1,0:T(8,128)} custom-call(f32[15360,128]{1,0:T(8,128)S(1)} %copy-done.5), custom_call_target="tpu_custom_call" | custom-call | flops 1 | bytes 1 | tf_op jit(solution)/shard_map/lay_late/pallas_call | solution.py:210
  79.3 1.2 stack.28
  80.4 0.0 copy-start.16
  80.5 0.0 copy-start.17
  80.5 1.2 convert_element_type.37.facts_ref
  81.6 0.0 copy-start.15
  81.6 0.0 copy-start.23
  81.7 4.7 %pick_facts.1 = f32[80,32]{1,0:T(8,128)S(1)} custom-call(s32[1,15360]{1,0:T(1,128)S(1)} %bitcast.50, f32[5,15360]{1,0:T(8,128)S(1)} %convert_element_type.37.facts_ref), custom_call_target="tpu_custom_call" | custom-call | flops 1 | bytes 1 | tf_op jit(solution)/shard_map/pick_facts/pallas_call | solution.py:297
  86.4 0.1 reshape.63
  86.5 10.0 %all-to-all-start.2 = ((f32[32,144,128]{2,1,0:T(8,128)}), f32[32,144,128]{2,1,0:T(8,128)}, u32[]{:S(2)}, u32[]{:S(2)}) async-start(f32[32,144,128]{2,1,0:T(8,128)} %lay_late.1), calls=%async_computation.2 | async-start | bytes 4718592 | tf_op jit(solution)/shard_map/all_to_all | solution.py:592
  96.6 3.3 %gather_fusion = s32[480]{0:T(512)S(1)} fusion(s32[128]{0:T(128)S(1)} %copy-done.11, s32[1024]{0:T(1024)S(1)} %pad_clamp_fusion), kind=kCustom, calls=%fused_computation | custom fusion | bytes 5760 | tf_op jit(solution)/shard_map/jit(_take)/gather | solution.py:601
  100.0 0.3 collective-permute-start.4
  100.3 0.1 reshape.64
  100.4 1.3 collective-permute-start.2
  101.8 0.1 fusion.24
  101.9 0.0 copy-done.20
  101.9 0.1 fusion.23
  102.0 0.0 copy-done.14
  102.1 0.2 fusion.12
  102.3 0.2 convolution_add_fusion
  102.5 0.1 reshape.65
  102.6 0.5 slice.53
  103.1 0.6 broadcast_compare_fusion
  103.7 0.1 copy.42.take_ref
  103.9 2.5 fusion.22
  106.4 3.2 %copy-done.6 = f32[15360,128]{1,0:T(8,128)S(1)} copy-done((f32[15360,128]{1,0:T(8,128)S(1)}, f32[15360,128]{1,0:T(8,128)}, u32[]{:S(2)}) %copy-start.6) | copy-done | bytes 7864344
  109.7 23.4 %merge_rows.1 = f32[32,160,128]{2,1,0:T(8,128)} custom-call(s32[15360]{0:T(1024)S(1)} %collective-permute-done.place_ref, f32[40,15360]{1,0:T(8,128)S(1)} %collective-permute-done.1.raw_ref, f32[15360,128]{1,0:T(8,128)S(1)} %copy-done.6, f32[480,1]{1,0:T(8,128)S(1)} %copy.42.take_ref), custom_call_target="tpu_custom_call" | custom-call | tf_op jit(solution)/shard_map/merge_rows/pallas_call | solution.py:239
  133.0 3.4 %collective-permute-done.2.got0 = f32[32,96,128]{2,1,0:T(8,128)} collective-permute-done((f32[32,96,128]{2,1,0:T(8,128)}, f32[32,96,128]{2,1,0:T(8,128)}, u32[]{:S(2)}, u32[]{:S(2)}) %collective-permute-start.2) | collective-permute-done | bytes 1572896 | tf_op jit(solution)/shard_map/ppermute | solution.py:613
  136.4 8.4 %all-to-all-start.1 = ((f32[32,160,128]{2,1,0:T(8,128)}), f32[32,160,128]{2,1,0:T(8,128)S(1)}, u32[]{:S(2)}, u32[]{:S(2)}) async-start(f32[32,160,128]{2,1,0:T(8,128)} %merge_rows.1), calls=%async_computation.1 | async-start | bytes 5242880 | tf_op jit(solution)/shard_map/all_to_all | solution.py:592
  144.8 3.0 %slice.73 = f32[32,120,128]{2,1,0:T(8,128)} slice(f32[32,144,128]{2,1,0:T(8,128)} %all-to-all-done.2.own1), slice={[0:32], [0:120], [0:128]} | slice | bytes 3932160 | tf_op jit(solution)/shard_map/slice | solution.py:617
  147.7 1.1 collective-permute-start.3
  148.9 2.0 fusion
  150.9 4.0 %pad_maximum_fusion.filter_hbm = f32[32,256,256]{2,1,0:T(8,128)} fusion(f32[32,256,128]{2,1,0:T(8,128)S(1)} %get-tuple-element.34, f32[32,256,128]{2,1,0:T(8,128)S(1)} %get-tuple-element.33), kind=kLoop, calls=%fused_computation.1 | loop fusion | flops 2097152 | bytes 16777216 | tf_op jit(solution)/shard_map/concatenate | solution.py:561
  154.9 0.9 copy.48.good_ref
  155.7 1.5 convolution_convert_fusion
  157.3 1.0 copy.45
  158.3 1.5 convolution_convert_fusion.1
  159.8 1.0 copy.44
  160.9 0.9 fusion.6.member_ref
  161.7 5.3 %copy.49.common_ref = f32[32,240,100]{2,1,0:T(8,128)} copy(f32[32,240,100]{1,2,0:T(8,128)} %all-gather.4.cloned.1.call-done) | data formatting | bytes 6144000 | tf_op jit(solution)/shard_map/all_gather | solution.py:598
  167.0 11.3 %all-to-all-done.1.early = f32[32,160,128]{2,1,0:T(8,128)S(1)} async-done(((f32[32,160,128]{2,1,0:T(8,128)}), f32[32,160,128]{2,1,0:T(8,128)S(1)}, u32[]{:S(2)}, u32[]{:S(2)}) %all-to-all-start.1) | async-done | bytes 2621472 | tf_op jit(solution)/shard_map/all_to_all | solution.py:592
  178.3 13.9 %collective-permute-done.3.got1 = f32[32,120,128]{2,1,0:T(8,128)} collective-permute-done((f32[32,120,128]{2,1,0:T(8,128)}, f32[32,120,128]{2,1,0:T(8,128)}, u32[]{:S(2)}, u32[]{:S(2)}) %collective-permute-start.3) | collective-permute-done | bytes 1966112 | tf_op jit(solution)/shard_map/ppermute | solution.py:617
  192.3 54.5 %deconvolve.1 = f32[480,3200]{1,0:T(8,128)} custom-call(f32[32,160,128]{2,1,0:T(8,128)} %copy-done.12, f32[32,96,128]{2,1,0:T(8,128)} %all-to-all-done.own0, f32[32,144,128]{2,1,0:T(8,128)} %all-to-all-done.2.own1, f32[32,96,128]{2,1,0:T(8,128)} %collective-permute-done.2.got0, f32[32,120,128]{2,1,0:T(8,128)} %collective-permute-done.3.got1, ...), custom_call_target="tpu_custom_call" | custom-call | tf_op jit(solution)/shard_map/deconvolve/pallas_call | solution.py:517
  (56 shorter events, 0.3 us)
Async XLA Ops:
  6.5 97.3 %copy-start = (f32[480]{0:T(512)S(1)}, f32[480]{0:T(512)}, u32[]{:S(2)}) copy-start(f32[480]{0:T(512)} %param.30) | copy-start | bytes 5764
  6.5 0.8 copy-start.9
  9.5 96.9 %collective-permute-start = (s32[15360]{0:T(1024)S(1)}, s32[15360]{0:T(1024)S(1)}, u32[]{:S(2)}, u32[]{:S(2)}) collective-permute-start(s32[15360]{0:T(1024)S(1)} %bitcast.51), channel_id=1, source_target_pairs={{0,32},{32,0},{64,96},{96,64},{1,33},{33,1},{65,97},{97,65},{2,34}... | collective-permute-start | bytes 184328 | tf_op jit(solution)/shard_map/ppermute | solution.py:585
  14.9 71.6 %collective-permute-start.1 = (f32[40,15360]{1,0:T(8,128)}, f32[40,15360]{1,0:T(8,128)S(1)}, u32[]{:S(2)}, u32[]{:S(2)}) collective-permute-start(f32[40,15360]{1,0:T(8,128)} %slice.72), channel_id=1, source_target_pairs={{0,32},{32,0},{64,96},{96,64},{1,33},{33,1},{65,97},{97,65},{2,34}... | collective-permute-start | bytes 7372808 | tf_op jit(solution)/shard_map/ppermute | solution.py:580
  15.0 2.8 %copy-start.2 = (f32[15360,100]{0,1:T(8,128)S(1)}, f32[15360,100]{0,1:T(8,128)}, u32[]{:S(2)}) copy-start(f32[15360,100]{0,1:T(8,128)} %param.24) | copy-start | bytes 18432004
  17.8 31.4 %copy-start.13 = (s32[15360]{0:T(1024)S(1)}, s32[15360]{0:T(1024)}, u32[]{:S(2)}) copy-start(s32[15360]{0:T(1024)} %param.25) | copy-start | bytes 184324
  17.8 31.4 %copy-start.18 = (s32[15360]{0:T(1024)S(1)}, s32[15360]{0:T(1024)}, u32[]{:S(2)}) copy-start(s32[15360]{0:T(1024)} %param.26) | copy-start | bytes 184324
  35.2 3.1 %copy-start.4 = (f32[15360,128]{1,0:T(8,128)}, f32[15360,128]{1,0:T(8,128)S(1)}, u32[]{:S(2)}) copy-start(f32[15360,128]{1,0:T(8,128)S(1)} %get-tuple-element.20.rows_ref.own_ref) | copy-start | bytes 23592964
  38.3 1.1 copy-start.8
  39.4 47.1 %all-to-all-start = ((f32[32,96,128]{2,1,0:T(8,128)}), f32[32,96,128]{2,1,0:T(8,128)}, u32[]{:S(2)}, u32[]{:S(2)}) async-start(f32[32,96,128]{2,1,0:T(8,128)} %copy-done.8), calls=%async_computation | async-start | bytes 3145728 | tf_op jit(solution)/shard_map/all_to_all | solution.py:592
  49.1 11.3 %copy-start.19 = (s32[15360]{0:T(1024)S(1)}, s32[15360]{0:T(1024)}, u32[]{:S(2)}) copy-start(s32[15360]{0:T(1024)} %param.28) | copy-start | bytes 184324
  49.1 22.1 %copy-start.10 = (s32[15360]{0:T(1024)S(1)}, s32[15360]{0:T(1024)}, u32[]{:S(2)}) copy-start(s32[15360]{0:T(1024)} %param.27) | copy-start | bytes 184324
  49.1 112.6 %all-gather.4.cloned.1.call-start = ((), (), s32[]{:S(2)}) async-start(), calls=%async_computation.3 | async-start | bytes 3514368 | tf_op jit(solution)/shard_map/all_gather | solution.py:598
  49.2 2.8 %copy-start.3 = (f32[15360,100]{0,1:T(8,128)S(1)}, f32[15360,100]{0,1:T(8,128)}, u32[]{:S(2)}) copy-start(f32[15360,100]{0,1:T(8,128)} %param.24) | copy-start | bytes 18432004
  59.1 11.3 %collective-permute-start.5 = (f32[120,100]{1,0:T(8,128)S(1)}, f32[120,100]{1,0:T(8,128)S(1)}, u32[]{:S(2)}, u32[]{:S(2)}) collective-permute-start(f32[120,100]{1,0:T(8,128)S(1)} %sum_groups.1), channel_id=1, source_target_pairs={{0,32},{32,0},{64,96},{96,64},{1,33},{33,1},{65,97},{97,65},{2,34}... | collective-permute-start | bytes 144008 | tf_op jit(solution)/shard_map/ppermute | solution.py:595
  71.2 3.2 %copy-start.5 = (f32[15360,128]{1,0:T(8,128)S(1)}, f32[15360,128]{1,0:T(8,128)}, u32[]{:S(2)}) copy-start(f32[15360,128]{1,0:T(8,128)} %copy-done.4) | copy-start | bytes 23592964
  79.3 17.3 %copy-start.11 = (s32[128]{0:T(128)S(1)}, s32[128]{0:T(128)}, u32[]{:S(2)}) copy-start(s32[128]{0:T(128)} %param.29) | copy-start | bytes 1540
  80.4 19.9 %copy-start.22 = (f32[3200]{0:T(1024)S(1)}, f32[3200]{0:T(1024)}, u32[]{:S(2)}) copy-start(f32[3200]{0:T(1024)} %param.31) | copy-start | bytes 38404
  80.4 21.3 %copy-start.21 = (f32[32,32]{1,0:T(8,128)S(1)}, f32[32,32]{1,0:T(8,128)}, u32[]{:S(2)}) copy-start(f32[32,32]{1,0:T(8,128)} %constant.116.clone) | copy-start | bytes 12292
  80.4 21.5 %copy-start.20 = (f32[32,32]{1,0:T(8,128)S(1)}, f32[32,32]{1,0:T(8,128)}, u32[]{:S(2)}) copy-start(f32[32,32]{1,0:T(8,128)} %constant.115.clone) | copy-start | bytes 12292
  80.4 21.6 %copy-start.14 = (f32[100,200]{1,0:T(8,128)S(1)}, f32[100,200]{1,0:T(8,128)}, u32[]{:S(2)}) copy-start(f32[100,200]{1,0:T(8,128)} %constant.130) | copy-start | bytes 240004
  80.4 21.6 %copy-start.16 = (f32[32,100]{1,0:T(8,128)S(1)}, f32[32,100]{1,0:T(8,128)}, u32[]{:S(2)}) copy-start(f32[32,100]{1,0:T(8,128)} %constant.118.clone) | copy-start | bytes 38404
  80.5 21.6 %copy-start.17 = (f32[32,100]{1,0:T(8,128)S(1)}, f32[32,100]{1,0:T(8,128)}, u32[]{:S(2)}) copy-start(f32[32,100]{1,0:T(8,128)} %constant.117.clone) | copy-start | bytes 38404
  81.6 20.6 %copy-start.15 = (f32[100,200]{1,0:T(8,128)S(1)}, f32[100,200]{1,0:T(8,128)}, u32[]{:S(2)}) copy-start(f32[100,200]{1,0:T(8,128)} %constant.131) | copy-start | bytes 240004
  81.6 21.4 %copy-start.23 = (s32[480]{0:T(512)S(1)}, s32[480]{0:T(512)}, u32[]{:S(2)}) copy-start(s32[480]{0:T(512)} %constant.111.clone) | copy-start | bytes 5764
  86.5 49.9 %all-to-all-start.2 = ((f32[32,144,128]{2,1,0:T(8,128)}), f32[32,144,128]{2,1,0:T(8,128)}, u32[]{:S(2)}, u32[]{:S(2)}) async-start(f32[32,144,128]{2,1,0:T(8,128)} %lay_late.1), calls=%async_computation.2 | async-start | bytes 4718592 | tf_op jit(solution)/shard_map/all_to_all | solution.py:592
  100.0 54.8 %collective-permute-start.4 = (s32[3,480]{1,0:T(4,128)S(1)}, s32[3,480]{1,0:T(4,128)S(1)}, u32[]{:S(2)}, u32[]{:S(2)}) collective-permute-start(s32[3,480]{1,0:T(4,128)S(1)} %pad_add_fusion), channel_id=1, source_target_pairs={{0,32},{32,0},{64,96},{96,64},{1,33},{33,1},{65,97},{97,65},{2,34}... | collective-permute-start | bytes 17288 | tf_op jit(solution)/shard_map/ppermute | solution.py:605
  100.4 35.9 %collective-permute-start.2 = (f32[32,96,128]{2,1,0:T(8,128)}, f32[32,96,128]{2,1,0:T(8,128)}, u32[]{:S(2)}, u32[]{:S(2)}) collective-permute-start(f32[32,96,128]{2,1,0:T(8,128)} %all-to-all-done.own0), channel_id=1, source_target_pairs={{0,32},{32,0},{64,96},{96,64},{1,33},{33,1},{65,97},{97,65},{2,34}... | collective-permute-start | bytes 4718600 | tf_op jit(solution)/shard_map/ppermute | solution.py:613
  103.9 29.1 %copy-start.7 = (f32[480,1]{1,0:T(8,128)}, f32[480,1]{1,0:T(8,128)S(1)}, u32[]{:S(2)}) copy-start(f32[480,1]{1,0:T(8,128)S(1)} %copy.42.take_ref) | copy-start | bytes 5764
  106.4 3.2 %copy-start.6 = (f32[15360,128]{1,0:T(8,128)S(1)}, f32[15360,128]{1,0:T(8,128)}, u32[]{:S(2)}) copy-start(f32[15360,128]{1,0:T(8,128)} %copy-done.4) | copy-start | bytes 23592964
  136.4 41.9 %all-to-all-start.1 = ((f32[32,160,128]{2,1,0:T(8,128)}), f32[32,160,128]{2,1,0:T(8,128)S(1)}, u32[]{:S(2)}, u32[]{:S(2)}) async-start(f32[32,160,128]{2,1,0:T(8,128)} %merge_rows.1), calls=%async_computation.1 | async-start | bytes 5242880 | tf_op jit(solution)/shard_map/all_to_all | solution.py:592
  147.7 44.5 %collective-permute-start.3 = (f32[32,120,128]{2,1,0:T(8,128)}, f32[32,120,128]{2,1,0:T(8,128)}, u32[]{:S(2)}, u32[]{:S(2)}) collective-permute-start(f32[32,120,128]{2,1,0:T(8,128)} %slice.73), channel_id=1, source_target_pairs={{0,32},{32,0},{64,96},{96,64},{1,33},{33,1},{65,97},{97,65},{2,34}... | collective-permute-start | bytes 5898248 | tf_op jit(solution)/shard_map/ppermute | solution.py:617
  178.3 13.9 %copy-start.12 = (f32[32,160,128]{2,1,0:T(8,128)}, f32[32,160,128]{2,1,0:T(8,128)S(1)}, u32[]{:S(2)}) copy-start(f32[32,160,128]{2,1,0:T(8,128)S(1)} %all-to-all-done.1.early) | copy-start | bytes 7864324
  192.3 54.5 %copy-start.1 = (f32[480]{0:T(512)S(1)}, f32[480]{0:T(512)}, u32[]{:S(2)}) copy-start(f32[480]{0:T(512)} %param.30) | copy-start | bytes 5764
Sparse Core Ops, SparseCore 0:
  71.3 62.9 all-gather.3

commit v5 on v4

--- a/solution.py
+++ b/solution.py
@@ -166,7 +166,7 @@
     lax.fori_loop(0, steps // 2, both, 0)
 
 
-def late_kernel(which, rows_ref, out_ref):
+def late_kernel(which, rows_ref, out_ref, low=0, high=SLABS):
     size = LATE_ROWS[which]
 
     def one_slot(slot, carry):
@@ -176,19 +176,22 @@
             out_ref[slot, :, piece * LATE : (piece + 1) * LATE] = rows_ref[pl.ds(at, size), EARLY:SLAB]
         return carry
 
-    lax.fori_loop(0, SLABS, one_slot, 0)
+    lax.fori_loop(low, high, one_slot, 0)
 
 
 def late_shape(which):
     return jax.ShapeDtypeStruct((SLABS, LATE_ROWS[which], PART), jnp.float32)
 
 
-def pack_kernel(place_ref, raw_ref, late_ref, rows_out, rows_ref, even_ref, odd_ref, rows_done):
+def pack_kernel(place_ref, raw_ref, late_out, rows_out, rows_ref, late_ref, even_ref, odd_ref, rows_done, late_done):
     turned_scatter(place_ref, raw_ref, rows_ref, even_ref, odd_ref)
     keep = pltpu.make_async_copy(rows_ref, rows_out, rows_done)
     keep.start()
     late_kernel(0, rows_ref, late_ref)
+    send = pltpu.make_async_copy(late_ref, late_out, late_done)
+    send.start()
     keep.wait()
+    send.wait()
 
 
 def pack_rows(place, raw_turned):
@@ -196,30 +199,52 @@
     return pl.pallas_call(
         pack_kernel,
         in_specs=[pl.BlockSpec(memory_space=pltpu.SMEM)] + whole(1),
-        out_specs=whole(1) + [pl.BlockSpec(memory_space=pl.ANY)],
+        out_specs=[pl.BlockSpec(memory_space=pltpu.HBM)] * 2,
         out_shape=[late_shape(0), jax.ShapeDtypeStruct((chan_count, PART), jnp.float32)],
-        scratch_shapes=[pltpu.VMEM((chan_count, PART), jnp.float32)]
+        scratch_shapes=[
+            pltpu.VMEM((chan_count, PART), jnp.float32),
+            pltpu.VMEM((SLABS, LATE_ROWS[0], PART), jnp.float32),
+        ]
         + [pltpu.VMEM((WIDE, PART), jnp.float32)] * 2
-        + [pltpu.SemaphoreType.DMA],
-        compiler_params=roomy(32),
+        + [pltpu.SemaphoreType.DMA] * 2,
+        compiler_params=roomy(60),
         name="pack_rows",
     )(place, raw_turned)
 
 
+def fetched_late_kernel(which, rows_hbm, out_ref, rows_ref, done_ref):
+    quarter = rows_ref.shape[0] // 4
+    copies = [
+        pltpu.make_async_copy(
+            rows_hbm.at[pl.ds(part * quarter, quarter)], rows_ref.at[pl.ds(part * quarter, quarter)], done_ref.at[part]
+        )
+        for part in range(4)
+    ]
+    for copy in copies:
+        copy.start()
+    for part, copy in enumerate(copies):
+        copy.wait()
+        late_kernel(which, rows_ref, out_ref, part * SLABS // 4, (part + 1) * SLABS // 4)
+
+
 def lay_late(rows, which):
     return pl.pallas_call(
-        functools.partial(late_kernel, which),
-        in_specs=whole(1),
+        functools.partial(fetched_late_kernel, which),
+        in_specs=[pl.BlockSpec(memory_space=pltpu.HBM)],
         out_specs=whole(1)[0],
         out_shape=late_shape(which),
-        compiler_params=roomy(20),
+        scratch_shapes=[pltpu.VMEM(rows.shape, jnp.float32), pltpu.SemaphoreType.DMA((4,))],
+        compiler_params=roomy(60),
         name="lay_late",
         cost_estimate=light,
     )(rows)
 
 
-def merge_kernel(place_ref, raw_ref, own_ref, take_ref, out_ref, rows_ref, even_ref, odd_ref):
+def merge_kernel(place_ref, raw_ref, own_hbm, take_ref, out_ref, rows_ref, even_ref, odd_ref, own_ref, own_done):
+    fetch = pltpu.make_async_copy(own_hbm, own_ref, own_done)
+    fetch.start()
     turned_scatter(place_ref, raw_ref, rows_ref, even_ref, odd_ref)
+    fetch.wait()
 
     def one_slot(slot, carry):
         start = pl.multiple_of(slot * WIRES, 8)
@@ -238,11 +263,13 @@
     chan_count = raw_turned.shape[1]
     return pl.pallas_call(
         merge_kernel,
-        in_specs=[pl.BlockSpec(memory_space=pltpu.SMEM)] + whole(3),
+        in_specs=[pl.BlockSpec(memory_space=pltpu.SMEM)] + whole(1) + [pl.BlockSpec(memory_space=pltpu.HBM)] + whole(1),
         out_specs=whole(1)[0],
         out_shape=jax.ShapeDtypeStruct((SLABS, EARLY_ROWS, PART), jnp.float32),
-        scratch_shapes=[pltpu.VMEM((chan_count, PART), jnp.float32)] + [pltpu.VMEM((WIDE, PART), jnp.float32)] * 2,
-        compiler_params=roomy(40),
+        scratch_shapes=[pltpu.VMEM((chan_count, PART), jnp.float32)]
+        + [pltpu.VMEM((WIDE, PART), jnp.float32)] * 2
+        + [pltpu.VMEM((chan_count, PART), jnp.float32), pltpu.SemaphoreType.DMA],
+        compiler_params=roomy(60),
         name="merge_rows",
     )(place, raw_turned, own, take)
 
@@ -593,28 +620,28 @@
 
     own0 = over_ticks(late0)
     common_got = lax.ppermute(common, "apa", swap)
+    facts = jnp.stack([chan_wire >> 5, chan_wire & 31, local_group, bad, chan_plane - pair_base])
+    facts = pick_facts(later_place - tick_index * WIRES, facts.astype(jnp.float32)).astype(jnp.int32)
+    own0, late1, early_got, common_got = lax.optimization_barrier((own0, late1, early_got, common_got))
     first = jnp.where(parity == 0, common, common_got)
     second = jnp.where(parity == 0, common_got, common)
     commons = lax.all_gather(jnp.concatenate([first, second], axis=0), "tick")
-    facts = jnp.stack([chan_wire >> 5, chan_wire & 31, local_group, bad, chan_plane - pair_base])
-    facts = pick_facts(later_place - tick_index * WIRES, facts.astype(jnp.float32)).astype(jnp.int32)
+    own1 = over_ticks(late1)
+    got0 = lax.ppermute(own0[:, : SENT[0]], "apa", swap)
+    take = jnp.asarray(row_order()) < cross_count
+    row_take = take.astype(jnp.float32)[:, None]
+    early = merge_rows(place_got, early_got, rows, row_take)
+    early, got0, facts = lax.optimization_barrier((early, got0, facts))
+    early = over_ticks(early)
+    got1 = lax.ppermute(own1[:, : SENT[1]], "apa", swap)
     row_offset = jnp.take(plane_offset, facts[4] + pair_base)
     row_wire = (facts[0] * 32 + facts[1] + row_offset) % WIRES
     facts = jnp.stack([row_wire, facts[2] + parity * group_count, facts[3]])
-    take = jnp.asarray(row_order()) < cross_count
     facts = jnp.where(take[None, :], lax.ppermute(facts, "apa", swap), facts)
-    row_take = take.astype(jnp.float32)[:, None]
     row_good = 1.0 - facts[2].astype(jnp.float32)[:, None]
     member = (facts[1][:, None] == jnp.arange(2 * group_count, dtype=jnp.int32)[None, :]).astype(jnp.bfloat16)
     high, low = picked_tables(facts[0])
     filters = make_filter(wire_kernel, time_kernel)
-    own0, late1, early_got = lax.optimization_barrier((own0, late1, early_got))
-    own1 = over_ticks(late1)
-    got0 = lax.ppermute(own0[:, : SENT[0]], "apa", swap)
-    early = merge_rows(place_got, early_got, rows, row_take)
-    early, got0 = lax.optimization_barrier((early, got0))
-    early = over_ticks(early)
-    got1 = lax.ppermute(own1[:, : SENT[1]], "apa", swap)
     return tail(early, (own0, own1), (got0, got1), row_take, row_good, commons, member, high, low, filters)[None]
 
 

time: 254 us -> 251 us (0.988)
  local copies, waits for them, and re-layouts: 37.9 us -> 24.2 us
  other arithmetic: 8.75 us -> 13.5 us
  Pallas kernels: 114 us -> 118 us
  waiting for transfers between devices: 38.6 us -> 41.6 us
    ppermute x1, waiting for transfers between devices: 0.01 us -> 35.3 us  [shards(): facts = jnp.where(take[None, :], lax.ppermute(facts, 'apa', swap), facts)]
    ppermute x1, waiting for transfers between devices: 13.9 us -> 0.01 us  [shards(): got1 = lax.ppermute(own1[:, :SENT[1]], 'apa', swap)]
    unnamed x49 -> x43, local copies, waits for them, and re-layouts: 18 us -> 5.75 us
    all_to_all x3, waiting for transfers between devices: 11.3 us -> 0.01 us  [over_ticks(): lax.all_to_all(value, 'tick', split_axis=0, concat_axis=0, tiled=True)]
    ppermute x1, waiting for transfers between devices: 9.96 us -> 6.23 us  [shards(): common_got = lax.ppermute(common, 'apa', swap)]
    concatenate x1, other arithmetic: 3.98 us -> 7.43 us  [make_filter(): return jnp.concatenate([real / denominator, -imag / denominator], axis=2)]
    ppermute x1, waiting for transfers between devices: 3.35 us -> 0.01 us  [shards(): got0 = lax.ppermute(own0[:, :SENT[0]], 'apa', swap)]
  transfers between devices with their start and end apart: 10 -> 10, of which waited for: 4 -> 2; matrix products, arithmetic and copies ran while one was open for 14% -> 14% of each run, Pallas kernels for 23% -> 25%
where the time goes in v5:
time: 251 us
  Pallas kernels  118 us (47%)
  waiting for transfers between devices  41.6 us (17%)
  starting transfers between devices  33.5 us (13%)
  local copies, waits for them, and re-layouts  24.2 us (10%)
  between operations  13.9 us (6%)
  other arithmetic  13.5 us (5%)
  matrix products  6.28 us (3%)
    pallas_call x1, Pallas kernels, tail(): pl.pallas_call(tail_kernel, in_specs=whole(11) + [pl.BlockSpec(memory_spa...  54.5 us
    ppermute x1, waiting for transfers between devices, shards(): facts = jnp.where(take[None, :], lax.ppermute(facts, 'apa', swap), facts)  35.3 us
    all_to_all x3, starting transfers between devices, over_ticks(): lax.all_to_all(value, 'tick', split_axis=0, concat_axis=0, tiled=True)  26.8 us
    pallas_call x1, Pallas kernels, merge_rows(): pl.pallas_call(merge_kernel, in_specs=[pl.BlockSpec(memory_space=pltpu.SM...  23.5 us
    pallas_call x1, Pallas kernels, pack_rows(): pl.pallas_call(pack_kernel, in_specs=[pl.BlockSpec(memory_space=pltpu.SME...  19.3 us
    concatenate x1, other arithmetic, make_filter(): return jnp.concatenate([real / denominator, -imag / denominator], axis=2)  7.43 us
    pallas_call x1, Pallas kernels, sum_groups(): pl.pallas_call(group_kernel, in_specs=whole(3), out_specs=whole(1)[0], ou...  7.07 us
    pallas_call x1, Pallas kernels, lay_late(): pl.pallas_call(functools.partial(fetched_late_kernel, which), in_specs=[p...  6.4 us
  transfers between devices with their start and end apart: 10, of which 2 were waited for; matrix products, arithmetic and copies ran while one was open for 14% of the time, Pallas kernels for 25%

profile of v5, /device:TPU:1, one launch (start us, length us, event | category | flops | bytes accessed | tf_op | source)
XLA Modules:
  0.0 250.5 jit_solution(6059405072498600946)
XLA Ops:
  6.5 3.3 %slice.72 = f32[40,15360]{1,0:T(8,128)} slice(f32[100,15360]{1,0:T(8,128)} %bitcast.44), slice={[0:40], [0:15360]} | slice | bytes 4915200 | tf_op jit(solution)/shard_map/slice | solution.py:607
  9.9 2.0 collective-permute-start.1
  11.9 2.1 rank_rows.1
  14.0 0.6 copy-done.4
  14.7 19.3 %pack_rows.1 = (f32[32,96,128]{2,1,0:T(8,128)}, f32[15360,128]{1,0:T(8,128)}) custom-call(s32[15360]{0:T(1024)} %bitcast.51, f32[100,15360]{1,0:T(8,128)} %bitcast.45), custom_call_target="tpu_custom_call" | custom-call | tf_op jit(solution)/shard_map/pack_rows/pallas_call | solution.py:199
  34.0 9.1 %all-to-all-start = ((f32[32,96,128]{2,1,0:T(8,128)}), f32[32,96,128]{2,1,0:T(8,128)S(1)}, u32[]{:S(2)}, u32[]{:S(2)}) async-start(f32[32,96,128]{2,1,0:T(8,128)} %get-tuple-element.21), calls=%async_computation | async-start | bytes 3145728 | tf_op jit(solution)/shard_map/all_to_all | solution.py:619
  43.1 0.0 all-gather.4.cloned.1.call-start
  43.1 0.3 collective-permute-start
  43.5 0.0 copy-start.2
  43.5 2.8 %copy-done.2 = f32[15360,100]{0,1:T(8,128)S(1)} copy-done((f32[15360,100]{0,1:T(8,128)S(1)}, f32[15360,100]{0,1:T(8,128)}, u32[]{:S(2)}) %copy-start.2) | copy-done | bytes 6144024
  46.3 7.1 %sum_groups.1 = f32[120,100]{1,0:T(8,128)S(1)} custom-call(f32[100,15360]{1,0:T(8,128)S(1)} %bitcast.46, s32[1,15360]{1,0:T(1,128)S(1)} %bitcast.47, f32[1,15360]{1,0:T(1,128)S(1)} %bitcast.54), custom_call_target="tpu_custom_call" | custom-call | flops 1 | bytes 1 | tf_op jit(solution)/shard_map/sum_groups/pallas_call | solution.py:296
  53.4 1.3 collective-permute-start.2
  54.7 6.4 %lay_late.1 = f32[32,144,128]{2,1,0:T(8,128)} custom-call(f32[15360,128]{1,0:T(8,128)} %get-tuple-element.22.rows_hbm.own_hbm), custom_call_target="tpu_custom_call" | custom-call | flops 1 | bytes 1 | tf_op jit(solution)/shard_map/lay_late/pallas_call | solution.py:231
  61.1 0.0 copy-start.17
  61.1 0.0 copy-start.15
  61.1 0.0 copy-start.16
  61.2 0.0 copy-start.11
  61.2 0.0 copy-start.13
  61.2 6.2 %collective-permute-done.2 = f32[120,100]{1,0:T(8,128)S(1)} collective-permute-done((f32[120,100]{1,0:T(8,128)S(1)}, f32[120,100]{1,0:T(8,128)S(1)}, u32[]{:S(2)}, u32[]{:S(2)}) %collective-permute-start.2) | collective-permute-done | bytes 48032 | tf_op jit(solution)/shard_map/ppermute | solution.py:622
  67.4 0.0 all-to-all-done.own0
  67.4 0.0 collective-permute-done.1.raw_ref
  67.4 0.0 copy-start.12
  67.5 0.0 copy-start.19
  67.5 0.8 copy.43
  68.2 0.0 all-gather.4.cloned.1.call-update
  68.3 0.1 reshape.64
  68.4 0.2 copy-done.8
  68.6 10.0 %all-to-all-start.2 = ((f32[32,144,128]{2,1,0:T(8,128)}), f32[32,144,128]{2,1,0:T(8,128)S(1)}, u32[]{:S(2)}, u32[]{:S(2)}) async-start(f32[32,144,128]{2,1,0:T(8,128)} %lay_late.1), calls=%async_computation.2 | async-start | bytes 4718592 | tf_op jit(solution)/shard_map/all_to_all | solution.py:619
  78.6 0.1 fusion.24
  78.7 0.0 copy-done.15
  78.8 1.3 collective-permute-start.3
  80.1 0.1 fusion.23
  80.2 0.5 stack.25
  80.8 4.7 %pick_facts.1 = f32[80,32]{1,0:T(8,128)S(1)} custom-call(s32[1,15360]{1,0:T(1,128)S(1)} %bitcast.50, f32[5,15360]{1,0:T(8,128)S(1)} %convert_element_type.38.facts_ref), custom_call_target="tpu_custom_call" | custom-call | flops 1 | bytes 1 | tf_op jit(solution)/shard_map/pick_facts/pallas_call | solution.py:324
  85.5 0.9 fusion.12
  86.4 0.9 convolution_add_fusion
  87.4 0.1 reshape.65
  87.5 0.5 slice.53
  88.0 0.6 broadcast_compare_fusion
  88.6 0.8 copy.42.take_ref
  89.5 0.1 reshape.63
  89.6 2.2 fusion.22
  91.8 0.0 collective-permute-done.place_ref
  91.8 23.5 %merge_rows.1 = f32[32,160,128]{2,1,0:T(8,128)} custom-call(s32[15360]{0:T(1024)} %collective-permute-done.place_ref, f32[40,15360]{1,0:T(8,128)} %collective-permute-done.1.raw_ref, f32[15360,128]{1,0:T(8,128)} %get-tuple-element.22.rows_hbm.own_hbm, f32[480,1]{1,0:T(8,128)} %copy.42.take_ref), custom_call_target="tpu_custom_call" | custom-call | tf_op jit(solution)/shard_map/merge_rows/pallas_call | solution.py:264
  115.3 0.0 collective-permute-done.3.got0
  115.4 7.7 %all-to-all-start.1 = ((f32[32,160,128]{2,1,0:T(8,128)}), f32[32,160,128]{2,1,0:T(8,128)}, u32[]{:S(2)}, u32[]{:S(2)}) async-start(f32[32,160,128]{2,1,0:T(8,128)} %merge_rows.1), calls=%async_computation.1 | async-start | bytes 5242880 | tf_op jit(solution)/shard_map/all_to_all | solution.py:619
  123.1 0.0 copy-start.6
  123.1 4.4 %fusion = (f32[32,256,128]{2,1,0:T(8,128)}, f32[32,256,128]{2,1,0:T(8,128)}) fusion(f32[32,128]{1,0:T(8,128)S(1)} %get-tuple-element.40, f32[256]{0:T(256)S(1)} %get-tuple-element.47, f32[32,128]{1,0:T(8,128)S(1)} %get-tuple-element.39, f32[256]{0:T(256)S(1)} %get-tuple-element.46), kind=kLoop, calls=%fused_computation.5 | loop fusion | flops 13631488 | bytes 8423424 | tf_op jit(solution)/shard_map/div | solution.py:588
  127.5 3.3 %gather_fusion = s32[480]{0:T(512)S(1)} fusion(s32[128]{0:T(128)S(1)} %copy-done.6, s32[1024]{0:T(1024)S(1)} %pad_clamp_fusion), kind=kCustom, calls=%fused_computation | custom fusion | bytes 5760 | tf_op jit(solution)/shard_map/jit(_take)/gather | solution.py:637
  130.9 1.5 slice.74
  132.4 1.2 collective-permute-start.4
  133.6 0.6 collective-permute-start.5
  134.1 7.4 %pad_maximum_fusion.filter_hbm = f32[32,256,256]{2,1,0:T(8,128)} fusion(f32[32,256,128]{2,1,0:T(8,128)} %get-tuple-element.38, f32[32,256,128]{2,1,0:T(8,128)} %get-tuple-element.37), kind=kLoop, calls=%fused_computation.1 | loop fusion | flops 2097152 | bytes 16777216 | tf_op jit(solution)/shard_map/concatenate | solution.py:588
  141.6 35.3 %collective-permute-done.5 = s32[3,480]{1,0:T(4,128)S(1)} collective-permute-done((s32[3,480]{1,0:T(4,128)S(1)}, s32[3,480]{1,0:T(4,128)S(1)}, u32[]{:S(2)}, u32[]{:S(2)}) %collective-permute-start.5) | collective-permute-done | bytes 5792 | tf_op jit(solution)/shard_map/ppermute | solution.py:640
  176.9 0.9 copy.48.good_ref
  177.8 1.5 convolution_convert_fusion
  179.3 1.0 copy.45
  180.3 0.5 convolution_convert_fusion.1
  180.8 1.0 copy.44
  181.9 0.8 fusion.6.member_ref
  182.7 5.3 %copy.49.common_ref = f32[32,240,100]{2,1,0:T(8,128)} copy(f32[32,240,100]{1,2,0:T(8,128)} %all-gather.4.cloned.1.call-done) | data formatting | bytes 6144000 | tf_op jit(solution)/shard_map/all_gather | solution.py:628
  187.9 0.0 collective-permute-done.4.got1
  187.9 1.3 copy-done.9
  189.2 54.5 %deconvolve.1 = f32[480,3200]{1,0:T(8,128)} custom-call(f32[32,160,128]{2,1,0:T(8,128)} %all-to-all-done.1.early, f32[32,96,128]{2,1,0:T(8,128)} %copy-done.8, f32[32,144,128]{2,1,0:T(8,128)} %copy-done.7, f32[32,96,128]{2,1,0:T(8,128)} %collective-permute-done.3.got0, f32[32,120,128]{2,1,0:T(8,128)} %copy-done.9, f32[480,1]{1,0:T(8,128)} %copy.42.take_ref, ...), custom_call_target="tpu_custom_call" | custom-call | tf_op jit(solution)/shard_map/deconvolve/pallas_call | solution.py:544
  (50 shorter events, 0.3 us)
Async XLA Ops:
  6.5 83.0 %copy-start = (f32[480]{0:T(512)S(1)}, f32[480]{0:T(512)}, u32[]{:S(2)}) copy-start(f32[480]{0:T(512)} %param.30) | copy-start | bytes 5764
  6.5 5.4 %copy-start.3 = (s32[15360]{0:T(1024)S(1)}, s32[15360]{0:T(1024)}, u32[]{:S(2)}) copy-start(s32[15360]{0:T(1024)} %param.27) | copy-start | bytes 184324
  9.9 57.6 %collective-permute-start.1 = (f32[40,15360]{1,0:T(8,128)}, f32[40,15360]{1,0:T(8,128)}, u32[]{:S(2)}, u32[]{:S(2)}) collective-permute-start(f32[40,15360]{1,0:T(8,128)} %slice.72), channel_id=1, source_target_pairs={{0,32},{32,0},{64,96},{96,64},{1,33},{33,1},{65,97},{97,65},{2,34}... | collective-permute-start | bytes 7372808 | tf_op jit(solution)/shard_map/ppermute | solution.py:607
  14.0 0.6 copy-start.4
  14.7 28.5 %copy-start.5 = (s32[1,15360]{1,0:T(1,128)S(1)}, s32[1,15360]{1,0:T(1,128)}, u32[]{:S(2)}) copy-start(s32[1,15360]{1,0:T(1,128)} %copy-done.4) | copy-start | bytes 184324
  14.7 28.8 %copy-start.10 = (s32[15360]{0:T(1024)S(1)}, s32[15360]{0:T(1024)}, u32[]{:S(2)}) copy-start(s32[15360]{0:T(1024)} %param.25) | copy-start | bytes 184324
  14.7 28.8 %copy-start.14 = (s32[15360]{0:T(1024)S(1)}, s32[15360]{0:T(1024)}, u32[]{:S(2)}) copy-start(s32[15360]{0:T(1024)} %param.26) | copy-start | bytes 184324
  34.0 33.4 %all-to-all-start = ((f32[32,96,128]{2,1,0:T(8,128)}), f32[32,96,128]{2,1,0:T(8,128)S(1)}, u32[]{:S(2)}, u32[]{:S(2)}) async-start(f32[32,96,128]{2,1,0:T(8,128)} %get-tuple-element.21), calls=%async_computation | async-start | bytes 3145728 | tf_op jit(solution)/shard_map/all_to_all | solution.py:619
  43.1 139.6 %all-gather.4.cloned.1.call-start = ((), (), s32[]{:S(2)}) async-start(), calls=%async_computation.3 | async-start | bytes 3514368 | tf_op jit(solution)/shard_map/all_gather | solution.py:628
  43.1 48.7 %collective-permute-start = (s32[15360]{0:T(1024)S(1)}, s32[15360]{0:T(1024)}, u32[]{:S(2)}, u32[]{:S(2)}) collective-permute-start(s32[15360]{0:T(1024)S(1)} %bitcast.52), channel_id=1, source_target_pairs={{0,32},{32,0},{64,96},{96,64},{1,33},{33,1},{65,97},{97,65},{2,34}... | collective-permute-start | bytes 184328 | tf_op jit(solution)/shard_map/ppermute | solution.py:612
  43.5 2.8 %copy-start.2 = (f32[15360,100]{0,1:T(8,128)S(1)}, f32[15360,100]{0,1:T(8,128)}, u32[]{:S(2)}) copy-start(f32[15360,100]{0,1:T(8,128)} %param.24) | copy-start | bytes 18432004
  53.4 14.0 %collective-permute-start.2 = (f32[120,100]{1,0:T(8,128)S(1)}, f32[120,100]{1,0:T(8,128)S(1)}, u32[]{:S(2)}, u32[]{:S(2)}) collective-permute-start(f32[120,100]{1,0:T(8,128)S(1)} %sum_groups.1), channel_id=1, source_target_pairs={{0,32},{32,0},{64,96},{96,64},{1,33},{33,1},{65,97},{97,65},{2,34}... | collective-permute-start | bytes 144008 | tf_op jit(solution)/shard_map/ppermute | solution.py:622
  54.7 13.6 %copy-start.18 = (f32[3200]{0:T(1024)S(1)}, f32[3200]{0:T(1024)}, u32[]{:S(2)}) copy-start(f32[3200]{0:T(1024)} %param.31) | copy-start | bytes 38404
  61.1 17.5 %copy-start.17 = (f32[32,32]{1,0:T(8,128)S(1)}, f32[32,32]{1,0:T(8,128)}, u32[]{:S(2)}) copy-start(f32[32,32]{1,0:T(8,128)} %constant.116.clone) | copy-start | bytes 12292
  61.1 17.6 %copy-start.15 = (s32[15360]{0:T(1024)S(1)}, s32[15360]{0:T(1024)}, u32[]{:S(2)}) copy-start(s32[15360]{0:T(1024)} %param.28) | copy-start | bytes 184324
  61.1 18.9 %copy-start.16 = (f32[32,32]{1,0:T(8,128)S(1)}, f32[32,32]{1,0:T(8,128)}, u32[]{:S(2)}) copy-start(f32[32,32]{1,0:T(8,128)} %constant.115.clone) | copy-start | bytes 12292
  61.2 24.4 %copy-start.11 = (f32[100,200]{1,0:T(8,128)S(1)}, f32[100,200]{1,0:T(8,128)}, u32[]{:S(2)}) copy-start(f32[100,200]{1,0:T(8,128)} %constant.130) | copy-start | bytes 240004
  61.2 24.4 %copy-start.13 = (f32[32,100]{1,0:T(8,128)S(1)}, f32[32,100]{1,0:T(8,128)}, u32[]{:S(2)}) copy-start(f32[32,100]{1,0:T(8,128)} %constant.118.clone) | copy-start | bytes 38404
  67.4 1.2 copy-start.8
  67.4 19.0 %copy-start.12 = (f32[100,200]{1,0:T(8,128)S(1)}, f32[100,200]{1,0:T(8,128)}, u32[]{:S(2)}) copy-start(f32[100,200]{1,0:T(8,128)} %constant.131) | copy-start | bytes 240004
  67.5 20.5 %copy-start.19 = (s32[480]{0:T(512)S(1)}, s32[480]{0:T(512)}, u32[]{:S(2)}) copy-start(s32[480]{0:T(512)} %constant.111.clone) | copy-start | bytes 5764
  68.6 46.7 %all-to-all-start.2 = ((f32[32,144,128]{2,1,0:T(8,128)}), f32[32,144,128]{2,1,0:T(8,128)S(1)}, u32[]{:S(2)}, u32[]{:S(2)}) async-start(f32[32,144,128]{2,1,0:T(8,128)} %lay_late.1), calls=%async_computation.2 | async-start | bytes 4718592 | tf_op jit(solution)/shard_map/all_to_all | solution.py:619
  78.8 36.6 %collective-permute-start.3 = (f32[32,96,128]{2,1,0:T(8,128)}, f32[32,96,128]{2,1,0:T(8,128)}, u32[]{:S(2)}, u32[]{:S(2)}) collective-permute-start(f32[32,96,128]{2,1,0:T(8,128)} %copy-done.8), channel_id=1, source_target_pairs={{0,32},{32,0},{64,96},{96,64},{1,33},{33,1},{65,97},{97,65},{2,34}... | collective-permute-start | bytes 4718600 | tf_op jit(solution)/shard_map/ppermute | solution.py:630
  115.4 15.5 %copy-start.7 = (f32[32,144,128]{2,1,0:T(8,128)}, f32[32,144,128]{2,1,0:T(8,128)S(1)}, u32[]{:S(2)}) copy-start(f32[32,144,128]{2,1,0:T(8,128)S(1)} %all-to-all-done.2.own1) | copy-start | bytes 7077892
  115.4 72.6 %all-to-all-start.1 = ((f32[32,160,128]{2,1,0:T(8,128)}), f32[32,160,128]{2,1,0:T(8,128)}, u32[]{:S(2)}, u32[]{:S(2)}) async-start(f32[32,160,128]{2,1,0:T(8,128)} %merge_rows.1), calls=%async_computation.1 | async-start | bytes 5242880 | tf_op jit(solution)/shard_map/all_to_all | solution.py:619
  123.1 4.4 %copy-start.6 = (s32[128]{0:T(128)S(1)}, s32[128]{0:T(128)}, u32[]{:S(2)}) copy-start(s32[128]{0:T(128)} %param.29) | copy-start | bytes 1540
  132.4 55.6 %collective-permute-start.4 = (f32[32,120,128]{2,1,0:T(8,128)}, f32[32,120,128]{2,1,0:T(8,128)S(1)}, u32[]{:S(2)}, u32[]{:S(2)}) collective-permute-start(f32[32,120,128]{2,1,0:T(8,128)} %slice.74), channel_id=1, source_target_pairs={{0,32},{32,0},{64,96},{96,64},{1,33},{33,1},{65,97},{97,65},{2,34}... | collective-permute-start | bytes 5898248 | tf_op jit(solution)/shard_map/ppermute | solution.py:636
  133.6 43.3 %collective-permute-start.5 = (s32[3,480]{1,0:T(4,128)S(1)}, s32[3,480]{1,0:T(4,128)S(1)}, u32[]{:S(2)}, u32[]{:S(2)}) collective-permute-start(s32[3,480]{1,0:T(4,128)S(1)} %pad_add_fusion), channel_id=1, source_target_pairs={{0,32},{32,0},{64,96},{96,64},{1,33},{33,1},{65,97},{97,65},{2,34}... | collective-permute-start | bytes 17288 | tf_op jit(solution)/shard_map/ppermute | solution.py:640
  134.1 46.2 %copy-start.20 = (bf16[512,480]{1,0:T(8,128)(2,1)S(1)}, bf16[512,480]{1,0:T(8,128)(2,1)}, u32[]{:S(2)}) copy-start(bf16[512,480]{1,0:T(8,128)(2,1)} %constant.112.clone) | copy-start | bytes 1474564
  187.9 1.3 copy-start.9
  189.2 54.5 %copy-start.1 = (f32[480]{0:T(512)S(1)}, f32[480]{0:T(512)}, u32[]{:S(2)}) copy-start(f32[480]{0:T(512)} %param.30) | copy-start | bytes 5764
Sparse Core Ops, SparseCore 0:
  68.4 79.2 all-gather.3

commit v6 on v5

--- a/solution.py
+++ b/solution.py
@@ -24,6 +24,7 @@
 LATE_BASE = (0, 192)
 BLOCK = 256
 WIDE = 512
+OUT_PART = 640
 SENT = (96, 120)
 
 highest = lax.Precision.HIGHEST
@@ -288,7 +289,9 @@
         high, low = split(raw_ref[:, part])
         return total + (across(member, high) + across(member, low))
 
-    out_ref[...] = lax.fori_loop(0, raw_ref.shape[1] // WIDE, some, jnp.zeros(out_ref.shape, jnp.float32))
+    zero = jnp.zeros((group_count, SLAB), jnp.float32)
+    out_ref[...] = jnp.zeros_like(out_ref)
+    out_ref[:, 0:SLAB] = lax.fori_loop(0, raw_ref.shape[1] // WIDE, some, zero)
 
 
 def sum_groups(raw_turned, local_group, good_mask):
@@ -297,7 +300,7 @@
         group_kernel,
         in_specs=whole(3),
         out_specs=whole(1)[0],
-        out_shape=jax.ShapeDtypeStruct((group_count, SLAB), jnp.float32),
+        out_shape=jax.ShapeDtypeStruct((group_count, PART), jnp.float32),
         compiler_params=roomy(24),
         name="sum_groups",
         cost_estimate=light,
@@ -392,46 +395,40 @@
             store(k + 4 * big, value)
 
 
-def tail_kernel(
-    early,
-    own0,
-    own1,
-    got0,
-    got1,
-    take_ref,
-    good_ref,
-    common_ref,
-    member_ref,
-    high_ref,
-    low_ref,
-    filter_hbm,
-    twist_ref,
-    tick_high_ref,
-    tick_low_ref,
-    untick_high_ref,
-    untick_low_ref,
-    back_high_ref,
-    back_low_ref,
-    out_ref,
-    rows_ref,
-    plane_ref,
-    both_ref,
-    covar_ref,
-    power_ref,
-    middle_ref,
-    filter_ref,
-    filter_done,
-):
-    fetch = pltpu.make_async_copy(filter_hbm, filter_ref, filter_done)
-    fetch.start()
-    both_ref[...] = jnp.zeros_like(both_ref)
+def tail_kernel(*refs):
+    sources, refs = refs[:6], refs[6:]
+    take_ref, good_ref, member_ref, high_ref, low_ref, real_hbm, imag_hbm, twist_ref = refs[:8]
+    tick_high_ref, tick_low_ref, untick_high_ref, untick_low_ref, back_high_ref, back_low_ref = refs[8:14]
+    out_hbm, held, refs = refs[14], refs[15:21], refs[21:]
+    rows_ref, plane_ref, covar_ref, power_ref, middle_ref, real_ref, imag_ref, out_ref = refs[:8]
+    fetched, filter_done, out_done = refs[8:]
+    early, own0, own1, got0, got1, common_ref = held
+    quarters = []
+    for quarter in range(4):
+        part = pl.ds(quarter * SLABS // 4, SLABS // 4)
+        quarters.append(
+            [
+                pltpu.make_async_copy(source.at[part], target.at[part], fetched.at[index, quarter])
+                for index, (source, target) in enumerate(zip(sources, held))
+            ]
+        )
+    for copies in quarters:
+        for copy in copies:
+            copy.start()
+    filter_copies = [
+        pltpu.make_async_copy(real_hbm, real_ref, filter_done.at[0]),
+        pltpu.make_async_copy(imag_hbm, imag_ref, filter_done.at[1]),
+    ]
+    for copy in filter_copies:
+        copy.start()
     covar_ref[...] = jnp.zeros_like(covar_ref)
     power_ref[...] = jnp.zeros_like(power_ref)
 
-    def spread_common(pair):
-        for slab in range(2):
-            both_ref[:, slab * PART : slab * PART + SLAB] = common_ref[2 * pair + slab]
-        high, low = split(both_ref[...])
+    def both_commons(pair):
+        return jnp.concatenate([common_ref[2 * pair], common_ref[2 * pair + 1]], axis=1)
+
+    def spread_common(commons):
+        high, low = split(commons)
         return dot(member_ref[...], high) + dot(member_ref[...], low)
 
     def spread_power(power):
@@ -460,19 +457,22 @@
                     if sent < LATE_ROWS[which]:
                         rest = slice(at + sent, at + LATE_ROWS[which])
                         rows_ref[pair, rest, lanes] = own[slab, sent : LATE_ROWS[which], part]
-        spread = spread_common(pair)
-        covar_ref[...] += rows_ref[pair] * spread
-        power_ref[...] += both_ref[...] * both_ref[...]
+        commons = both_commons(pair)
+        covar_ref[...] += rows_ref[pair] * spread_common(commons)
+        power_ref[...] += commons * commons
         return carry
 
-    lax.fori_loop(0, SLABS // 2, assemble, 0)
+    for quarter in range(4):
+        for copy in quarters[quarter]:
+            copy.wait()
+        lax.fori_loop(quarter * SLABS // 8, (quarter + 1) * SLABS // 8, assemble, 0)
     covar = jnp.sum(covar_ref[...], axis=1, keepdims=True) / TICKS
     power = jnp.sum(power_ref[...], axis=1, keepdims=True) / TICKS
     power = spread_power(jnp.broadcast_to(power, (power.shape[0], PART)))[:, 0:1]
     weight = covar / (power + epsilon_power)
 
     def to_wires(pair, carry):
-        cleaned = good_ref[...] * (rows_ref[pair] - weight * spread_common(pair))
+        cleaned = good_ref[...] * (rows_ref[pair] - weight * spread_common(both_commons(pair)))
         row_high, row_low = split(cleaned)
         result = three_dot(high_ref[...], low_ref[...], row_high, row_low)
         for slab in range(2):
@@ -512,7 +512,7 @@
         data_high, data_low = split(jnp.concatenate([plane_ref[item, 0], plane_ref[item, 1]], axis=1))
         spectrum = three_dot(data_high, data_low, tick_high_ref[...], tick_low_ref[...])
         real, imag = spectrum[:, :PART], spectrum[:, PART:]
-        filter_real, filter_imag = filter_ref[item, :, :PART], filter_ref[item, :, PART:]
+        filter_real, filter_imag = real_ref[item], imag_ref[item]
         mixed = jnp.concatenate(
             [real * filter_real - imag * filter_imag, real * filter_imag + imag * filter_real], axis=1
         )
@@ -522,9 +522,11 @@
         plane_ref[item, 1] = result[:, PART:]
         return carry
 
-    fetch.wait()
+    for copy in filter_copies:
+        copy.wait()
     lax.fori_loop(0, SLABS, filtered, 0, unroll=8)
     lax.fori_loop(0, HALF // 8, functools.partial(slabs_over, sign=1), 0)
+    out_copies = []
     for pair in range(SLABS // 2):
         both = jnp.concatenate(
             [plane_ref[2 * pair + slab].reshape(2 * HALF, PART) for slab in range(2)], axis=1
@@ -534,27 +536,39 @@
         for slab in range(2):
             at = (2 * pair + slab) * SLAB
             out_ref[:, at : at + SLAB] = result[:, slab * PART : slab * PART + SLAB]
+        while len(out_copies) < 5 and (len(out_copies) + 1) * OUT_PART <= (pair + 1) * 2 * SLAB:
+            part = pl.ds(len(out_copies) * OUT_PART, OUT_PART)
+            out_copies.append(pltpu.make_async_copy(out_ref.at[:, part], out_hbm.at[:, part], out_done.at[len(out_copies)]))
+            out_copies[-1].start()
+    for copy in out_copies:
+        copy.wait()
 
 
 def tail(early, own, got, take, good, commons, member, high, low, filters):
     back_high, back_low = two_halves(wire_tables()[1])
     tick, untick, twist = tick_tables()
     tables = (twist, *two_halves(tick), *two_halves(untick), back_high, back_low)
-    operands = (early, *own, *got, take, good, commons, member, high, low, filters, *tables)
+    moved = (early, *own, *got, commons)
+    operands = (*moved, take, good, member, high, low, *filters, *tables)
+    far = [pl.BlockSpec(memory_space=pltpu.HBM)]
     return pl.pallas_call(
         tail_kernel,
-        in_specs=whole(11) + [pl.BlockSpec(memory_space=pl.ANY)] + whole(len(operands) - 12),
-        out_specs=whole(1)[0],
+        in_specs=far * 6 + whole(5) + far * 2 + whole(len(tables)),
+        out_specs=far[0],
         out_shape=jax.ShapeDtypeStruct((WIRES, TICKS), jnp.float32),
-        scratch_shapes=[
+        scratch_shapes=[pltpu.VMEM(value.shape, jnp.float32) for value in moved]
+        + [
             pltpu.VMEM((SLABS // 2, WIRES, HALF), jnp.float32),
             pltpu.VMEM((SLABS, 2, HALF, PART), jnp.float32),
-            pltpu.VMEM((commons.shape[1], HALF), jnp.float32),
             pltpu.VMEM((WIRES, HALF), jnp.float32),
             pltpu.VMEM((commons.shape[1], HALF), jnp.float32),
             pltpu.VMEM((SLABS, 2, 8, PART), jnp.float32),
-            pltpu.VMEM((SLABS, HALF, HALF), jnp.float32),
-            pltpu.SemaphoreType.DMA,
+            pltpu.VMEM((SLABS, HALF, PART), jnp.float32),
+            pltpu.VMEM((SLABS, HALF, PART), jnp.float32),
+            pltpu.VMEM((WIRES, TICKS), jnp.float32),
+            pltpu.SemaphoreType.DMA((6, 4)),
+            pltpu.SemaphoreType.DMA((2,)),
+            pltpu.SemaphoreType.DMA((5,)),
         ],
         compiler_params=roomy(60),
         name="deconvolve",
@@ -585,7 +599,7 @@
     real = wire_resp[0] * time_real - wire_resp[1] * time_imag
     imag = wire_resp[0] * time_imag + wire_resp[1] * time_real
     denominator = real * real + imag * imag + regular_term
-    return jnp.concatenate([real / denominator, -imag / denominator], axis=2)
+    return real / denominator, -imag / denominator
 
 
 def picked_tables(wires):
@@ -622,7 +636,7 @@
     common_got = lax.ppermute(common, "apa", swap)
     facts = jnp.stack([chan_wire >> 5, chan_wire & 31, local_group, bad, chan_plane - pair_base])
     facts = pick_facts(later_place - tick_index * WIRES, facts.astype(jnp.float32)).astype(jnp.int32)
-    own0, late1, early_got, common_got = lax.optimization_barrier((own0, late1, early_got, common_got))
+    own0, late1, early_got, common_got, facts = lax.optimization_barrier((own0, late1, early_got, common_got, facts))
     first = jnp.where(parity == 0, common, common_got)
     second = jnp.where(parity == 0, common_got, common)
     commons = lax.all_gather(jnp.concatenate([first, second], axis=0), "tick")
@@ -631,16 +645,20 @@
     take = jnp.asarray(row_order()) < cross_count
     row_take = take.astype(jnp.float32)[:, None]
     early = merge_rows(place_got, early_got, rows, row_take)
-    early, got0, facts = lax.optimization_barrier((early, got0, facts))
+    facts_got = lax.ppermute(facts, "apa", swap)
+    early, got0, facts, facts_got, late_sent = lax.optimization_barrier(
+        (early, got0, facts, facts_got, own1[:, : SENT[1]])
+    )
+    got1 = lax.ppermute(late_sent, "apa", swap)
     early = over_ticks(early)
-    got1 = lax.ppermute(own1[:, : SENT[1]], "apa", swap)
+    row_side = jnp.where(take, 1 - parity, parity)
+    facts = jnp.where(take[None, :], facts_got, facts)
     row_offset = jnp.take(plane_offset, facts[4] + pair_base)
     row_wire = (facts[0] * 32 + facts[1] + row_offset) % WIRES
-    facts = jnp.stack([row_wire, facts[2] + parity * group_count, facts[3]])
-    facts = jnp.where(take[None, :], lax.ppermute(facts, "apa", swap), facts)
-    row_good = 1.0 - facts[2].astype(jnp.float32)[:, None]
-    member = (facts[1][:, None] == jnp.arange(2 * group_count, dtype=jnp.int32)[None, :]).astype(jnp.bfloat16)
-    high, low = picked_tables(facts[0])
+    row_group = facts[2] + row_side * group_count
+    row_good = 1.0 - facts[3].astype(jnp.float32)[:, None]
+    member = (row_group[:, None] == jnp.arange(2 * group_count, dtype=jnp.int32)[None, :]).astype(jnp.bfloat16)
+    high, low = picked_tables(row_wire)
     filters = make_filter(wire_kernel, time_kernel)
     return tail(early, (own0, own1), (got0, got1), row_take, row_good, commons, member, high, low, filters)[None]
 

time: 251 us -> 229 us (0.912)
  waiting for transfers between devices: 41.6 us -> 34.1 us
  local copies, waits for them, and re-layouts: 24.2 us -> 18.8 us
  other arithmetic: 13.5 us -> 9.14 us
  Pallas kernels: 118 us -> 114 us
    concatenate x1, other arithmetic: 7.43 us -> 0.66 us  [shards(): commons = lax.all_gather(jnp.concatenate([first, second], axis=0), 'tick')]
    ppermute x1, waiting for transfers between devices: 6.23 us -> 0.2 us  [shards(): common_got = lax.ppermute(common, 'apa', swap)]
    all_gather x1 -> x0, local copies, waits for them, and re-layouts: 5.25 us -> none  [shards(): commons = lax.all_gather(jnp.concatenate([first, second], axis=0), 'tick')]
    pallas_call x1, Pallas kernels: 54.5 us -> 51 us  [tail(): pl.pallas_call(tail_kernel, in_specs=far * 6 + whole(5) + far * 2 + whole...]
    unnamed x43 -> x40, local copies, waits for them, and re-layouts: 5.75 us -> 4.8 us
  transfers between devices with their start and end apart: 10 -> 10, of which waited for: 2 -> 3; matrix products, arithmetic and copies ran while one was open for 14% -> 10% of each run, Pallas kernels for 25% -> 28%
where the time goes in v6:
time: 229 us; the launch traced here: 228 us
  Pallas kernels  114 us (50%)
  waiting for transfers between devices  34.1 us (15%)
  starting transfers between devices  33.1 us (14%)
  local copies, waits for them, and re-layouts  18.8 us (8%)
  between operations  13.8 us (6%)
  other arithmetic  9.14 us (4%)
  matrix products  5.12 us (2%)
    pallas_call x1, Pallas kernels, tail(): pl.pallas_call(tail_kernel, in_specs=far * 6 + whole(5) + far * 2 + whole...  51 us
    ppermute x1, waiting for transfers between devices, shards(): got1 = lax.ppermute(late_sent, 'apa', swap)  30.7 us
    all_to_all x3, starting transfers between devices, over_ticks(): lax.all_to_all(value, 'tick', split_axis=0, concat_axis=0, tiled=True)  27.2 us
    pallas_call x1, Pallas kernels, merge_rows(): pl.pallas_call(merge_kernel, in_specs=[pl.BlockSpec(memory_space=pltpu.SM...  23.5 us
    pallas_call x1, Pallas kernels, pack_rows(): pl.pallas_call(pack_kernel, in_specs=[pl.BlockSpec(memory_space=pltpu.SME...  19.4 us
    pallas_call x1, Pallas kernels, sum_groups(): pl.pallas_call(group_kernel, in_specs=whole(3), out_specs=whole(1)[0], ou...  7.08 us
    pallas_call x1, Pallas kernels, lay_late(): pl.pallas_call(functools.partial(fetched_late_kernel, which), in_specs=[p...  6.3 us
    unnamed x40, local copies, waits for them, and re-layouts  4.8 us
  transfers between devices with their start and end apart: 10, of which 3 were waited for; matrix products, arithmetic and copies ran while one was open for 10% of the time, Pallas kernels for 28%

profile of v6, /device:TPU:1, one launch (start us, length us, event | category | flops | bytes accessed | tf_op | source)
XLA Modules:
  0.0 228.2 jit_solution(13938012546479088335)
XLA Ops:
  6.5 3.3 %slice.60 = f32[40,15360]{1,0:T(8,128)} slice(f32[100,15360]{1,0:T(8,128)} %bitcast.43), slice={[0:40], [0:15360]} | slice | bytes 4915200 | tf_op jit(solution)/shard_map/slice | solution.py:621
  9.9 2.0 collective-permute-start.1
  11.9 2.1 rank_rows.1
  14.0 0.6 copy-done.3
  14.7 19.4 %pack_rows.1 = (f32[32,96,128]{2,1,0:T(8,128)}, f32[15360,128]{1,0:T(8,128)}) custom-call(s32[15360]{0:T(1024)} %bitcast.50, f32[100,15360]{1,0:T(8,128)} %bitcast.44), custom_call_target="tpu_custom_call" | custom-call | tf_op jit(solution)/shard_map/pack_rows/pallas_call | solution.py:200
  34.0 9.1 %all-to-all-start = ((f32[32,96,128]{2,1,0:T(8,128)}), f32[32,96,128]{2,1,0:T(8,128)S(1)}, u32[]{:S(2)}, u32[]{:S(2)}) async-start(f32[32,96,128]{2,1,0:T(8,128)} %get-tuple-element.24), calls=%async_computation | async-start | bytes 3145728 | tf_op jit(solution)/shard_map/all_to_all | solution.py:633
  43.1 0.0 copy-start.15
  43.1 0.0 all-gather.3.cloned.1.call-start
  43.2 0.0 copy-start.1
  43.2 2.8 %copy-done.1 = f32[15360,100]{0,1:T(8,128)S(1)} copy-done((f32[15360,100]{0,1:T(8,128)S(1)}, f32[15360,100]{0,1:T(8,128)}, u32[]{:S(2)}) %copy-start.1) | copy-done | bytes 6144024
  46.0 7.1 %sum_groups.1 = f32[120,128]{1,0:T(8,128)S(1)} custom-call(f32[100,15360]{1,0:T(8,128)S(1)} %bitcast.45, s32[1,15360]{1,0:T(1,128)S(1)} %bitcast.46, f32[1,15360]{1,0:T(1,128)S(1)} %bitcast.53), custom_call_target="tpu_custom_call" | custom-call | flops 1 | bytes 1 | tf_op jit(solution)/shard_map/sum_groups/pallas_call | solution.py:299
  53.1 0.3 collective-permute-start.2
  53.5 0.5 stack.20
  54.1 4.7 %pick_facts.1 = f32[80,32]{1,0:T(8,128)S(1)} custom-call(s32[1,15360]{1,0:T(1,128)S(1)} %bitcast.49, f32[5,15360]{1,0:T(8,128)S(1)} %convert_element_type.38.facts_ref), custom_call_target="tpu_custom_call" | custom-call | flops 1 | bytes 1 | tf_op jit(solution)/shard_map/pick_facts/pallas_call | solution.py:327
  58.8 0.1 reshape.63
  58.9 0.6 slice_convert_fusion
  59.5 6.3 %lay_late.1 = f32[32,144,128]{2,1,0:T(8,128)} custom-call(f32[15360,128]{1,0:T(8,128)} %get-tuple-element.25.rows_hbm.own_hbm), custom_call_target="tpu_custom_call" | custom-call | flops 1 | bytes 1 | tf_op jit(solution)/shard_map/lay_late/pallas_call | solution.py:232
  65.8 0.0 copy-start.16
  65.8 0.0 copy-start.12
  65.8 0.0 copy-start.13
  65.9 0.0 copy-start.9
  65.9 0.0 copy-start.17
  65.9 0.2 collective-permute-done.2
  66.1 0.0 all-to-all-done.refs_1_
  66.1 0.0 collective-permute-done.1.raw_ref
  66.1 1.2 broadcast_select_fusion.1
  67.3 0.7 pad_maximum_fusion
  68.0 0.0 all-gather.3.cloned.1.call-update
  68.0 9.8 %all-to-all-start.1 = ((f32[32,144,128]{2,1,0:T(8,128)}), f32[32,144,128]{2,1,0:T(8,128)S(1)}, u32[]{:S(2)}, u32[]{:S(2)}) async-start(f32[32,144,128]{2,1,0:T(8,128)} %lay_late.1), calls=%async_computation.1 | async-start | bytes 4718592 | tf_op jit(solution)/shard_map/all_to_all | solution.py:633
  77.8 1.3 collective-permute-start
  79.1 0.8 reshape.64
  79.9 0.3 collective-permute-start.3
  80.2 0.8 fusion.23
  81.1 0.0 copy-done.16
  81.1 0.1 fusion.22
  81.2 0.0 copy-done.12
  81.3 0.0 copy-done.13
  81.3 1.1 fusion.12
  82.4 1.1 convolution_add_fusion
  83.5 0.1 reshape.65
  83.6 0.5 slice.45
  84.1 1.0 fusion.21
  85.1 0.6 broadcast_compare_fusion
  85.8 1.3 collective-permute-start.4
  87.1 0.8 copy.34.take_ref.refs_6_
  87.9 0.0 collective-permute-done.place_ref
  87.9 23.5 %merge_rows.1 = f32[32,160,128]{2,1,0:T(8,128)} custom-call(s32[15360]{0:T(1024)} %collective-permute-done.place_ref, f32[40,15360]{1,0:T(8,128)} %collective-permute-done.1.raw_ref, f32[15360,128]{1,0:T(8,128)} %get-tuple-element.25.rows_hbm.own_hbm, f32[480,1]{1,0:T(8,128)} %copy.34.take_ref.refs_6_), custom_call_target="tpu_custom_call" | custom-call | tf_op jit(solution)/shard_map/merge_rows/pallas_call | solution.py:265
  111.4 0.0 all-to-all-done.1.refs_2_
  111.4 1.5 slice.62
  112.9 3.2 %collective-permute-done.4 = s32[5,480]{1,0:T(8,128)S(1)} collective-permute-done((s32[5,480]{1,0:T(8,128)}, s32[5,480]{1,0:T(8,128)S(1)}, u32[]{:S(2)}, u32[]{:S(2)}) %collective-permute-start.4) | collective-permute-done | bytes 9632 | tf_op jit(solution)/shard_map/ppermute | solution.py:648
  116.1 8.3 %all-to-all-start.2 = ((f32[32,160,128]{2,1,0:T(8,128)}), f32[32,160,128]{2,1,0:T(8,128)}, u32[]{:S(2)}, u32[]{:S(2)}) async-start(f32[32,160,128]{2,1,0:T(8,128)} %merge_rows.1), calls=%async_computation.2 | async-start | bytes 5242880 | tf_op jit(solution)/shard_map/all_to_all | solution.py:633
  124.4 0.6 collective-permute-start.5
  125.1 4.4 %negate_divide_fusion = (f32[32,256,128]{2,1,0:T(8,128)}, f32[32,256,128]{2,1,0:T(8,128)}) fusion(f32[32,128]{1,0:T(8,128)S(1)} %get-tuple-element.46, f32[256]{0:T(256)S(1)} %get-tuple-element.50, f32[32,128]{1,0:T(8,128)S(1)} %get-tuple-element.45, f32[256]{0:T(256)S(1)} %get-tuple-element.49), kind=kLoop, calls=%fused_computation.1 | loop fusion | flops 13631488 | bytes 8423424 | tf_op jit(solution)/shard_map/div | solution.py:602
  129.5 0.8 copy.39.refs_7_
  130.4 3.3 %gather_fusion = s32[480]{0:T(512)S(1)} fusion(s32[128]{0:T(128)S(1)} %copy-done.5, s32[1024]{0:T(1024)S(1)} %pad_clamp_fusion), kind=kCustom, calls=%fused_computation | custom fusion | bytes 5760 | tf_op jit(solution)/shard_map/jit(_take)/gather | solution.py:656
  133.8 0.5 convolution_convert_fusion
  134.3 1.0 copy.36
  135.3 0.5 convolution_convert_fusion.1
  135.8 1.0 copy.35
  136.8 0.6 multiply_add_fusion.1
  137.5 0.8 fusion.6.refs_8_
  138.3 30.7 %collective-permute-done.5.refs_4_ = f32[32,120,128]{2,1,0:T(8,128)S(1)} collective-permute-done((f32[32,120,128]{2,1,0:T(8,128)}, f32[32,120,128]{2,1,0:T(8,128)S(1)}, u32[]{:S(2)}, u32[]{:S(2)}) %collective-permute-start.5) | collective-permute-done | bytes 1966112 | tf_op jit(solution)/shard_map/ppermute | solution.py:652
  169.0 1.3 copy-done.8
  170.3 51.0 %deconvolve.1 = f32[480,3200]{1,0:T(8,128)} custom-call(f32[32,160,128]{2,1,0:T(8,128)} %all-to-all-done.2.refs_0_, f32[32,96,128]{2,1,0:T(8,128)} %copy-done.7, f32[32,144,128]{2,1,0:T(8,128)} %copy-done.6, f32[32,96,128]{2,1,0:T(8,128)} %collective-permute-done.3.refs_3_, f32[32,120,128]{2,1,0:T(8,128)} %copy-done.8, f32[32,240,128]{2,1,0:T(8,128)} %bitcast.54, ...), custom_call_target="tpu_custom_call" | custom-call | tf_op jit(solution)/shard_map/deconvolve/pallas_call | solution.py:554
  (44 shorter events, 0.2 us)
Async XLA Ops:
  6.5 77.6 %copy-start = (f32[480]{0:T(512)S(1)}, f32[480]{0:T(512)}, u32[]{:S(2)}) copy-start(f32[480]{0:T(512)} %param.30) | copy-start | bytes 5764
  6.5 5.4 %copy-start.2 = (s32[15360]{0:T(1024)S(1)}, s32[15360]{0:T(1024)}, u32[]{:S(2)}) copy-start(s32[15360]{0:T(1024)} %param.27) | copy-start | bytes 184324
  9.9 56.2 %collective-permute-start.1 = (f32[40,15360]{1,0:T(8,128)}, f32[40,15360]{1,0:T(8,128)}, u32[]{:S(2)}, u32[]{:S(2)}) collective-permute-start(f32[40,15360]{1,0:T(8,128)} %slice.60), channel_id=1, source_target_pairs={{0,32},{32,0},{64,96},{96,64},{1,33},{33,1},{65,97},{97,65},{2,34}... | collective-permute-start | bytes 7372808 | tf_op jit(solution)/shard_map/ppermute | solution.py:621
  14.0 0.6 copy-start.3
  14.7 28.5 %copy-start.10 = (s32[15360]{0:T(1024)S(1)}, s32[15360]{0:T(1024)}, u32[]{:S(2)}) copy-start(s32[15360]{0:T(1024)} %param.25) | copy-start | bytes 184324
  14.7 28.5 %copy-start.14 = (s32[15360]{0:T(1024)S(1)}, s32[15360]{0:T(1024)}, u32[]{:S(2)}) copy-start(s32[15360]{0:T(1024)} %param.26) | copy-start | bytes 184324
  34.0 32.1 %all-to-all-start = ((f32[32,96,128]{2,1,0:T(8,128)}), f32[32,96,128]{2,1,0:T(8,128)S(1)}, u32[]{:S(2)}, u32[]{:S(2)}) async-start(f32[32,96,128]{2,1,0:T(8,128)} %get-tuple-element.24), calls=%async_computation | async-start | bytes 3145728 | tf_op jit(solution)/shard_map/all_to_all | solution.py:633
  43.1 10.4 %copy-start.15 = (s32[15360]{0:T(1024)S(1)}, s32[15360]{0:T(1024)}, u32[]{:S(2)}) copy-start(s32[15360]{0:T(1024)} %param.28) | copy-start | bytes 184324
  43.1 125.9 %all-gather.3.cloned.1.call-start = ((), (), s32[]{:S(2)}) async-start(), calls=%async_computation.3 | async-start | bytes 4055040 | tf_op jit(solution)/shard_map/all_gather | solution.py:642
  43.2 2.8 %copy-start.1 = (f32[15360,100]{0,1:T(8,128)S(1)}, f32[15360,100]{0,1:T(8,128)}, u32[]{:S(2)}) copy-start(f32[15360,100]{0,1:T(8,128)} %param.24) | copy-start | bytes 18432004
  46.0 8.0 %copy-start.4 = (s32[1,15360]{1,0:T(1,128)S(1)}, s32[1,15360]{1,0:T(1,128)}, u32[]{:S(2)}) copy-start(s32[1,15360]{1,0:T(1,128)} %copy-done.3) | copy-start | bytes 184324
  53.1 13.0 %collective-permute-start.2 = (f32[120,128]{1,0:T(8,128)S(1)}, f32[120,128]{1,0:T(8,128)}, u32[]{:S(2)}, u32[]{:S(2)}) collective-permute-start(f32[120,128]{1,0:T(8,128)S(1)} %sum_groups.1), channel_id=1, source_target_pairs={{0,32},{32,0},{64,96},{96,64},{1,33},{33,1},{65,97},{97,65},{2,34}... | collective-permute-start | bytes 184328 | tf_op jit(solution)/shard_map/ppermute | solution.py:636
  65.8 15.3 %copy-start.16 = (f32[32,32]{1,0:T(8,128)S(1)}, f32[32,32]{1,0:T(8,128)}, u32[]{:S(2)}) copy-start(f32[32,32]{1,0:T(8,128)} %constant.116.clone) | copy-start | bytes 12292
  65.8 15.4 %copy-start.12 = (f32[32,100]{1,0:T(8,128)S(1)}, f32[32,100]{1,0:T(8,128)}, u32[]{:S(2)}) copy-start(f32[32,100]{1,0:T(8,128)} %constant.119.clone) | copy-start | bytes 38404
  65.8 15.4 %copy-start.13 = (f32[32,100]{1,0:T(8,128)S(1)}, f32[32,100]{1,0:T(8,128)}, u32[]{:S(2)}) copy-start(f32[32,100]{1,0:T(8,128)} %constant.118.clone) | copy-start | bytes 38404
  65.9 18.2 %copy-start.9 = (f32[512,480]{1,0:T(8,128)S(1)}, f32[512,480]{1,0:T(8,128)}, u32[]{:S(2)}) copy-start(f32[512,480]{1,0:T(8,128)} %constant.115.clone) | copy-start | bytes 2949124
  65.9 19.2 %copy-start.17 = (s32[480]{0:T(512)S(1)}, s32[480]{0:T(512)}, u32[]{:S(2)}) copy-start(s32[480]{0:T(512)} %constant.112.clone) | copy-start | bytes 5764
  66.1 1.9 copy-start.7
  68.0 43.4 %all-to-all-start.1 = ((f32[32,144,128]{2,1,0:T(8,128)}), f32[32,144,128]{2,1,0:T(8,128)S(1)}, u32[]{:S(2)}, u32[]{:S(2)}) async-start(f32[32,144,128]{2,1,0:T(8,128)} %lay_late.1), calls=%async_computation.1 | async-start | bytes 4718592 | tf_op jit(solution)/shard_map/all_to_all | solution.py:633
  77.8 10.1 %collective-permute-start = (s32[15360]{0:T(1024)S(1)}, s32[15360]{0:T(1024)}, u32[]{:S(2)}, u32[]{:S(2)}) collective-permute-start(s32[15360]{0:T(1024)S(1)} %bitcast.52), channel_id=1, source_target_pairs={{0,32},{32,0},{64,96},{96,64},{1,33},{33,1},{65,97},{97,65},{2,34}... | collective-permute-start | bytes 184328 | tf_op jit(solution)/shard_map/ppermute | solution.py:626
  79.9 36.2 %collective-permute-start.3 = (f32[32,96,128]{2,1,0:T(8,128)}, f32[32,96,128]{2,1,0:T(8,128)}, u32[]{:S(2)}, u32[]{:S(2)}) collective-permute-start(f32[32,96,128]{2,1,0:T(8,128)} %copy-done.7), channel_id=1, source_target_pairs={{0,32},{32,0},{64,96},{96,64},{1,33},{33,1},{65,97},{97,65},{2,34}... | collective-permute-start | bytes 4718600 | tf_op jit(solution)/shard_map/ppermute | solution.py:644
  85.8 30.3 %collective-permute-start.4 = (s32[5,480]{1,0:T(8,128)}, s32[5,480]{1,0:T(8,128)S(1)}, u32[]{:S(2)}, u32[]{:S(2)}) collective-permute-start(s32[5,480]{1,0:T(8,128)} %slice_convert_fusion), channel_id=1, source_target_pairs={{0,32},{32,0},{64,96},{96,64},{1,33},{33,1},{65,97},{97,65},{2,34}... | collective-permute-start | bytes 28808 | tf_op jit(solution)/shard_map/ppermute | solution.py:648
  111.4 4.7 %copy-start.6 = (f32[32,144,128]{2,1,0:T(8,128)}, f32[32,144,128]{2,1,0:T(8,128)S(1)}, u32[]{:S(2)}) copy-start(f32[32,144,128]{2,1,0:T(8,128)S(1)} %all-to-all-done.1.refs_2_) | copy-start | bytes 7077892
  116.1 52.9 %all-to-all-start.2 = ((f32[32,160,128]{2,1,0:T(8,128)}), f32[32,160,128]{2,1,0:T(8,128)}, u32[]{:S(2)}, u32[]{:S(2)}) async-start(f32[32,160,128]{2,1,0:T(8,128)} %merge_rows.1), calls=%async_computation.2 | async-start | bytes 5242880 | tf_op jit(solution)/shard_map/all_to_all | solution.py:633
  124.4 44.6 %collective-permute-start.5 = (f32[32,120,128]{2,1,0:T(8,128)}, f32[32,120,128]{2,1,0:T(8,128)S(1)}, u32[]{:S(2)}, u32[]{:S(2)}) collective-permute-start(f32[32,120,128]{2,1,0:T(8,128)} %slice.62), channel_id=1, source_target_pairs={{0,32},{32,0},{64,96},{96,64},{1,33},{33,1},{65,97},{97,65},{2,34}... | collective-permute-start | bytes 5898248 | tf_op jit(solution)/shard_map/ppermute | solution.py:652
  125.1 4.4 %copy-start.11 = (s32[5,480]{1,0:T(8,128)S(1)}, s32[5,480]{1,0:T(8,128)}, u32[]{:S(2)}) copy-start(s32[5,480]{1,0:T(8,128)} %slice_convert_fusion) | copy-start | bytes 28804
  125.1 5.3 %copy-start.5 = (s32[128]{0:T(128)S(1)}, s32[128]{0:T(128)}, u32[]{:S(2)}) copy-start(s32[128]{0:T(128)} %param.29) | copy-start | bytes 1540
  125.1 8.7 %copy-start.19 = (bf16[512,480]{1,0:T(8,128)(2,1)S(1)}, bf16[512,480]{1,0:T(8,128)(2,1)}, u32[]{:S(2)}) copy-start(bf16[512,480]{1,0:T(8,128)(2,1)} %constant.114.clone) | copy-start | bytes 1474564
  129.5 5.8 %copy-start.18 = (bf16[512,480]{1,0:T(8,128)(2,1)S(1)}, bf16[512,480]{1,0:T(8,128)(2,1)}, u32[]{:S(2)}) copy-start(bf16[512,480]{1,0:T(8,128)(2,1)} %constant.113.clone) | copy-start | bytes 1474564
  169.0 1.3 copy-start.8
Sparse Core Ops, SparseCore 0:
  68.1 71.2 all-gather.2

commit v7 on v6

--- a/solution.py
+++ b/solution.py
@@ -94,7 +94,9 @@
     return np.where(row < 192, row, late).astype(np.int32)
 
 
-def rank_kernel(plane_ref, base_ref, cross_ref, place_ref, count_ref):
+def rank_kernel(plane_ref, base_ref, cross_ref, raw_hbm, place_ref, count_ref, early_hbm, early_done):
+    send = pltpu.make_async_copy(raw_hbm.at[pl.ds(0, EARLY)], early_hbm, early_done)
+    send.start()
     tri_row = lax.broadcasted_iota(jnp.int32, (BLOCK, BLOCK), 0)
     tri_col = lax.broadcasted_iota(jnp.int32, (BLOCK, BLOCK), 1)
     earlier = (tri_row < tri_col).astype(jnp.float32).astype(jnp.bfloat16)
@@ -118,24 +120,27 @@
         row = jnp.where(order < 192, order, jnp.where(order < 420, near_row, far_row))
         place_ref[:, part] = (local[:, part] % SLABS) * WIRES + row
     count_ref[...] = jnp.broadcast_to(cross_count.astype(jnp.int32), count_ref.shape)
-
-
-def rank_rows(chan_plane, pair_base, cross_side):
+    send.wait()
+
+
+def rank_rows(chan_plane, pair_base, cross_side, raw_turned):
     chan_count = chan_plane.shape[0]
     scalar = pl.BlockSpec(memory_space=pltpu.SMEM)
-    whole = pl.BlockSpec(memory_space=pltpu.VMEM)
-    place, count = pl.pallas_call(
+    far = pl.BlockSpec(memory_space=pltpu.HBM)
+    place, count, early = pl.pallas_call(
         rank_kernel,
-        in_specs=[whole, scalar, scalar],
-        out_specs=[whole, whole],
+        in_specs=whole(1) + [scalar, scalar, far],
+        out_specs=whole(2) + [far],
         out_shape=[
             jax.ShapeDtypeStruct((1, chan_count), jnp.int32),
             jax.ShapeDtypeStruct((8, 128), jnp.int32),
+            jax.ShapeDtypeStruct((EARLY, chan_count), jnp.float32),
         ],
-        compiler_params=roomy(16),
+        scratch_shapes=[pltpu.SemaphoreType.DMA],
+        compiler_params=roomy(60),
         name="rank_rows",
-    )(chan_plane[None, :], pair_base[None], cross_side[None])
-    return place[0], count[0, 0]
+    )(chan_plane[None, :], pair_base[None], cross_side[None], raw_turned)
+    return place[0], count[0, 0], early
 
 
 def whole(count):
@@ -396,13 +401,13 @@
 
 
 def tail_kernel(*refs):
-    sources, refs = refs[:6], refs[6:]
+    sources, got1, refs = refs[:5], refs[5], refs[6:]
     take_ref, good_ref, member_ref, high_ref, low_ref, real_hbm, imag_hbm, twist_ref = refs[:8]
     tick_high_ref, tick_low_ref, untick_high_ref, untick_low_ref, back_high_ref, back_low_ref = refs[8:14]
-    out_hbm, held, refs = refs[14], refs[15:21], refs[21:]
+    out_hbm, held, refs = refs[14], refs[15:20], refs[20:]
     rows_ref, plane_ref, covar_ref, power_ref, middle_ref, real_ref, imag_ref, out_ref = refs[:8]
     fetched, filter_done, out_done = refs[8:]
-    early, own0, own1, got0, got1, common_ref = held
+    early, own0, own1, got0, common_ref = held
     quarters = []
     for quarter in range(4):
         part = pl.ds(quarter * SLABS // 4, SLABS // 4)
@@ -506,7 +511,7 @@
         slab_points(load, store, middle_ref, sign)
         return carry
 
-    lax.fori_loop(0, HALF // 8, functools.partial(slabs_over, sign=-1), 0)
+    lax.fori_loop(0, HALF // 8, functools.partial(slabs_over, sign=-1), 0, unroll=2)
 
     def filtered(item, carry):
         data_high, data_low = split(jnp.concatenate([plane_ref[item, 0], plane_ref[item, 1]], axis=1))
@@ -524,8 +529,8 @@
 
     for copy in filter_copies:
         copy.wait()
-    lax.fori_loop(0, SLABS, filtered, 0, unroll=8)
-    lax.fori_loop(0, HALF // 8, functools.partial(slabs_over, sign=1), 0)
+    lax.fori_loop(0, SLABS, filtered, 0, unroll=16)
+    lax.fori_loop(0, HALF // 8, functools.partial(slabs_over, sign=1), 0, unroll=2)
     out_copies = []
     for pair in range(SLABS // 2):
         both = jnp.concatenate(
@@ -548,12 +553,12 @@
     back_high, back_low = two_halves(wire_tables()[1])
     tick, untick, twist = tick_tables()
     tables = (twist, *two_halves(tick), *two_halves(untick), back_high, back_low)
-    moved = (early, *own, *got, commons)
-    operands = (*moved, take, good, member, high, low, *filters, *tables)
+    moved = (early, *own, got[0], commons)
+    operands = (*moved, got[1], take, good, member, high, low, *filters, *tables)
     far = [pl.BlockSpec(memory_space=pltpu.HBM)]
     return pl.pallas_call(
         tail_kernel,
-        in_specs=far * 6 + whole(5) + far * 2 + whole(len(tables)),
+        in_specs=far * 5 + whole(6) + far * 2 + whole(len(tables)),
         out_specs=far[0],
         out_shape=jax.ShapeDtypeStruct((WIRES, TICKS), jnp.float32),
         scratch_shapes=[pltpu.VMEM(value.shape, jnp.float32) for value in moved]
@@ -566,11 +571,11 @@
             pltpu.VMEM((SLABS, HALF, PART), jnp.float32),
             pltpu.VMEM((SLABS, HALF, PART), jnp.float32),
             pltpu.VMEM((WIRES, TICKS), jnp.float32),
-            pltpu.SemaphoreType.DMA((6, 4)),
+            pltpu.SemaphoreType.DMA((5, 4)),
             pltpu.SemaphoreType.DMA((2,)),
             pltpu.SemaphoreType.DMA((5,)),
         ],
-        compiler_params=roomy(60),
+        compiler_params=roomy(48),
         name="deconvolve",
     )(*operands)
 
@@ -618,11 +623,11 @@
     parity = apa_index % 2
     swap = [(i, i ^ 1) for i in range(lax.axis_size("apa"))]
     raw_turned = raw.T
-    early_got = lax.ppermute(raw_turned[:EARLY], "apa", swap)
     local_group = group_id - apa_index * group_count
     good_mask = 1.0 - bad.astype(jnp.float32)
     pair_base = (apa_index // 2 * 2 * SLABS).astype(jnp.int32)
-    place, cross_count = rank_rows(chan_plane, pair_base, (1 - parity).astype(jnp.int32))
+    place, cross_count, early_sent = rank_rows(chan_plane, pair_base, (1 - parity).astype(jnp.int32), raw_turned)
+    early_got = lax.ppermute(early_sent, "apa", swap)
     place_got = lax.ppermute(place, "apa", swap)
     late0, rows = pack_rows(place, raw_turned)
     late0, later_place, later_raw = lax.optimization_barrier((late0, place, raw_turned))

time: 229 us -> 303 us (1.32)
  Pallas kernels: 114 us -> 187 us
    pallas_call x2, Pallas kernels: 53.1 us -> 127 us  [the longest x1 77 us: rank_rows(): pl.pallas_call(rank_kernel, in_specs=whole(1) + [scalar, scalar, far], ou...]
    unnamed x40 -> x48, local copies, waits for them, and re-layouts: 4.8 us -> 8.3 us
    ppermute x1, waiting for transfers between devices: 0.2 us -> 3.56 us  [shards(): common_got = lax.ppermute(common, 'apa', swap)]
    ppermute x1, waiting for transfers between devices: 3.15 us -> 0.01 us  [shards(): facts_got = lax.ppermute(facts, 'apa', swap)]
  transfers between devices with their start and end apart: 10 -> 10, of which waited for: 3 -> 2; matrix products, arithmetic and copies ran while one was open for 10% -> 8% of each run, Pallas kernels for 28% -> 20%
where the time goes in v7:
time: 303 us; the launch traced here: 302 us
  Pallas kernels  187 us (62%)
  starting transfers between devices  34.2 us (11%)
  waiting for transfers between devices  32.8 us (11%)
  local copies, waits for them, and re-layouts  19.2 us (6%)
  between operations  13.9 us (5%)
  matrix products  8.14 us (3%)
  other arithmetic  6.71 us (2%)
    pallas_call x1, Pallas kernels, rank_rows(): pl.pallas_call(rank_kernel, in_specs=whole(1) + [scalar, scalar, far], ou...  77 us
    pallas_call x1, Pallas kernels, tail(): pl.pallas_call(tail_kernel, in_specs=far * 5 + whole(6) + far * 2 + whole...  49.5 us
    ppermute x1, waiting for transfers between devices, shards(): got1 = lax.ppermute(late_sent, 'apa', swap)  29.2 us
    all_to_all x3, starting transfers between devices, over_ticks(): lax.all_to_all(value, 'tick', split_axis=0, concat_axis=0, tiled=True)  27.4 us
    pallas_call x1, Pallas kernels, merge_rows(): pl.pallas_call(merge_kernel, in_specs=[pl.BlockSpec(memory_space=pltpu.SM...  23.5 us
    pallas_call x1, Pallas kernels, pack_rows(): pl.pallas_call(pack_kernel, in_specs=[pl.BlockSpec(memory_space=pltpu.SME...  19.3 us
    unnamed x48, local copies, waits for them, and re-layouts  8.3 us
    pallas_call x1, Pallas kernels, sum_groups(): pl.pallas_call(group_kernel, in_specs=whole(3), out_specs=whole(1)[0], ou...  7.08 us
  transfers between devices with their start and end apart: 10, of which 2 were waited for; matrix products, arithmetic and copies ran while one was open for 8% of the time, Pallas kernels for 20%

profile of v7, /device:TPU:1, one launch (start us, length us, event | category | flops | bytes accessed | tf_op | source)
XLA Modules:
  0.0 302.3 jit_solution(4080838137365283951)
XLA Ops:
  6.5 77.0 %rank_rows.1 = (s32[1,15360]{1,0:T(1,128)}, s32[8,128]{1,0:T(8,128)}, f32[40,15360]{1,0:T(8,128)}) custom-call(s32[1,15360]{1,0:T(1,128)} %bitcast.53, s32[1]{0:T(128)} %bitcast.1.base_ref, s32[1]{0:T(128)} %bitcast.2.cross_ref, f32[100,15360]{1,0:T(8,128)} %bitcast.43), custom_call_target="tpu_custom_call" | custom-call | tf_op jit(solution)/shard_map/rank_rows/pallas_call | solution.py:130
  83.6 2.1 collective-permute-start.1
  85.7 19.3 %pack_rows.1 = (f32[32,96,128]{2,1,0:T(8,128)}, f32[15360,128]{1,0:T(8,128)}) custom-call(s32[15360]{0:T(1024)} %bitcast.58, f32[100,15360]{1,0:T(8,128)} %bitcast.44), custom_call_target="tpu_custom_call" | custom-call | tf_op jit(solution)/shard_map/pack_rows/pallas_call | solution.py:205
  105.0 9.1 %all-to-all-start = ((f32[32,96,128]{2,1,0:T(8,128)}), f32[32,96,128]{2,1,0:T(8,128)S(1)}, u32[]{:S(2)}, u32[]{:S(2)}) async-start(f32[32,96,128]{2,1,0:T(8,128)} %get-tuple-element.25), calls=%async_computation | async-start | bytes 3145728 | tf_op jit(solution)/shard_map/all_to_all | solution.py:638
  114.1 0.0 copy-start.12
  114.1 0.0 copy-start.20
  114.1 0.0 all-gather.3.cloned.1.call-start
  114.2 0.0 copy-start.1
  114.2 2.8 copy-done.1
  117.0 7.1 %sum_groups.1 = f32[120,128]{1,0:T(8,128)S(1)} custom-call(f32[100,15360]{1,0:T(8,128)S(1)} %bitcast.45, s32[1,15360]{1,0:T(1,128)S(1)} %bitcast.48, f32[1,15360]{1,0:T(1,128)S(1)} %bitcast.51), custom_call_target="tpu_custom_call" | custom-call | flops 1 | bytes 1 | tf_op jit(solution)/shard_map/sum_groups/pallas_call | solution.py:304
  124.1 0.3 collective-permute-start.2
  124.5 0.5 stack.20
  125.1 4.7 %pick_facts.1 = f32[80,32]{1,0:T(8,128)S(1)} custom-call(s32[1,15360]{1,0:T(1,128)S(1)} %bitcast.50, f32[5,15360]{1,0:T(8,128)S(1)} %convert_element_type.38.facts_ref), custom_call_target="tpu_custom_call" | custom-call | flops 1 | bytes 1 | tf_op jit(solution)/shard_map/pick_facts/pallas_call | solution.py:332
  129.8 0.1 reshape.63
  129.9 6.3 %lay_late.1 = f32[32,144,128]{2,1,0:T(8,128)} custom-call(f32[15360,128]{1,0:T(8,128)} %get-tuple-element.26.rows_hbm.own_hbm), custom_call_target="tpu_custom_call" | custom-call | flops 1 | bytes 1 | tf_op jit(solution)/shard_map/lay_late/pallas_call | solution.py:237
  136.2 0.0 copy-start.22
  136.3 0.0 copy-start.15
  136.3 0.0 copy-start.17
  136.3 0.0 copy-start.18
  136.3 0.0 copy-start.16
  136.3 0.0 copy-start.23
  136.3 3.6 %collective-permute-done.2 = f32[120,128]{1,0:T(8,128)S(1)} collective-permute-done((f32[120,128]{1,0:T(8,128)S(1)}, f32[120,128]{1,0:T(8,128)S(1)}, u32[]{:S(2)}, u32[]{:S(2)}) %collective-permute-start.2) | collective-permute-done | bytes 61472 | tf_op jit(solution)/shard_map/ppermute | solution.py:641
  139.9 0.0 all-to-all-done.refs_1_
  139.9 0.7 pad_maximum_fusion
  140.6 0.0 all-gather.3.cloned.1.call-update
  140.6 10.0 %all-to-all-start.1 = ((f32[32,144,128]{2,1,0:T(8,128)}), f32[32,144,128]{2,1,0:T(8,128)}, u32[]{:S(2)}, u32[]{:S(2)}) async-start(f32[32,144,128]{2,1,0:T(8,128)} %lay_late.1), calls=%async_computation.1 | async-start | bytes 4718592 | tf_op jit(solution)/shard_map/all_to_all | solution.py:638
  150.6 1.3 collective-permute-start
  151.9 0.1 reshape.64
  152.0 0.3 collective-permute-start.3
  152.4 0.8 fusion.23
  153.2 0.9 fusion.22
  154.1 0.0 copy-done.15
  154.1 0.0 copy-done.17
  154.1 0.2 fusion.12
  154.3 0.2 convolution_add_fusion
  154.5 0.1 reshape.65
  154.6 1.3 slice.41
  155.9 2.2 fusion.21
  158.1 0.0 copy-done.23
  158.1 0.7 broadcast_compare_fusion
  158.8 1.3 collective-permute-start.4
  160.1 0.9 copy.34.take_ref.refs_6_
  160.9 0.6 copy-done.21
  161.6 23.5 %merge_rows.1 = f32[32,160,128]{2,1,0:T(8,128)} custom-call(s32[15360]{0:T(1024)} %copy-done.21, f32[40,15360]{1,0:T(8,128)} %collective-permute-done.1.raw_ref, f32[15360,128]{1,0:T(8,128)} %get-tuple-element.26.rows_hbm.own_hbm, f32[480,1]{1,0:T(8,128)} %copy.34.take_ref.refs_6_), custom_call_target="tpu_custom_call" | custom-call | tf_op jit(solution)/shard_map/merge_rows/pallas_call | solution.py:270
  185.1 3.0 slice.57
  188.1 8.3 %all-to-all-start.2 = ((f32[32,160,128]{2,1,0:T(8,128)}), f32[32,160,128]{2,1,0:T(8,128)}, u32[]{:S(2)}, u32[]{:S(2)}) async-start(f32[32,160,128]{2,1,0:T(8,128)} %merge_rows.1), calls=%async_computation.2 | async-start | bytes 5242880 | tf_op jit(solution)/shard_map/all_to_all | solution.py:638
  196.4 1.3 collective-permute-start.5
  197.8 4.4 %negate_divide_fusion = (f32[32,256,128]{2,1,0:T(8,128)}, f32[32,256,128]{2,1,0:T(8,128)}) fusion(f32[32,128]{1,0:T(8,128)S(1)} %get-tuple-element.48, f32[256]{0:T(256)S(1)} %get-tuple-element.52, f32[32,128]{1,0:T(8,128)S(1)} %get-tuple-element.47, f32[256]{0:T(256)S(1)} %get-tuple-element.51), kind=kLoop, calls=%fused_computation.1 | loop fusion | flops 13631488 | bytes 8423424 | tf_op jit(solution)/shard_map/div | solution.py:607
  202.2 0.1 copy.39.refs_7_
  202.4 3.3 %gather_fusion = s32[480]{0:T(512)S(1)} fusion(s32[128]{0:T(128)S(1)} %copy-done.10, s32[1024]{0:T(1024)S(1)} %pad_clamp_fusion), kind=kCustom, calls=%fused_computation | custom fusion | bytes 5760 | tf_op jit(solution)/shard_map/jit(_take)/gather | solution.py:661
  205.8 1.5 convolution_convert_fusion
  207.3 0.2 copy.36
  207.5 2.3 convolution_convert_fusion.1
  209.9 1.2 copy.35
  211.1 0.7 multiply_add_fusion.1
  211.8 0.1 fusion.6.refs_8_
  211.9 29.2 %collective-permute-done.5.refs_5_ = f32[32,120,128]{2,1,0:T(8,128)} collective-permute-done((f32[32,120,128]{2,1,0:T(8,128)}, f32[32,120,128]{2,1,0:T(8,128)}, u32[]{:S(2)}, u32[]{:S(2)}) %collective-permute-start.5) | collective-permute-done | bytes 1966112 | tf_op jit(solution)/shard_map/ppermute | solution.py:657
  241.2 0.0 copy-start.3
  241.2 1.0 copy-done.3
  242.2 1.0 copy-done.4
  243.2 0.9 copy-done.6
  244.1 0.9 copy-done.7
  245.0 0.9 copy-done.8
  245.9 49.5 %deconvolve.1 = f32[480,3200]{1,0:T(8,128)} custom-call(f32[32,160,128]{2,1,0:T(8,128)} %all-to-all-done.2.refs_0_, f32[32,96,128]{2,1,0:T(8,128)S(1)} %all-to-all-done.refs_1_, f32[32,144,128]{2,1,0:T(8,128)} %all-to-all-done.1.refs_2_, f32[32,96,128]{2,1,0:T(8,128)} %copy-done.11, f32[32,240,128]{2,1,0:T(8,128)} %bitcast.52, ...), custom_call_target="tpu_custom_call" | custom-call | tf_op jit(solution)/shard_map/deconvolve/pallas_call | solution.py:559
  (51 shorter events, 0.2 us)
Async XLA Ops:
  6.5 149.3 %copy-start = (f32[480]{0:T(512)S(1)}, f32[480]{0:T(512)}, u32[]{:S(2)}) copy-start(f32[480]{0:T(512)} %param.30) | copy-start | bytes 5764
  83.6 56.3 %collective-permute-start.1 = (f32[40,15360]{1,0:T(8,128)}, f32[40,15360]{1,0:T(8,128)}, u32[]{:S(2)}, u32[]{:S(2)}) collective-permute-start(f32[40,15360]{1,0:T(8,128)} %get-tuple-element.27), channel_id=1, source_target_pairs={{0,32},{32,0},{64,96},{96,64},{1,33},{33,1},{65,97},{97,65},{2,34}... | collective-permute-start | bytes 7372808 | tf_op jit(solution)/shard_map/ppermute | solution.py:630
  85.7 28.5 %copy-start.13 = (s32[15360]{0:T(1024)S(1)}, s32[15360]{0:T(1024)}, u32[]{:S(2)}) copy-start(s32[15360]{0:T(1024)} %param.25) | copy-start | bytes 184324
  85.7 28.5 %copy-start.19 = (s32[15360]{0:T(1024)S(1)}, s32[15360]{0:T(1024)}, u32[]{:S(2)}) copy-start(s32[15360]{0:T(1024)} %param.26) | copy-start | bytes 184324
  105.0 34.9 %all-to-all-start = ((f32[32,96,128]{2,1,0:T(8,128)}), f32[32,96,128]{2,1,0:T(8,128)S(1)}, u32[]{:S(2)}, u32[]{:S(2)}) async-start(f32[32,96,128]{2,1,0:T(8,128)} %get-tuple-element.25), calls=%async_computation | async-start | bytes 3145728 | tf_op jit(solution)/shard_map/all_to_all | solution.py:638
  114.1 10.4 %copy-start.12 = (s32[15360]{0:T(1024)S(1)}, s32[15360]{0:T(1024)}, u32[]{:S(2)}) copy-start(s32[15360]{0:T(1024)} %param.27) | copy-start | bytes 184324
  114.1 10.4 %copy-start.20 = (s32[15360]{0:T(1024)S(1)}, s32[15360]{0:T(1024)}, u32[]{:S(2)}) copy-start(s32[15360]{0:T(1024)} %param.28) | copy-start | bytes 184324
  114.1 127.0 %all-gather.3.cloned.1.call-start = ((), (), s32[]{:S(2)}) async-start(), calls=%async_computation.3 | async-start | bytes 4055040 | tf_op jit(solution)/shard_map/all_gather | solution.py:647
  114.2 2.8 copy-start.1
  117.0 8.0 %copy-start.14 = (s32[1,15360]{1,0:T(1,128)S(1)}, s32[1,15360]{1,0:T(1,128)}, u32[]{:S(2)}) copy-start(s32[1,15360]{1,0:T(1,128)} %get-tuple-element.23) | copy-start | bytes 184324
  124.1 15.8 %collective-permute-start.2 = (f32[120,128]{1,0:T(8,128)S(1)}, f32[120,128]{1,0:T(8,128)S(1)}, u32[]{:S(2)}, u32[]{:S(2)}) collective-permute-start(f32[120,128]{1,0:T(8,128)S(1)} %sum_groups.1), channel_id=1, source_target_pairs={{0,32},{32,0},{64,96},{96,64},{1,33},{33,1},{65,97},{97,65},{2,34}... | collective-permute-start | bytes 184328 | tf_op jit(solution)/shard_map/ppermute | solution.py:641
  136.2 15.7 %copy-start.22 = (f32[3200]{0:T(1024)S(1)}, f32[3200]{0:T(1024)}, u32[]{:S(2)}) copy-start(f32[3200]{0:T(1024)} %param.31) | copy-start | bytes 38404
  136.3 17.8 %copy-start.15 = (f32[100,200]{1,0:T(8,128)S(1)}, f32[100,200]{1,0:T(8,128)}, u32[]{:S(2)}) copy-start(f32[100,200]{1,0:T(8,128)} %constant.131) | copy-start | bytes 240004
  136.3 17.8 %copy-start.17 = (f32[32,100]{1,0:T(8,128)S(1)}, f32[32,100]{1,0:T(8,128)}, u32[]{:S(2)}) copy-start(f32[32,100]{1,0:T(8,128)} %constant.119.clone) | copy-start | bytes 38404
  136.3 17.8 %copy-start.18 = (f32[32,100]{1,0:T(8,128)S(1)}, f32[32,100]{1,0:T(8,128)}, u32[]{:S(2)}) copy-start(f32[32,100]{1,0:T(8,128)} %constant.118.clone) | copy-start | bytes 38404
  136.3 18.0 %copy-start.16 = (f32[100,200]{1,0:T(8,128)S(1)}, f32[100,200]{1,0:T(8,128)}, u32[]{:S(2)}) copy-start(f32[100,200]{1,0:T(8,128)} %constant.132) | copy-start | bytes 240004
  136.3 21.8 %copy-start.23 = (s32[480]{0:T(512)S(1)}, s32[480]{0:T(512)}, u32[]{:S(2)}) copy-start(s32[480]{0:T(512)} %constant.112.clone) | copy-start | bytes 5764
  140.6 44.5 %all-to-all-start.1 = ((f32[32,144,128]{2,1,0:T(8,128)}), f32[32,144,128]{2,1,0:T(8,128)}, u32[]{:S(2)}, u32[]{:S(2)}) async-start(f32[32,144,128]{2,1,0:T(8,128)} %lay_late.1), calls=%async_computation.1 | async-start | bytes 4718592 | tf_op jit(solution)/shard_map/all_to_all | solution.py:638
  150.6 10.3 %collective-permute-start = (s32[15360]{0:T(1024)S(1)}, s32[15360]{0:T(1024)S(1)}, u32[]{:S(2)}, u32[]{:S(2)}) collective-permute-start(s32[15360]{0:T(1024)S(1)} %bitcast.60), channel_id=1, source_target_pairs={{0,32},{32,0},{64,96},{96,64},{1,33},{33,1},{65,97},{97,65},{2,34}... | collective-permute-start | bytes 184328 | tf_op jit(solution)/shard_map/ppermute | solution.py:631
  152.0 36.0 %collective-permute-start.3 = (f32[32,96,128]{2,1,0:T(8,128)S(1)}, f32[32,96,128]{2,1,0:T(8,128)S(1)}, u32[]{:S(2)}, u32[]{:S(2)}) collective-permute-start(f32[32,96,128]{2,1,0:T(8,128)S(1)} %all-to-all-done.refs_1_), channel_id=1, source_target_pairs={{0,32},{32,0},{64,96},{96,64},{1,33},{33,1},{65,97},{97,65},{2,34}... | collective-permute-start | bytes 4718600 | tf_op jit(solution)/shard_map/ppermute | solution.py:649
  158.8 29.3 %collective-permute-start.4 = (s32[5,480]{1,0:T(8,128)S(1)}, s32[5,480]{1,0:T(8,128)S(1)}, u32[]{:S(2)}, u32[]{:S(2)}) collective-permute-start(s32[5,480]{1,0:T(8,128)S(1)} %slice_convert_fusion), channel_id=1, source_target_pairs={{0,32},{32,0},{64,96},{96,64},{1,33},{33,1},{65,97},{97,65},{2,34}... | collective-permute-start | bytes 28808 | tf_op jit(solution)/shard_map/ppermute | solution.py:653
  160.9 0.6 copy-start.21
  188.1 9.7 %copy-start.11 = (f32[32,96,128]{2,1,0:T(8,128)}, f32[32,96,128]{2,1,0:T(8,128)S(1)}, u32[]{:S(2)}) copy-start(f32[32,96,128]{2,1,0:T(8,128)S(1)} %collective-permute-done.3.refs_3_) | copy-start | bytes 4718596
  188.1 53.0 %all-to-all-start.2 = ((f32[32,160,128]{2,1,0:T(8,128)}), f32[32,160,128]{2,1,0:T(8,128)}, u32[]{:S(2)}, u32[]{:S(2)}) async-start(f32[32,160,128]{2,1,0:T(8,128)} %merge_rows.1), calls=%async_computation.2 | async-start | bytes 5242880 | tf_op jit(solution)/shard_map/all_to_all | solution.py:638
  196.4 44.7 %collective-permute-start.5 = (f32[32,120,128]{2,1,0:T(8,128)}, f32[32,120,128]{2,1,0:T(8,128)}, u32[]{:S(2)}, u32[]{:S(2)}) collective-permute-start(f32[32,120,128]{2,1,0:T(8,128)} %slice.57), channel_id=1, source_target_pairs={{0,32},{32,0},{64,96},{96,64},{1,33},{33,1},{65,97},{97,65},{2,34}... | collective-permute-start | bytes 5898248 | tf_op jit(solution)/shard_map/ppermute | solution.py:657
  197.8 4.6 %copy-start.10 = (s32[128]{0:T(128)S(1)}, s32[128]{0:T(128)}, u32[]{:S(2)}) copy-start(s32[128]{0:T(128)} %param.29) | copy-start | bytes 1540
  202.2 39.0 %copy-start.2 = (f32[480,1]{1,0:T(8,128)S(1)}, f32[480,1]{1,0:T(8,128)}, u32[]{:S(2)}) copy-start(f32[480,1]{1,0:T(8,128)} %copy.34.take_ref.refs_6_) | copy-start | bytes 5764
  202.2 39.0 %copy-start.5 = (bf16[256,256]{1,0:T(8,128)(2,1)S(1)}, bf16[256,256]{1,0:T(8,128)(2,1)}, u32[]{:S(2)}) copy-start(bf16[256,256]{1,0:T(8,128)(2,1)} %constant.125.clone.refs_17_) | copy-start | bytes 393220
  202.2 39.0 %copy-start.9 = (f32[32,2,1,128]{3,2,1,0:T(1,128)S(1)}, f32[32,2,1,128]{3,2,1,0:T(1,128)}, u32[]{:S(2)}) copy-start(f32[32,2,1,128]{3,2,1,0:T(1,128)} %constant.121.clone.refs_13_) | copy-start | bytes 98308
  241.2 1.0 copy-start.3
  242.2 1.0 copy-start.4
  243.2 0.9 copy-start.6
  244.1 0.9 copy-start.7
  245.0 0.9 copy-start.8
Sparse Core Ops, SparseCore 0:
  140.7 77.4 all-gather.2

commit v8 on v7

--- a/solution.py
+++ b/solution.py
@@ -94,11 +94,14 @@
     return np.where(row < 192, row, late).astype(np.int32)
 
 
-def rank_kernel(plane_ref, base_ref, cross_ref, raw_hbm, place_ref, count_ref, early_hbm, early_done):
-    send = pltpu.make_async_copy(raw_hbm.at[pl.ds(0, EARLY)], early_hbm, early_done)
-    send.start()
+def rank_kernel(plane_ref, base_ref, cross_ref, raw_hbm, place_ref, count_ref, early_hbm, early_ref, early_done):
+    fetch = pltpu.make_async_copy(raw_hbm.at[pl.ds(0, EARLY)], early_ref, early_done.at[0])
+    fetch.start()
     tri_row = lax.broadcasted_iota(jnp.int32, (BLOCK, BLOCK), 0)
     tri_col = lax.broadcasted_iota(jnp.int32, (BLOCK, BLOCK), 1)
+    fetch.wait()
+    send = pltpu.make_async_copy(early_ref, early_hbm, early_done.at[1])
+    send.start()
     earlier = (tri_row < tri_col).astype(jnp.float32).astype(jnp.bfloat16)
     names = lax.broadcasted_iota(jnp.int32, (2 * SLABS, BLOCK), 0)
     pair_base = base_ref[0]
@@ -136,7 +139,7 @@
             jax.ShapeDtypeStruct((8, 128), jnp.int32),
             jax.ShapeDtypeStruct((EARLY, chan_count), jnp.float32),
         ],
-        scratch_shapes=[pltpu.SemaphoreType.DMA],
+        scratch_shapes=[pltpu.VMEM((EARLY, chan_count), jnp.float32), pltpu.SemaphoreType.DMA((2,))],
         compiler_params=roomy(60),
         name="rank_rows",
     )(chan_plane[None, :], pair_base[None], cross_side[None], raw_turned)
@@ -401,13 +404,13 @@
 
 
 def tail_kernel(*refs):
-    sources, got1, refs = refs[:5], refs[5], refs[6:]
+    sources, refs = refs[:6], refs[6:]
     take_ref, good_ref, member_ref, high_ref, low_ref, real_hbm, imag_hbm, twist_ref = refs[:8]
     tick_high_ref, tick_low_ref, untick_high_ref, untick_low_ref, back_high_ref, back_low_ref = refs[8:14]
-    out_hbm, held, refs = refs[14], refs[15:20], refs[20:]
+    out_hbm, held, refs = refs[14], refs[15:21], refs[21:]
     rows_ref, plane_ref, covar_ref, power_ref, middle_ref, real_ref, imag_ref, out_ref = refs[:8]
     fetched, filter_done, out_done = refs[8:]
-    early, own0, own1, got0, common_ref = held
+    early, own0, own1, got0, got1, common_ref = held
     quarters = []
     for quarter in range(4):
         part = pl.ds(quarter * SLABS // 4, SLABS // 4)
@@ -553,12 +556,12 @@
     back_high, back_low = two_halves(wire_tables()[1])
     tick, untick, twist = tick_tables()
     tables = (twist, *two_halves(tick), *two_halves(untick), back_high, back_low)
-    moved = (early, *own, got[0], commons)
-    operands = (*moved, got[1], take, good, member, high, low, *filters, *tables)
+    moved = (early, *own, *got, commons)
+    operands = (*moved, take, good, member, high, low, *filters, *tables)
     far = [pl.BlockSpec(memory_space=pltpu.HBM)]
     return pl.pallas_call(
         tail_kernel,
-        in_specs=far * 5 + whole(6) + far * 2 + whole(len(tables)),
+        in_specs=far * 6 + whole(5) + far * 2 + whole(len(tables)),
         out_specs=far[0],
         out_shape=jax.ShapeDtypeStruct((WIRES, TICKS), jnp.float32),
         scratch_shapes=[pltpu.VMEM(value.shape, jnp.float32) for value in moved]
@@ -571,11 +574,11 @@
             pltpu.VMEM((SLABS, HALF, PART), jnp.float32),
             pltpu.VMEM((SLABS, HALF, PART), jnp.float32),
             pltpu.VMEM((WIRES, TICKS), jnp.float32),
-            pltpu.SemaphoreType.DMA((5, 4)),
+            pltpu.SemaphoreType.DMA((6, 4)),
             pltpu.SemaphoreType.DMA((2,)),
             pltpu.SemaphoreType.DMA((5,)),
         ],
-        compiler_params=roomy(48),
+        compiler_params=roomy(60),
         name="deconvolve",
     )(*operands)
 

time: 303 us -> 230 us (0.76)
  Pallas kernels: 187 us -> 116 us
  local copies, waits for them, and re-layouts: 19.2 us -> 15.6 us
    pallas_call x1, Pallas kernels: 77 us -> 5.3 us  [rank_rows(): pl.pallas_call(rank_kernel, in_specs=whole(1) + [scalar, scalar, far], ou...]
    unnamed x48 -> x34, local copies, waits for them, and re-layouts: 8.3 us -> 4.19 us
  transfers between devices with their start and end apart: 10 -> 10, of which waited for: 2 -> 3; matrix products, arithmetic and copies ran while one was open for 8% -> 11% of each run, Pallas kernels for 20% -> 27%
where the time goes in v8:
time: 230 us; the launch traced here: 229 us
  Pallas kernels  116 us (50%)
  waiting for transfers between devices  35.1 us (15%)
  starting transfers between devices  33.4 us (15%)
  local copies, waits for them, and re-layouts  15.6 us (7%)
  between operations  13.8 us (6%)
  other arithmetic  8.89 us (4%)
  matrix products  6.17 us (3%)
    pallas_call x1, Pallas kernels, tail(): pl.pallas_call(tail_kernel, in_specs=far * 6 + whole(5) + far * 2 + whole...  50 us
    ppermute x1, waiting for transfers between devices, shards(): got1 = lax.ppermute(late_sent, 'apa', swap)  29.7 us
    all_to_all x3, starting transfers between devices, over_ticks(): lax.all_to_all(value, 'tick', split_axis=0, concat_axis=0, tiled=True)  27.5 us
    pallas_call x1, Pallas kernels, merge_rows(): pl.pallas_call(merge_kernel, in_specs=[pl.BlockSpec(memory_space=pltpu.SM...  23.5 us
    pallas_call x1, Pallas kernels, pack_rows(): pl.pallas_call(pack_kernel, in_specs=[pl.BlockSpec(memory_space=pltpu.SME...  19.4 us
    pallas_call x1, Pallas kernels, sum_groups(): pl.pallas_call(group_kernel, in_specs=whole(3), out_specs=whole(1)[0], ou...  7.08 us
    pallas_call x1, Pallas kernels, lay_late(): pl.pallas_call(functools.partial(fetched_late_kernel, which), in_specs=[p...  6.32 us
    pallas_call x1, Pallas kernels, rank_rows(): pl.pallas_call(rank_kernel, in_specs=whole(1) + [scalar, scalar, far], ou...  5.3 us
  transfers between devices with their start and end apart: 10, of which 3 were waited for; matrix products, arithmetic and copies ran while one was open for 11% of the time, Pallas kernels for 27%

profile of v8, /device:TPU:1, one launch (start us, length us, event | category | flops | bytes accessed | tf_op | source)
XLA Modules:
  0.0 229.2 jit_solution(16182429965392065705)
XLA Ops:
  6.5 5.3 %rank_rows.1 = (s32[1,15360]{1,0:T(1,128)}, s32[8,128]{1,0:T(8,128)}, f32[40,15360]{1,0:T(8,128)}) custom-call(s32[1,15360]{1,0:T(1,128)} %bitcast.53, s32[1]{0:T(128)} %bitcast.1.base_ref, s32[1]{0:T(128)} %bitcast.2.cross_ref, f32[100,15360]{1,0:T(8,128)} %bitcast.43), custom_call_target="tpu_custom_call" | custom-call | tf_op jit(solution)/shard_map/rank_rows/pallas_call | solution.py:133
  11.8 2.1 collective-permute-start.1
  14.0 19.4 %pack_rows.1 = (f32[32,96,128]{2,1,0:T(8,128)}, f32[15360,128]{1,0:T(8,128)}) custom-call(s32[15360]{0:T(1024)} %bitcast.58, f32[100,15360]{1,0:T(8,128)} %bitcast.44), custom_call_target="tpu_custom_call" | custom-call | tf_op jit(solution)/shard_map/pack_rows/pallas_call | solution.py:208
  33.4 9.1 %all-to-all-start = ((f32[32,96,128]{2,1,0:T(8,128)}), f32[32,96,128]{2,1,0:T(8,128)S(1)}, u32[]{:S(2)}, u32[]{:S(2)}) async-start(f32[32,96,128]{2,1,0:T(8,128)} %get-tuple-element.25), calls=%async_computation | async-start | bytes 3145728 | tf_op jit(solution)/shard_map/all_to_all | solution.py:641
  42.4 0.0 copy-start.7
  42.4 0.0 copy-start.13
  42.4 0.0 all-gather.3.cloned.1.call-start
  42.5 0.0 copy-done.8
  42.6 0.0 copy-start.1
  42.6 2.8 %copy-done.1 = f32[15360,100]{0,1:T(8,128)S(1)} copy-done((f32[15360,100]{0,1:T(8,128)S(1)}, f32[15360,100]{0,1:T(8,128)}, u32[]{:S(2)}) %copy-start.1) | copy-done | bytes 6144024
  45.4 7.1 %sum_groups.1 = f32[120,128]{1,0:T(8,128)S(1)} custom-call(f32[100,15360]{1,0:T(8,128)S(1)} %bitcast.45, s32[1,15360]{1,0:T(1,128)S(1)} %bitcast.46, f32[1,15360]{1,0:T(1,128)S(1)} %bitcast.49), custom_call_target="tpu_custom_call" | custom-call | flops 1 | bytes 1 | tf_op jit(solution)/shard_map/sum_groups/pallas_call | solution.py:307
  52.5 0.3 collective-permute-start.2
  52.8 0.0 copy-done.13
  52.8 0.5 stack.20
  53.4 4.7 %pick_facts.1 = f32[80,32]{1,0:T(8,128)S(1)} custom-call(s32[1,15360]{1,0:T(1,128)S(1)} %bitcast.48, f32[5,15360]{1,0:T(8,128)S(1)} %convert_element_type.38.facts_ref), custom_call_target="tpu_custom_call" | custom-call | flops 1 | bytes 1 | tf_op jit(solution)/shard_map/pick_facts/pallas_call | solution.py:335
  58.2 0.1 reshape.63
  58.3 6.3 %lay_late.1 = f32[32,144,128]{2,1,0:T(8,128)} custom-call(f32[15360,128]{1,0:T(8,128)} %get-tuple-element.26.rows_hbm.own_hbm), custom_call_target="tpu_custom_call" | custom-call | flops 1 | bytes 1 | tf_op jit(solution)/shard_map/lay_late/pallas_call | solution.py:240
  64.6 0.0 copy-start.14
  64.6 0.0 copy-start.10
  64.6 0.0 copy-start.11
  64.6 0.0 copy-start.6
  64.6 3.5 %collective-permute-done.2 = f32[120,128]{1,0:T(8,128)} collective-permute-done((f32[120,128]{1,0:T(8,128)S(1)}, f32[120,128]{1,0:T(8,128)}, u32[]{:S(2)}, u32[]{:S(2)}) %collective-permute-start.2) | collective-permute-done | bytes 61472 | tf_op jit(solution)/shard_map/ppermute | solution.py:644
  68.2 0.0 all-to-all-done.refs_1_
  68.2 0.0 collective-permute-done.1.raw_ref
  68.2 0.9 broadcast_select_fusion.1
  69.1 0.7 pad_maximum_fusion
  69.7 0.0 all-gather.3.cloned.1.call-update
  69.8 10.1 %all-to-all-start.1 = ((f32[32,144,128]{2,1,0:T(8,128)}), f32[32,144,128]{2,1,0:T(8,128)S(1)}, u32[]{:S(2)}, u32[]{:S(2)}) async-start(f32[32,144,128]{2,1,0:T(8,128)} %lay_late.1), calls=%async_computation.1 | async-start | bytes 4718592 | tf_op jit(solution)/shard_map/all_to_all | solution.py:641
  79.9 1.3 collective-permute-start
  81.2 0.8 reshape.64
  82.0 0.3 collective-permute-start.3
  82.3 0.8 fusion.23
  83.2 0.0 copy-done.14
  83.2 0.1 fusion.22
  83.3 0.0 copy-done.10
  83.3 1.1 fusion.12
  84.4 1.1 convolution_add_fusion
  85.5 0.1 reshape.65
  85.6 1.2 slice.41
  86.9 1.0 fusion.21
  87.9 1.3 broadcast_compare_fusion
  89.2 1.2 collective-permute-start.4
  90.4 0.9 copy.34.take_ref.refs_6_
  91.3 0.0 collective-permute-done.place_ref
  91.3 23.5 %merge_rows.1 = f32[32,160,128]{2,1,0:T(8,128)} custom-call(s32[15360]{0:T(1024)} %collective-permute-done.place_ref, f32[40,15360]{1,0:T(8,128)} %collective-permute-done.1.raw_ref, f32[15360,128]{1,0:T(8,128)} %get-tuple-element.26.rows_hbm.own_hbm, f32[480,1]{1,0:T(8,128)} %copy.34.take_ref.refs_6_), custom_call_target="tpu_custom_call" | custom-call | tf_op jit(solution)/shard_map/merge_rows/pallas_call | solution.py:273
  114.8 0.0 all-to-all-done.1.refs_2_
  114.8 1.5 slice.57
  116.3 1.8 collective-permute-done.4
  118.2 0.0 collective-permute-done.3.refs_3_
  118.2 8.3 %all-to-all-start.2 = ((f32[32,160,128]{2,1,0:T(8,128)}), f32[32,160,128]{2,1,0:T(8,128)}, u32[]{:S(2)}, u32[]{:S(2)}) async-start(f32[32,160,128]{2,1,0:T(8,128)} %merge_rows.1), calls=%async_computation.2 | async-start | bytes 5242880 | tf_op jit(solution)/shard_map/all_to_all | solution.py:641
  126.5 0.6 collective-permute-start.5
  127.2 4.4 %negate_divide_fusion = (f32[32,256,128]{2,1,0:T(8,128)}, f32[32,256,128]{2,1,0:T(8,128)}) fusion(f32[32,128]{1,0:T(8,128)S(1)} %get-tuple-element.48, f32[256]{0:T(256)S(1)} %get-tuple-element.52, f32[32,128]{1,0:T(8,128)S(1)} %get-tuple-element.47, f32[256]{0:T(256)S(1)} %get-tuple-element.51), kind=kLoop, calls=%fused_computation.1 | loop fusion | flops 13631488 | bytes 8423424 | tf_op jit(solution)/shard_map/div | solution.py:610
  131.6 0.8 copy.39.refs_7_
  132.5 3.3 %gather_fusion = s32[480]{0:T(512)S(1)} fusion(s32[128]{0:T(128)S(1)} %copy-done.2, s32[1024]{0:T(1024)S(1)} %pad_clamp_fusion), kind=kCustom, calls=%fused_computation | custom fusion | bytes 5760 | tf_op jit(solution)/shard_map/jit(_take)/gather | solution.py:664
  135.8 1.5 convolution_convert_fusion
  137.4 1.0 copy.36
  138.4 0.5 convolution_convert_fusion.1
  138.9 1.0 copy.35
  140.0 0.6 multiply_add_fusion.1
  140.6 0.8 fusion.6.refs_8_
  141.4 29.7 %collective-permute-done.5.refs_4_ = f32[32,120,128]{2,1,0:T(8,128)S(1)} collective-permute-done((f32[32,120,128]{2,1,0:T(8,128)}, f32[32,120,128]{2,1,0:T(8,128)S(1)}, u32[]{:S(2)}, u32[]{:S(2)}) %collective-permute-start.5) | collective-permute-done | bytes 1966112 | tf_op jit(solution)/shard_map/ppermute | solution.py:660
  171.1 0.0 all-to-all-done.2.refs_0_
  171.1 1.3 copy-done.5
  172.4 50.0 %deconvolve.1 = f32[480,3200]{1,0:T(8,128)} custom-call(f32[32,160,128]{2,1,0:T(8,128)} %all-to-all-done.2.refs_0_, f32[32,96,128]{2,1,0:T(8,128)} %copy-done.4, f32[32,144,128]{2,1,0:T(8,128)} %copy-done.3, f32[32,96,128]{2,1,0:T(8,128)} %collective-permute-done.3.refs_3_, f32[32,120,128]{2,1,0:T(8,128)} %copy-done.5, f32[32,240,128]{2,1,0:T(8,128)} %bitcast.50, ...), custom_call_target="tpu_custom_call" | custom-call | tf_op jit(solution)/shard_map/deconvolve/pallas_call | solution.py:562
  (37 shorter events, 0.2 us)
Async XLA Ops:
  6.5 80.4 %copy-start = (f32[480]{0:T(512)S(1)}, f32[480]{0:T(512)}, u32[]{:S(2)}) copy-start(f32[480]{0:T(512)} %param.30) | copy-start | bytes 5764
  11.8 56.3 %collective-permute-start.1 = (f32[40,15360]{1,0:T(8,128)}, f32[40,15360]{1,0:T(8,128)}, u32[]{:S(2)}, u32[]{:S(2)}) collective-permute-start(f32[40,15360]{1,0:T(8,128)} %get-tuple-element.27), channel_id=1, source_target_pairs={{0,32},{32,0},{64,96},{96,64},{1,33},{33,1},{65,97},{97,65},{2,34}... | collective-permute-start | bytes 7372808 | tf_op jit(solution)/shard_map/ppermute | solution.py:633
  14.0 28.5 %copy-start.8 = (s32[15360]{0:T(1024)S(1)}, s32[15360]{0:T(1024)}, u32[]{:S(2)}) copy-start(s32[15360]{0:T(1024)} %param.25) | copy-start | bytes 184324
  14.0 28.6 %copy-start.12 = (s32[15360]{0:T(1024)S(1)}, s32[15360]{0:T(1024)}, u32[]{:S(2)}) copy-start(s32[15360]{0:T(1024)} %param.26) | copy-start | bytes 184324
  33.4 34.8 %all-to-all-start = ((f32[32,96,128]{2,1,0:T(8,128)}), f32[32,96,128]{2,1,0:T(8,128)S(1)}, u32[]{:S(2)}, u32[]{:S(2)}) async-start(f32[32,96,128]{2,1,0:T(8,128)} %get-tuple-element.25), calls=%async_computation | async-start | bytes 3145728 | tf_op jit(solution)/shard_map/all_to_all | solution.py:641
  42.4 10.4 %copy-start.7 = (s32[15360]{0:T(1024)S(1)}, s32[15360]{0:T(1024)}, u32[]{:S(2)}) copy-start(s32[15360]{0:T(1024)} %param.27) | copy-start | bytes 184324
  42.4 10.4 %copy-start.13 = (s32[15360]{0:T(1024)S(1)}, s32[15360]{0:T(1024)}, u32[]{:S(2)}) copy-start(s32[15360]{0:T(1024)} %param.28) | copy-start | bytes 184324
  42.4 128.7 %all-gather.3.cloned.1.call-start = ((), (), s32[]{:S(2)}) async-start(), calls=%async_computation.3 | async-start | bytes 4055040 | tf_op jit(solution)/shard_map/all_gather | solution.py:650
  42.6 2.8 %copy-start.1 = (f32[15360,100]{0,1:T(8,128)S(1)}, f32[15360,100]{0,1:T(8,128)}, u32[]{:S(2)}) copy-start(f32[15360,100]{0,1:T(8,128)} %param.24) | copy-start | bytes 18432004
  45.4 8.0 %copy-start.9 = (s32[1,15360]{1,0:T(1,128)S(1)}, s32[1,15360]{1,0:T(1,128)}, u32[]{:S(2)}) copy-start(s32[1,15360]{1,0:T(1,128)} %get-tuple-element.23) | copy-start | bytes 184324
  52.5 15.7 %collective-permute-start.2 = (f32[120,128]{1,0:T(8,128)S(1)}, f32[120,128]{1,0:T(8,128)}, u32[]{:S(2)}, u32[]{:S(2)}) collective-permute-start(f32[120,128]{1,0:T(8,128)S(1)} %sum_groups.1), channel_id=1, source_target_pairs={{0,32},{32,0},{64,96},{96,64},{1,33},{33,1},{65,97},{97,65},{2,34}... | collective-permute-start | bytes 184328 | tf_op jit(solution)/shard_map/ppermute | solution.py:644
  64.6 18.6 %copy-start.14 = (f32[32,32]{1,0:T(8,128)S(1)}, f32[32,32]{1,0:T(8,128)}, u32[]{:S(2)}) copy-start(f32[32,32]{1,0:T(8,128)} %constant.116.clone) | copy-start | bytes 12292
  64.6 18.7 %copy-start.10 = (f32[32,100]{1,0:T(8,128)S(1)}, f32[32,100]{1,0:T(8,128)}, u32[]{:S(2)}) copy-start(f32[32,100]{1,0:T(8,128)} %constant.119.clone) | copy-start | bytes 38404
  64.6 18.7 %copy-start.11 = (f32[32,100]{1,0:T(8,128)S(1)}, f32[32,100]{1,0:T(8,128)}, u32[]{:S(2)}) copy-start(f32[32,100]{1,0:T(8,128)} %constant.118.clone) | copy-start | bytes 38404
  64.6 22.3 %copy-start.6 = (f32[512,480]{1,0:T(8,128)S(1)}, f32[512,480]{1,0:T(8,128)}, u32[]{:S(2)}) copy-start(f32[512,480]{1,0:T(8,128)} %constant.115.clone) | copy-start | bytes 2949124
  68.2 1.6 copy-start.4
  69.8 45.0 %all-to-all-start.1 = ((f32[32,144,128]{2,1,0:T(8,128)}), f32[32,144,128]{2,1,0:T(8,128)S(1)}, u32[]{:S(2)}, u32[]{:S(2)}) async-start(f32[32,144,128]{2,1,0:T(8,128)} %lay_late.1), calls=%async_computation.1 | async-start | bytes 4718592 | tf_op jit(solution)/shard_map/all_to_all | solution.py:641
  79.9 11.4 %collective-permute-start = (s32[15360]{0:T(1024)S(1)}, s32[15360]{0:T(1024)}, u32[]{:S(2)}, u32[]{:S(2)}) collective-permute-start(s32[15360]{0:T(1024)S(1)} %bitcast.60), channel_id=1, source_target_pairs={{0,32},{32,0},{64,96},{96,64},{1,33},{33,1},{65,97},{97,65},{2,34}... | collective-permute-start | bytes 184328 | tf_op jit(solution)/shard_map/ppermute | solution.py:634
  82.0 36.2 %collective-permute-start.3 = (f32[32,96,128]{2,1,0:T(8,128)}, f32[32,96,128]{2,1,0:T(8,128)}, u32[]{:S(2)}, u32[]{:S(2)}) collective-permute-start(f32[32,96,128]{2,1,0:T(8,128)} %copy-done.4), channel_id=1, source_target_pairs={{0,32},{32,0},{64,96},{96,64},{1,33},{33,1},{65,97},{97,65},{2,34}... | collective-permute-start | bytes 4718600 | tf_op jit(solution)/shard_map/ppermute | solution.py:652
  89.2 29.0 %collective-permute-start.4 = (s32[5,480]{1,0:T(8,128)S(1)}, s32[5,480]{1,0:T(8,128)S(1)}, u32[]{:S(2)}, u32[]{:S(2)}) collective-permute-start(s32[5,480]{1,0:T(8,128)S(1)} %slice_convert_fusion), channel_id=1, source_target_pairs={{0,32},{32,0},{64,96},{96,64},{1,33},{33,1},{65,97},{97,65},{2,34}... | collective-permute-start | bytes 28808 | tf_op jit(solution)/shard_map/ppermute | solution.py:656
  114.8 3.4 %copy-start.3 = (f32[32,144,128]{2,1,0:T(8,128)}, f32[32,144,128]{2,1,0:T(8,128)S(1)}, u32[]{:S(2)}) copy-start(f32[32,144,128]{2,1,0:T(8,128)S(1)} %all-to-all-done.1.refs_2_) | copy-start | bytes 7077892
  118.2 52.9 %all-to-all-start.2 = ((f32[32,160,128]{2,1,0:T(8,128)}), f32[32,160,128]{2,1,0:T(8,128)}, u32[]{:S(2)}, u32[]{:S(2)}) async-start(f32[32,160,128]{2,1,0:T(8,128)} %merge_rows.1), calls=%async_computation.2 | async-start | bytes 5242880 | tf_op jit(solution)/shard_map/all_to_all | solution.py:641
  126.5 44.6 %collective-permute-start.5 = (f32[32,120,128]{2,1,0:T(8,128)}, f32[32,120,128]{2,1,0:T(8,128)S(1)}, u32[]{:S(2)}, u32[]{:S(2)}) collective-permute-start(f32[32,120,128]{2,1,0:T(8,128)} %slice.57), channel_id=1, source_target_pairs={{0,32},{32,0},{64,96},{96,64},{1,33},{33,1},{65,97},{97,65},{2,34}... | collective-permute-start | bytes 5898248 | tf_op jit(solution)/shard_map/ppermute | solution.py:660
  127.2 5.3 %copy-start.2 = (s32[128]{0:T(128)S(1)}, s32[128]{0:T(128)}, u32[]{:S(2)}) copy-start(s32[128]{0:T(128)} %param.29) | copy-start | bytes 1540
  131.6 6.9 %copy-start.16 = (bf16[512,480]{1,0:T(8,128)(2,1)S(1)}, bf16[512,480]{1,0:T(8,128)(2,1)}, u32[]{:S(2)}) copy-start(bf16[512,480]{1,0:T(8,128)(2,1)} %constant.113.clone) | copy-start | bytes 1474564
  131.6 8.4 %copy-start.15 = (s32[480]{0:T(512)S(1)}, s32[480]{0:T(512)}, u32[]{:S(2)}) copy-start(s32[480]{0:T(512)} %constant.112.clone) | copy-start | bytes 5764
  171.1 1.3 copy-start.5
Sparse Core Ops, SparseCore 0:
  69.9 71.5 all-gather.2

commit v9 on v6

--- a/solution.py
+++ b/solution.py
@@ -92,6 +92,39 @@
     place = row - 192 - 144 * piece
     late = np.where(place < 114, 192 + 114 * piece + place, 420 + 30 * piece + place - 114)
     return np.where(row < 192, row, late).astype(np.int32)
+
+
+def early_kernel(raw_hbm, early_hbm, early_ref, fetched, sent):
+    fetches, sends = [], []
+    for piece in range(EARLY // 8):
+        part = pl.ds(piece * 8, 8)
+        fetches.append(pltpu.make_async_copy(raw_hbm.at[part], early_ref.at[part], fetched.at[piece]))
+        sends.append(pltpu.make_async_copy(early_ref.at[part], early_hbm.at[part], sent.at[piece]))
+    for fetch in fetches:
+        fetch.start()
+    for fetch, send in zip(fetches, sends):
+        fetch.wait()
+        send.start()
+    for send in sends:
+        send.wait()
+
+
+def early_ticks(raw_turned):
+    chan_count = raw_turned.shape[1]
+    far = pl.BlockSpec(memory_space=pltpu.HBM)
+    return pl.pallas_call(
+        early_kernel,
+        in_specs=[far],
+        out_specs=far,
+        out_shape=jax.ShapeDtypeStruct((EARLY, chan_count), jnp.float32),
+        scratch_shapes=[
+            pltpu.VMEM((EARLY, chan_count), jnp.float32),
+            pltpu.SemaphoreType.DMA((EARLY // 8,)),
+            pltpu.SemaphoreType.DMA((EARLY // 8,)),
+        ],
+        compiler_params=roomy(60),
+        name="early_ticks",
+    )(raw_turned)
 
 
 def rank_kernel(plane_ref, base_ref, cross_ref, place_ref, count_ref):
@@ -123,11 +156,10 @@
 def rank_rows(chan_plane, pair_base, cross_side):
     chan_count = chan_plane.shape[0]
     scalar = pl.BlockSpec(memory_space=pltpu.SMEM)
-    whole = pl.BlockSpec(memory_space=pltpu.VMEM)
     place, count = pl.pallas_call(
         rank_kernel,
-        in_specs=[whole, scalar, scalar],
-        out_specs=[whole, whole],
+        in_specs=whole(1) + [scalar, scalar],
+        out_specs=whole(2),
         out_shape=[
             jax.ShapeDtypeStruct((1, chan_count), jnp.int32),
             jax.ShapeDtypeStruct((8, 128), jnp.int32),
@@ -506,7 +538,7 @@
         slab_points(load, store, middle_ref, sign)
         return carry
 
-    lax.fori_loop(0, HALF // 8, functools.partial(slabs_over, sign=-1), 0)
+    lax.fori_loop(0, HALF // 8, functools.partial(slabs_over, sign=-1), 0, unroll=2)
 
     def filtered(item, carry):
         data_high, data_low = split(jnp.concatenate([plane_ref[item, 0], plane_ref[item, 1]], axis=1))
@@ -524,8 +556,8 @@
 
     for copy in filter_copies:
         copy.wait()
-    lax.fori_loop(0, SLABS, filtered, 0, unroll=8)
-    lax.fori_loop(0, HALF // 8, functools.partial(slabs_over, sign=1), 0)
+    lax.fori_loop(0, SLABS, filtered, 0, unroll=16)
+    lax.fori_loop(0, HALF // 8, functools.partial(slabs_over, sign=1), 0, unroll=2)
     out_copies = []
     for pair in range(SLABS // 2):
         both = jnp.concatenate(
@@ -618,14 +650,15 @@
     parity = apa_index % 2
     swap = [(i, i ^ 1) for i in range(lax.axis_size("apa"))]
     raw_turned = raw.T
-    early_got = lax.ppermute(raw_turned[:EARLY], "apa", swap)
     local_group = group_id - apa_index * group_count
     good_mask = 1.0 - bad.astype(jnp.float32)
     pair_base = (apa_index // 2 * 2 * SLABS).astype(jnp.int32)
+    early_sent, chan_plane = lax.optimization_barrier((early_ticks(raw_turned), chan_plane))
+    early_got = lax.ppermute(early_sent, "apa", swap)
     place, cross_count = rank_rows(chan_plane, pair_base, (1 - parity).astype(jnp.int32))
-    place_got = lax.ppermute(place, "apa", swap)
     late0, rows = pack_rows(place, raw_turned)
     late0, later_place, later_raw = lax.optimization_barrier((late0, place, raw_turned))
+    place_got = lax.ppermute(later_place, "apa", swap)
     common = sum_groups(later_raw, local_group, good_mask)
     late1 = lay_late(rows, 1)
 
@@ -636,7 +669,9 @@
     common_got = lax.ppermute(common, "apa", swap)
     facts = jnp.stack([chan_wire >> 5, chan_wire & 31, local_group, bad, chan_plane - pair_base])
     facts = pick_facts(later_place - tick_index * WIRES, facts.astype(jnp.float32)).astype(jnp.int32)
-    own0, late1, early_got, common_got, facts = lax.optimization_barrier((own0, late1, early_got, common_got, facts))
+    own0, late1, early_got, common_got, facts, place_got = lax.optimization_barrier(
+        (own0, late1, early_got, common_got, facts, place_got)
+    )
     first = jnp.where(parity == 0, common, common_got)
     second = jnp.where(parity == 0, common_got, common)
     commons = lax.all_gather(jnp.concatenate([first, second], axis=0), "tick")

time: 229 us -> 227 us (level)
  local copies, waits for them, and re-layouts: 18.8 us -> 15.5 us
    slice x1 -> x0, local copies, waits for them, and re-layouts: 3.31 us -> none  [shards(): early_got = lax.ppermute(raw_turned[:EARLY], 'apa', swap)]
    pallas_call x1 -> x2, Pallas kernels: 2.13 us -> 4.69 us  [the longest x1 2.56 us: early_ticks(): pl.pallas_call(early_kernel, in_specs=[far], out_specs=far, out_shape=jax...]
    unnamed x40 -> x32, local copies, waits for them, and re-layouts: 4.8 us -> 4.79 us
  transfers between devices with their start and end apart: 10 -> 10, of which waited for: 3 -> 3; matrix products, arithmetic and copies ran while one was open for 10% -> 11% of each run, Pallas kernels for 28% -> 28%
where the time goes in v9:
time: 227 us
  Pallas kernels  116 us (51%)
  starting transfers between devices  33.9 us (15%)
  waiting for transfers between devices  32 us (14%)
  local copies, waits for them, and re-layouts  15.5 us (7%)
  between operations  13.8 us (6%)
  other arithmetic  8.95 us (4%)
  matrix products  6.75 us (3%)
    pallas_call x1, Pallas kernels, tail(): pl.pallas_call(tail_kernel, in_specs=far * 6 + whole(5) + far * 2 + whole...  50 us
    ppermute x1, waiting for transfers between devices, shards(): got1 = lax.ppermute(late_sent, 'apa', swap)  28.8 us
    all_to_all x3, starting transfers between devices, over_ticks(): lax.all_to_all(value, 'tick', split_axis=0, concat_axis=0, tiled=True)  27.2 us
    pallas_call x1, Pallas kernels, merge_rows(): pl.pallas_call(merge_kernel, in_specs=[pl.BlockSpec(memory_space=pltpu.SM...  23.5 us
    pallas_call x1, Pallas kernels, pack_rows(): pl.pallas_call(pack_kernel, in_specs=[pl.BlockSpec(memory_space=pltpu.SME...  19.4 us
    pallas_call x1, Pallas kernels, sum_groups(): pl.pallas_call(group_kernel, in_specs=whole(3), out_specs=whole(1)[0], ou...  7.07 us
    pallas_call x1, Pallas kernels, lay_late(): pl.pallas_call(functools.partial(fetched_late_kernel, which), in_specs=[p...  6.3 us
    unnamed x32, local copies, waits for them, and re-layouts  4.79 us
  transfers between devices with their start and end apart: 10, of which 3 were waited for; matrix products, arithmetic and copies ran while one was open for 11% of the time, Pallas kernels for 28%

profile of v9, /device:TPU:1, one launch (start us, length us, event | category | flops | bytes accessed | tf_op | source)
XLA Modules:
  0.0 226.5 jit_solution(10098928443707249920)
XLA Ops:
  6.5 0.0 copy-start
  6.5 2.6 %early_ticks.1 = f32[40,15360]{1,0:T(8,128)} custom-call(f32[100,15360]{1,0:T(8,128)} %bitcast.43), custom_call_target="tpu_custom_call" | custom-call | tf_op jit(solution)/shard_map/early_ticks/pallas_call | solution.py:115
  9.1 2.1 collective-permute-start
  11.2 2.1 rank_rows.1
  13.4 0.0 copy-start.3
  13.4 0.6 copy-done.3
  14.0 19.4 %pack_rows.1 = (f32[32,96,128]{2,1,0:T(8,128)}, f32[15360,128]{1,0:T(8,128)}) custom-call(s32[15360]{0:T(1024)} %bitcast.50, f32[100,15360]{1,0:T(8,128)} %bitcast.44), custom_call_target="tpu_custom_call" | custom-call | tf_op jit(solution)/shard_map/pack_rows/pallas_call | solution.py:232
  33.4 9.1 %all-to-all-start = ((f32[32,96,128]{2,1,0:T(8,128)}), f32[32,96,128]{2,1,0:T(8,128)S(1)}, u32[]{:S(2)}, u32[]{:S(2)}) async-start(f32[32,96,128]{2,1,0:T(8,128)} %get-tuple-element.28), calls=%async_computation | async-start | bytes 3145728 | tf_op jit(solution)/shard_map/all_to_all | solution.py:666
  42.5 0.0 copy-start.13
  42.5 0.0 all-gather.3.cloned.1.call-start
  42.5 0.0 copy-done.10
  42.6 0.0 copy-start.1
  42.6 2.8 %copy-done.1 = f32[15360,100]{0,1:T(8,128)S(1)} copy-done((f32[15360,100]{0,1:T(8,128)S(1)}, f32[15360,100]{0,1:T(8,128)}, u32[]{:S(2)}) %copy-start.1) | copy-done | bytes 6144024
  45.4 7.1 %sum_groups.1 = f32[120,128]{1,0:T(8,128)S(1)} custom-call(f32[100,15360]{1,0:T(8,128)S(1)} %bitcast.45, s32[1,15360]{1,0:T(1,128)S(1)} %bitcast.46, f32[1,15360]{1,0:T(1,128)S(1)} %bitcast.53), custom_call_target="tpu_custom_call" | custom-call | flops 1 | bytes 1 | tf_op jit(solution)/shard_map/sum_groups/pallas_call | solution.py:331
  52.5 0.3 collective-permute-start.1
  52.8 1.2 collective-permute-start.2
  54.0 0.5 stack.20
  54.6 4.7 %pick_facts.1 = f32[80,32]{1,0:T(8,128)S(1)} custom-call(s32[1,15360]{1,0:T(1,128)S(1)} %bitcast.49, f32[5,15360]{1,0:T(8,128)S(1)} %convert_element_type.38.facts_ref), custom_call_target="tpu_custom_call" | custom-call | flops 1 | bytes 1 | tf_op jit(solution)/shard_map/pick_facts/pallas_call | solution.py:359
  59.4 0.1 reshape.63
  59.5 6.3 %lay_late.1 = f32[32,144,128]{2,1,0:T(8,128)} custom-call(f32[15360,128]{1,0:T(8,128)} %get-tuple-element.29.rows_hbm.own_hbm), custom_call_target="tpu_custom_call" | custom-call | flops 1 | bytes 1 | tf_op jit(solution)/shard_map/lay_late/pallas_call | solution.py:264
  65.8 0.0 copy-start.11
  65.8 0.0 copy-start.9
  65.8 0.0 collective-permute-done.1
  65.8 0.9 collective-permute-done.2.place_ref
  66.8 0.0 all-to-all-done.refs_1_
  66.8 0.0 collective-permute-done.raw_ref
  66.8 0.9 broadcast_select_fusion.1
  67.7 0.7 pad_maximum_fusion
  68.3 0.0 all-gather.3.cloned.1.call-update
  68.4 10.1 %all-to-all-start.1 = ((f32[32,144,128]{2,1,0:T(8,128)}), f32[32,144,128]{2,1,0:T(8,128)S(1)}, u32[]{:S(2)}, u32[]{:S(2)}) async-start(f32[32,144,128]{2,1,0:T(8,128)} %lay_late.1), calls=%async_computation.1 | async-start | bytes 4718592 | tf_op jit(solution)/shard_map/all_to_all | solution.py:666
  78.5 0.8 reshape.64
  79.3 1.3 collective-permute-start.3
  80.6 0.8 fusion.23
  81.4 0.9 fusion.22
  82.3 0.0 copy-done.11
  82.3 0.9 fusion.12
  83.2 1.1 convolution_add_fusion
  84.3 0.1 reshape.65
  84.4 0.5 slice.41
  85.0 0.0 copy-done
  85.0 1.0 fusion.21
  86.0 1.3 broadcast_compare_fusion
  87.3 0.3 collective-permute-start.4
  87.6 0.9 copy.34.take_ref.refs_6_
  88.4 23.5 %merge_rows.1 = f32[32,160,128]{2,1,0:T(8,128)} custom-call(s32[15360]{0:T(1024)} %collective-permute-done.2.place_ref, f32[40,15360]{1,0:T(8,128)} %collective-permute-done.raw_ref, f32[15360,128]{1,0:T(8,128)} %get-tuple-element.29.rows_hbm.own_hbm, f32[480,1]{1,0:T(8,128)} %copy.34.take_ref.refs_6_), custom_call_target="tpu_custom_call" | custom-call | tf_op jit(solution)/shard_map/merge_rows/pallas_call | solution.py:297
  111.9 0.0 all-to-all-done.1.refs_2_
  111.9 1.6 slice.57
  113.5 2.3 %collective-permute-done.4 = s32[5,480]{1,0:T(8,128)S(1)} collective-permute-done((s32[5,480]{1,0:T(8,128)S(1)}, s32[5,480]{1,0:T(8,128)S(1)}, u32[]{:S(2)}, u32[]{:S(2)}) %collective-permute-start.4) | collective-permute-done | bytes 9632 | tf_op jit(solution)/shard_map/ppermute | solution.py:683
  115.8 0.0 collective-permute-done.3.refs_3_
  115.8 8.0 %all-to-all-start.2 = ((f32[32,160,128]{2,1,0:T(8,128)}), f32[32,160,128]{2,1,0:T(8,128)}, u32[]{:S(2)}, u32[]{:S(2)}) async-start(f32[32,160,128]{2,1,0:T(8,128)} %merge_rows.1), calls=%async_computation.2 | async-start | bytes 5242880 | tf_op jit(solution)/shard_map/all_to_all | solution.py:666
  123.8 1.5 collective-permute-start.5
  125.3 4.4 %negate_divide_fusion = (f32[32,256,128]{2,1,0:T(8,128)}, f32[32,256,128]{2,1,0:T(8,128)}) fusion(f32[32,128]{1,0:T(8,128)S(1)} %get-tuple-element.52, f32[256]{0:T(256)S(1)} %get-tuple-element.56, f32[32,128]{1,0:T(8,128)S(1)} %get-tuple-element.51, f32[256]{0:T(256)S(1)} %get-tuple-element.55), kind=kLoop, calls=%fused_computation.1 | loop fusion | flops 13631488 | bytes 8423424 | tf_op jit(solution)/shard_map/div | solution.py:634
  129.8 0.8 copy.39.refs_7_
  130.6 3.3 %gather_fusion = s32[480]{0:T(512)S(1)} fusion(s32[128]{0:T(128)S(1)} %copy-done.5, s32[1024]{0:T(1024)S(1)} %pad_clamp_fusion), kind=kCustom, calls=%fused_computation | custom fusion | bytes 5760 | tf_op jit(solution)/shard_map/jit(_take)/gather | solution.py:691
  134.0 1.5 convolution_convert_fusion
  135.6 1.0 copy.36
  136.6 0.5 convolution_convert_fusion.1
  137.1 1.0 copy.35
  138.1 0.6 multiply_add_fusion.1
  138.8 0.8 fusion.6.refs_8_
  139.6 28.8 %collective-permute-done.5.refs_4_ = f32[32,120,128]{2,1,0:T(8,128)S(1)} collective-permute-done((f32[32,120,128]{2,1,0:T(8,128)}, f32[32,120,128]{2,1,0:T(8,128)S(1)}, u32[]{:S(2)}, u32[]{:S(2)}) %collective-permute-start.5) | collective-permute-done | bytes 1966112 | tf_op jit(solution)/shard_map/ppermute | solution.py:687
  168.4 0.0 all-to-all-done.2.refs_0_
  168.4 1.3 copy-done.8
  169.7 50.0 %deconvolve.1 = f32[480,3200]{1,0:T(8,128)} custom-call(f32[32,160,128]{2,1,0:T(8,128)} %all-to-all-done.2.refs_0_, f32[32,96,128]{2,1,0:T(8,128)} %copy-done.7, f32[32,144,128]{2,1,0:T(8,128)} %copy-done.6, f32[32,96,128]{2,1,0:T(8,128)} %collective-permute-done.3.refs_3_, f32[32,120,128]{2,1,0:T(8,128)} %copy-done.8, f32[32,240,128]{2,1,0:T(8,128)} %bitcast.54, ...), custom_call_target="tpu_custom_call" | custom-call | tf_op jit(solution)/shard_map/deconvolve/pallas_call | solution.py:586
  (36 shorter events, 0.2 us)
Async XLA Ops:
  6.5 78.4 %copy-start = (f32[480]{0:T(512)S(1)}, f32[480]{0:T(512)}, u32[]{:S(2)}) copy-start(f32[480]{0:T(512)} %param.30) | copy-start | bytes 5764
  6.5 4.7 %copy-start.2 = (s32[15360]{0:T(1024)S(1)}, s32[15360]{0:T(1024)}, u32[]{:S(2)}) copy-start(s32[15360]{0:T(1024)} %param.27) | copy-start | bytes 184324
  9.1 57.7 %collective-permute-start = (f32[40,15360]{1,0:T(8,128)}, f32[40,15360]{1,0:T(8,128)}, u32[]{:S(2)}, u32[]{:S(2)}) collective-permute-start(f32[40,15360]{1,0:T(8,128)} %early_ticks.1), channel_id=1, source_target_pairs={{0,32},{32,0},{64,96},{96,64},{1,33},{33,1},{65,97},{97,65},{2,34}... | collective-permute-start | bytes 7372808 | tf_op jit(solution)/shard_map/ppermute | solution.py:657
  13.4 0.6 copy-start.3
  14.0 28.5 %copy-start.10 = (s32[15360]{0:T(1024)S(1)}, s32[15360]{0:T(1024)}, u32[]{:S(2)}) copy-start(s32[15360]{0:T(1024)} %param.25) | copy-start | bytes 184324
  14.0 28.5 %copy-start.12 = (s32[15360]{0:T(1024)S(1)}, s32[15360]{0:T(1024)}, u32[]{:S(2)}) copy-start(s32[15360]{0:T(1024)} %param.26) | copy-start | bytes 184324
  33.4 33.4 %all-to-all-start = ((f32[32,96,128]{2,1,0:T(8,128)}), f32[32,96,128]{2,1,0:T(8,128)S(1)}, u32[]{:S(2)}, u32[]{:S(2)}) async-start(f32[32,96,128]{2,1,0:T(8,128)} %get-tuple-element.28), calls=%async_computation | async-start | bytes 3145728 | tf_op jit(solution)/shard_map/all_to_all | solution.py:666
  42.4 10.4 %copy-start.4 = (s32[1,15360]{1,0:T(1,128)S(1)}, s32[1,15360]{1,0:T(1,128)}, u32[]{:S(2)}) copy-start(s32[1,15360]{1,0:T(1,128)} %copy-done.3) | copy-start | bytes 184324
  42.5 11.6 %copy-start.13 = (s32[15360]{0:T(1024)S(1)}, s32[15360]{0:T(1024)}, u32[]{:S(2)}) copy-start(s32[15360]{0:T(1024)} %param.28) | copy-start | bytes 184324
  42.5 125.9 %all-gather.3.cloned.1.call-start = ((), (), s32[]{:S(2)}) async-start(), calls=%async_computation.3 | async-start | bytes 4055040 | tf_op jit(solution)/shard_map/all_gather | solution.py:677
  42.6 2.8 %copy-start.1 = (f32[15360,100]{0,1:T(8,128)S(1)}, f32[15360,100]{0,1:T(8,128)}, u32[]{:S(2)}) copy-start(f32[15360,100]{0,1:T(8,128)} %param.24) | copy-start | bytes 18432004
  52.5 13.4 %collective-permute-start.1 = (f32[120,128]{1,0:T(8,128)S(1)}, f32[120,128]{1,0:T(8,128)}, u32[]{:S(2)}, u32[]{:S(2)}) collective-permute-start(f32[120,128]{1,0:T(8,128)S(1)} %sum_groups.1), channel_id=1, source_target_pairs={{0,32},{32,0},{64,96},{96,64},{1,33},{33,1},{65,97},{97,65},{2,34}... | collective-permute-start | bytes 184328 | tf_op jit(solution)/shard_map/ppermute | solution.py:669
  52.8 13.9 %collective-permute-start.2 = (s32[15360]{0:T(1024)S(1)}, s32[15360]{0:T(1024)}, u32[]{:S(2)}, u32[]{:S(2)}) collective-permute-start(s32[15360]{0:T(1024)S(1)} %bitcast.51), channel_id=1, source_target_pairs={{0,32},{32,0},{64,96},{96,64},{1,33},{33,1},{65,97},{97,65},{2,34}... | collective-permute-start | bytes 184328 | tf_op jit(solution)/shard_map/ppermute | solution.py:661
  65.8 16.5 %copy-start.11 = (f32[100,200]{1,0:T(8,128)S(1)}, f32[100,200]{1,0:T(8,128)}, u32[]{:S(2)}) copy-start(f32[100,200]{1,0:T(8,128)} %constant.131) | copy-start | bytes 240004
  65.8 19.2 %copy-start.9 = (f32[512,480]{1,0:T(8,128)S(1)}, f32[512,480]{1,0:T(8,128)}, u32[]{:S(2)}) copy-start(f32[512,480]{1,0:T(8,128)} %constant.115.clone) | copy-start | bytes 2949124
  66.8 1.6 copy-start.7
  68.4 43.6 %all-to-all-start.1 = ((f32[32,144,128]{2,1,0:T(8,128)}), f32[32,144,128]{2,1,0:T(8,128)S(1)}, u32[]{:S(2)}, u32[]{:S(2)}) async-start(f32[32,144,128]{2,1,0:T(8,128)} %lay_late.1), calls=%async_computation.1 | async-start | bytes 4718592 | tf_op jit(solution)/shard_map/all_to_all | solution.py:666
  79.3 36.5 %collective-permute-start.3 = (f32[32,96,128]{2,1,0:T(8,128)}, f32[32,96,128]{2,1,0:T(8,128)}, u32[]{:S(2)}, u32[]{:S(2)}) collective-permute-start(f32[32,96,128]{2,1,0:T(8,128)} %copy-done.7), channel_id=1, source_target_pairs={{0,32},{32,0},{64,96},{96,64},{1,33},{33,1},{65,97},{97,65},{2,34}... | collective-permute-start | bytes 4718600 | tf_op jit(solution)/shard_map/ppermute | solution.py:679
  87.3 28.5 %collective-permute-start.4 = (s32[5,480]{1,0:T(8,128)S(1)}, s32[5,480]{1,0:T(8,128)S(1)}, u32[]{:S(2)}, u32[]{:S(2)}) collective-permute-start(s32[5,480]{1,0:T(8,128)S(1)} %slice_convert_fusion), channel_id=1, source_target_pairs={{0,32},{32,0},{64,96},{96,64},{1,33},{33,1},{65,97},{97,65},{2,34}... | collective-permute-start | bytes 28808 | tf_op jit(solution)/shard_map/ppermute | solution.py:683
  111.9 3.9 %copy-start.6 = (f32[32,144,128]{2,1,0:T(8,128)}, f32[32,144,128]{2,1,0:T(8,128)S(1)}, u32[]{:S(2)}) copy-start(f32[32,144,128]{2,1,0:T(8,128)S(1)} %all-to-all-done.1.refs_2_) | copy-start | bytes 7077892
  115.8 52.6 %all-to-all-start.2 = ((f32[32,160,128]{2,1,0:T(8,128)}), f32[32,160,128]{2,1,0:T(8,128)}, u32[]{:S(2)}, u32[]{:S(2)}) async-start(f32[32,160,128]{2,1,0:T(8,128)} %merge_rows.1), calls=%async_computation.2 | async-start | bytes 5242880 | tf_op jit(solution)/shard_map/all_to_all | solution.py:666
  123.8 44.6 %collective-permute-start.5 = (f32[32,120,128]{2,1,0:T(8,128)}, f32[32,120,128]{2,1,0:T(8,128)S(1)}, u32[]{:S(2)}, u32[]{:S(2)}) collective-permute-start(f32[32,120,128]{2,1,0:T(8,128)} %slice.57), channel_id=1, source_target_pairs={{0,32},{32,0},{64,96},{96,64},{1,33},{33,1},{65,97},{97,65},{2,34}... | collective-permute-start | bytes 5898248 | tf_op jit(solution)/shard_map/ppermute | solution.py:687
  125.3 5.3 %copy-start.5 = (s32[128]{0:T(128)S(1)}, s32[128]{0:T(128)}, u32[]{:S(2)}) copy-start(s32[128]{0:T(128)} %param.29) | copy-start | bytes 1540
  129.7 6.9 %copy-start.15 = (bf16[512,480]{1,0:T(8,128)(2,1)S(1)}, bf16[512,480]{1,0:T(8,128)(2,1)}, u32[]{:S(2)}) copy-start(bf16[512,480]{1,0:T(8,128)(2,1)} %constant.113.clone) | copy-start | bytes 1474564
  129.7 8.4 %copy-start.14 = (s32[480]{0:T(512)S(1)}, s32[480]{0:T(512)}, u32[]{:S(2)}) copy-start(s32[480]{0:T(512)} %constant.112.clone) | copy-start | bytes 5764
  168.4 1.3 copy-start.8
Sparse Core Ops, SparseCore 0:
  68.5 79.9 all-gather.2
